TPU v7x, 32 devices: a whole 2x2x4 slice. The times are simulated.
32 devices in a mesh: dp: 8 (over z, x), tensor: 4 (over y, core).
Axes of the slice: x: 2, y: 2, z: 4, core: 2. Of those that a mesh axis runs over, the one named last changes fastest.
Arguments:
- inputs: bfloat16 [8192, 2048], P('dp'), may hold values from -6 to 6
- first_gain: float32 [2048], replicated, may hold values from 0.25 to 1.75
- first_bias: float32 [2048], replicated, may hold values from -1.75 to 1.75
- query_weight: bfloat16 [2048, 2048], P(None, 'tensor'), may hold values from -0.125 to 0.125
- query_bias: float32 [2048], P('tensor'), may hold values from -1.75 to 1.75
- keyval_weight: bfloat16 [2048, 256], replicated, may hold values from -0.1875 to 0.1875
- value_bias: float32 [128], replicated, may hold values from -3 to 3
- output_weight: bfloat16 [2048, 2048], P('tensor'), may hold values from -1 to 1
- output_bias: float32 [2048], replicated, may hold values from -1.75 to 1.75
- second_gain: float32 [2048], replicated, may hold values from 0.25 to 1.75
- second_bias: float32 [2048], replicated, may hold values from -1.75 to 1.75
- up_weight: bfloat16 [2048, 8192], P(None, 'tensor'), may hold values from -0.125 to 0.125
- up_bias: float32 [8192], P('tensor'), may hold values from -1.75 to 1.75
- down_weight: bfloat16 [8192, 2048], P('tensor'), may hold values from -0.09375 to 0.09375
- down_bias: float32 [2048], replicated, may hold values from -1.75 to 1.75
- cotangent: bfloat16 [8192, 2048], P('dp'), may hold values from -6 to 6
Outputs:
- layer_out: bfloat16 [8192, 2048], P('dp')
- grad_inputs: float32 [8192, 2048], P('dp')
- grad_first_gain: float32 [2048], replicated
- grad_first_bias: float32 [2048], replicated
- grad_query_weight: float32 [2048, 2048], P('dp', 'tensor')
- grad_query_bias: float32 [2048], P('tensor')
- grad_keyval_weight: float32 [2048, 256], P('dp')
- grad_value_bias: float32 [128], replicated
- grad_output_weight: float32 [2048, 2048], P('tensor', 'dp')
- grad_output_bias: float32 [2048], replicated
- grad_second_gain: float32 [2048], replicated
- grad_second_bias: float32 [2048], replicated
- grad_up_weight: float32 [2048, 8192], P('dp', 'tensor')
- grad_up_bias: float32 [8192], P('tensor')
- grad_down_weight: float32 [8192, 2048], P('tensor', 'dp')
- grad_down_bias: float32 [2048], replicated
All inputs are finite; a program needn't handle non-finite values.
Results may differ from a plain program's by a relative error of at most 0.024.
Values may be sent and summed in bfloat16 or wider, within the bound.
A program may use at most 320 MiB of HBM per device.

v0:
```python
from functools import partial

import jax
import jax.numpy as jnp
from jax import lax
from jax.sharding import PartitionSpec as P

SPAN = 8


EPSILON = 1e-05
NEG_LARGE = -1e30


def shifted(value, axis, steps):
    count = lax.axis_size(axis)
    first, last = (max(0, -steps), min(count, count - steps))
    return lax.ppermute(value, axis, [(source, source + steps) for source in range(first, last)])


def layer_norm(values, norm_gain, norm_bias):
    average = jnp.mean(values, axis=-1, keepdims=True)
    centred = values - average
    variance = jnp.mean(centred * centred, axis=-1, keepdims=True)
    return centred * lax.rsqrt(variance + EPSILON) * norm_gain + norm_bias


def gelu_tanh(values):
    return jax.nn.gelu(values, approximate=True)


def over_rows(left, right):
    return lax.dot_general(
        left, right, (((0,), (0,)), ((), ())), preferred_element_type=jnp.float32
    )


def over_cols(left, right):
    return lax.dot_general(
        left, right, (((1,), (1,)), ((), ())), preferred_element_type=jnp.float32
    )


def per_device(
    inputs,
    first_gain,
    first_bias,
    query_weight,
    query_bias,
    keyval_weight,
    value_bias,
    output_weight,
    output_bias,
    second_gain,
    second_bias,
    up_weight,
    up_bias,
    down_weight,
    down_bias,
    cotangent,
):
    tok_rows = inputs.shape[0]
    head_size = value_bias.shape[0]
    local_heads = query_weight.shape[1] // head_size
    score_scale = head_size ** (-0.5)
    position = lax.axis_index("dp") % SPAN
    causal = jnp.arange(tok_rows)[:, None] >= jnp.arange(tok_rows)[None, :]
    x_full = inputs.astype(jnp.float32)
    normed1_full, first_pull = jax.vjp(layer_norm, x_full, first_gain, first_bias)
    normed1 = normed1_full.astype(jnp.bfloat16)
    query_pre = jnp.dot(normed1, query_weight, preferred_element_type=jnp.float32) + query_bias
    queries = (
        (query_pre * score_scale).astype(jnp.bfloat16).reshape(tok_rows, local_heads, head_size)
    )
    kv_bias = jnp.concatenate([jnp.zeros_like(value_bias), value_bias])
    keyval = (jnp.dot(normed1, keyval_weight, preferred_element_type=jnp.float32) + kv_bias).astype(
        jnp.bfloat16
    )

    def score_block(kv_block, diagonal):
        scores = jnp.einsum(
            "qhd,kd->hqk", queries, kv_block[:, :head_size], preferred_element_type=jnp.float32
        )
        if diagonal:
            scores = jnp.where(causal[None], scores, NEG_LARGE)
        return scores

    def fold_stats(carried, kv_block, diagonal):
        run_peak, run_total = carried
        scores = score_block(kv_block, diagonal)
        new_peak = jnp.maximum(run_peak, jnp.max(scores, axis=-1))
        run_total = run_total * jnp.exp(run_peak - new_peak) + jnp.sum(
            jnp.exp(scores - new_peak[..., None]), axis=-1
        )
        return (new_peak, run_total)

    def keep_first(carried, kv_block):
        return carried

    kv_blocks = [keyval]
    for offset in range(1, SPAN):
        kv_blocks.append(shifted(keyval, "dp", offset))
    running = (
        jnp.full((local_heads, tok_rows), NEG_LARGE, jnp.float32),
        jnp.zeros((local_heads, tok_rows), jnp.float32),
    )
    for offset in range(SPAN):
        if offset == 0:
            running = fold_stats(running, kv_blocks[0], True)
        else:
            running = lax.cond(
                offset <= position,
                partial(fold_stats, diagonal=False),
                keep_first,
                running,
                kv_blocks[offset],
            )
    log_total = running[0] + jnp.log(running[1])

    def fold_context(carried, kv_block, diagonal):
        attn_probs = jnp.exp(score_block(kv_block, diagonal) - log_total[..., None]).astype(
            jnp.bfloat16
        )
        return carried + jnp.einsum(
            "hqk,kd->qhd", attn_probs, kv_block[:, head_size:], preferred_element_type=jnp.float32
        )

    context = jnp.zeros((tok_rows, local_heads, head_size), jnp.float32)
    for offset in range(SPAN):
        if offset == 0:
            context = fold_context(context, kv_blocks[0], True)
        else:
            context = lax.cond(
                offset <= position,
                partial(fold_context, diagonal=False),
                keep_first,
                context,
                kv_blocks[offset],
            )
    context_low = context.reshape(tok_rows, -1).astype(jnp.bfloat16)
    attn_part = jnp.dot(context_low, output_weight, preferred_element_type=jnp.float32)
    middle = (
        x_full
        + lax.psum(attn_part.astype(jnp.bfloat16), "tensor").astype(jnp.float32)
        + output_bias
    )
    normed2_full, second_pull = jax.vjp(layer_norm, middle, second_gain, second_bias)
    normed2 = normed2_full.astype(jnp.bfloat16)
    pre_act = jnp.dot(normed2, up_weight, preferred_element_type=jnp.float32) + up_bias
    act_full, gelu_pull = jax.vjp(gelu_tanh, pre_act)
    activ = act_full.astype(jnp.bfloat16)
    mlp_part = jnp.dot(activ, down_weight, preferred_element_type=jnp.float32)
    result = (
        middle + lax.psum(mlp_part.astype(jnp.bfloat16), "tensor").astype(jnp.float32) + down_bias
    )
    layer_out = result.astype(jnp.bfloat16)
    grad_full = cotangent.astype(jnp.float32)
    d_down_bias = jnp.sum(grad_full, axis=0)
    grad_down_part = over_rows(activ, cotangent)
    d_pre = gelu_pull(over_cols(cotangent, down_weight))[0].astype(jnp.bfloat16)
    grad_up_part = over_rows(normed2, d_pre)
    d_up_bias = jnp.sum(d_pre.astype(jnp.float32), axis=0)
    d_normed2 = lax.psum(over_cols(d_pre, up_weight).astype(jnp.bfloat16), "tensor").astype(
        jnp.float32
    )
    d_middle_norm, d_second_gain, d_second_bias = second_pull(d_normed2)
    d_middle = grad_full + d_middle_norm
    d_output_bias = jnp.sum(d_middle, axis=0)
    d_middle_low = d_middle.astype(jnp.bfloat16)
    grad_out_part = over_rows(context_low, d_middle_low)
    d_context = (
        over_cols(d_middle_low, output_weight)
        .astype(jnp.bfloat16)
        .reshape(tok_rows, local_heads, head_size)
    )
    delta = jnp.einsum("qhd,qhd->hq", d_context.astype(jnp.float32), context)

    def block_grads(kv_block, diagonal):
        key_rows = kv_block[:, :head_size]
        value_rows = kv_block[:, head_size:]
        attn_probs = jnp.exp(score_block(kv_block, diagonal) - log_total[..., None])
        d_probs = jnp.einsum(
            "qhd,kd->hqk", d_context, value_rows, preferred_element_type=jnp.float32
        )
        d_scores = (attn_probs * (d_probs - delta[..., None])).astype(jnp.bfloat16)
        d_query = jnp.einsum("hqk,kd->qhd", d_scores, key_rows, preferred_element_type=jnp.float32)
        d_key = jnp.einsum("hqk,qhd->kd", d_scores, queries, preferred_element_type=jnp.float32)
        d_value = jnp.einsum(
            "hqk,qhd->kd",
            attn_probs.astype(jnp.bfloat16),
            d_context,
            preferred_element_type=jnp.float32,
        )
        return (d_query, jnp.concatenate([d_key, d_value], axis=1))

    def no_grads(kv_block):
        return (
            jnp.zeros((tok_rows, local_heads, head_size), jnp.float32),
            jnp.zeros((tok_rows, 2 * head_size), jnp.float32),
        )

    d_query_sum = jnp.zeros((tok_rows, local_heads, head_size), jnp.float32)
    d_kv_sum = jnp.zeros((tok_rows, 2 * head_size), jnp.float32)
    for offset in range(SPAN):
        if offset == 0:
            kv_block = keyval
        else:
            kv_block = shifted(keyval, "dp", offset)
        if offset == 0:
            d_query_part, d_kv_part = block_grads(kv_block, True)
            d_kv_sum = d_kv_part
        else:
            d_query_part, d_kv_part = lax.cond(
                offset <= position, partial(block_grads, diagonal=False), no_grads, kv_block
            )
            d_kv_sum = d_kv_sum + shifted(d_kv_part.astype(jnp.bfloat16), "dp", -offset).astype(
                d_kv_part.dtype
            )
        d_query_sum = d_query_sum + d_query_part
    d_queries = (d_query_sum * score_scale).reshape(tok_rows, -1).astype(jnp.bfloat16)
    grad_query_part = over_rows(normed1, d_queries)
    d_query_bias = jnp.sum(d_queries.astype(jnp.float32), axis=0)
    d_normed1_query = over_cols(d_queries, query_weight)
    d_normed1_sum, d_kv_total = (
        lax.psum(d_normed1_query.astype(jnp.bfloat16), "tensor").astype(jnp.float32),
        lax.psum(d_kv_sum.astype(jnp.bfloat16), "tensor").astype(jnp.float32),
    )
    d_keyval = d_kv_total.astype(jnp.bfloat16)
    grad_kv_part = over_rows(normed1, d_keyval)
    d_value_bias = jnp.sum(d_keyval[:, head_size:].astype(jnp.float32), axis=0)
    d_normed1 = d_normed1_sum + over_cols(d_keyval, keyval_weight)
    d_x_norm, d_first_gain, d_first_bias = first_pull(d_normed1)
    grad_inputs = d_middle + d_x_norm
    sent_query, sent_kv, sent_out, sent_up, sent_down = (
        lax.psum_scatter(
            grad_query_part.astype(jnp.bfloat16), "dp", scatter_dimension=0, tiled=True
        ).astype(jnp.float32),
        lax.psum_scatter(
            grad_kv_part.astype(jnp.bfloat16), "dp", scatter_dimension=0, tiled=True
        ).astype(jnp.float32),
        lax.psum_scatter(
            grad_out_part.astype(jnp.bfloat16), "dp", scatter_dimension=1, tiled=True
        ).astype(jnp.float32),
        lax.psum_scatter(
            grad_up_part.astype(jnp.bfloat16), "dp", scatter_dimension=0, tiled=True
        ).astype(jnp.float32),
        lax.psum_scatter(
            grad_down_part.astype(jnp.bfloat16), "dp", scatter_dimension=1, tiled=True
        ).astype(jnp.float32),
    )
    bias_sums = (
        lax.psum(d_first_gain.astype(jnp.bfloat16), "dp").astype(jnp.float32),
        lax.psum(d_first_bias.astype(jnp.bfloat16), "dp").astype(jnp.float32),
        lax.psum(d_query_bias.astype(jnp.bfloat16), "dp").astype(jnp.float32),
        lax.psum(d_value_bias.astype(jnp.bfloat16), "dp").astype(jnp.float32),
        lax.psum(d_output_bias.astype(jnp.bfloat16), "dp").astype(jnp.float32),
        lax.psum(d_second_gain.astype(jnp.bfloat16), "dp").astype(jnp.float32),
        lax.psum(d_second_bias.astype(jnp.bfloat16), "dp").astype(jnp.float32),
        lax.psum(d_up_bias.astype(jnp.bfloat16), "dp").astype(jnp.float32),
        lax.psum(d_down_bias.astype(jnp.bfloat16), "dp").astype(jnp.float32),
    )
    return (
        layer_out,
        grad_inputs,
        bias_sums[0],
        bias_sums[1],
        sent_query,
        bias_sums[2],
        sent_kv,
        bias_sums[3],
        sent_out,
        bias_sums[4],
        bias_sums[5],
        bias_sums[6],
        sent_up,
        bias_sums[7],
        sent_down,
        bias_sums[8],
    )


def solution(mesh):
    in_specs = (
        P("dp", None),
        P(),
        P(),
        P(None, "tensor"),
        P("tensor"),
        P(),
        P(),
        P("tensor", None),
        P(),
        P(),
        P(),
        P(None, "tensor"),
        P("tensor"),
        P("tensor", None),
        P(),
        P("dp", None),
    )
    out_specs = (
        P("dp", None),
        P("dp", None),
        P(),
        P(),
        P("dp", "tensor"),
        P("tensor"),
        P("dp", None),
        P(),
        P("tensor", "dp"),
        P(),
        P(),
        P(),
        P("dp", "tensor"),
        P("tensor"),
        P("tensor", "dp"),
        P(),
    )
    return jax.shard_map(
        per_device, mesh=mesh, in_specs=in_specs, out_specs=out_specs, check_vma=False
    )
```

profile of v0, /device:TPU:0, one launch (start us, length us, event | category | flops | bytes accessed | tf_op | source)
XLA Modules:
  0.0 1510.2 jit_solution(6930662168636804116)
XLA Ops:
  18.0 8.7 collective-permute-start.6
  38.2 8.2 fusion.220
  46.4 24.7 %collective-permute-done.1 = bf16[1024,256]{1,0:T(8,128)(2,1)} collective-permute-done((bf16[1024,256]{1,0:T(8,128)(2,1)}, bf16[1024,256]{1,0:T(8,128)(2,1)}, u32[]{:S(2)}, u32[]{:S(2)}) %collective-permute-start.1) | collective-permute-done | bytes 524320 | tf_op jit(solution)/shard_map/ppermute | solution.py:18
  71.2 17.3 %collective-permute-start.3 = (bf16[1024,256]{1,0:T(8,128)(2,1)}, bf16[1024,256]{1,0:T(8,128)(2,1)}, u32[]{:S(2)}, u32[]{:S(2)}) collective-permute-start(bf16[1024,256]{1,0:T(8,128)(2,1)} %fusion.260), channel_id=1, source_target_pairs={{0,16},{4,20},{8,24},{12,28},{1,17},{5,21},{9,25},{13,29},{2,18},{... | collective-permute-start | bytes 1572872 | tf_op jit(solution)/shard_map/ppermute | solution.py:18
  90.7 9.0 exponential_reduce_fusion
  100.1 10.5 collective-permute-done.2
  111.1 6.8 conditional.26
  117.9 6.7 conditional.27
  124.6 11.6 convolution_bitcast_fusion.14
  139.5 7.3 conditional.31
  146.8 9.8 conditional.33
  159.2 5.6 convolution_convert_fusion.5
  164.9 194.8 %all-reduce.7.cloned.1.call-done = bf16[1024,2048]{1,0:T(8,128)(2,1)} async-done(((bf16[1024,2048]{1,0:T(8,128)(2,1)}), bf16[1024,2048]{1,0:T(8,128)(2,1)}) %all-reduce.7.cloned.1.call-update) | async-done | bytes 4194320 | tf_op jit(solution)/shard_map/psum | solution.py:144
  368.6 13.9 fusion.277
  382.5 20.6 %fusion.282 = (bf16[2048]{0:T(1024)(128)(2,1)}, bf16[1024,2048]{1,0:T(8,128)(2,1)}) fusion(f32[1024,2048]{1,0:T(8,128)} %fusion.277, f32[2048]{0:T(1024)S(1)} %copy-done.60, bf16[1024,2048]{1,0:T(8,128)(2,1)S(1)} %copy-done.22, bf16[2048,2048]{1,0:T(8,128)(2,1)} %param.71), kind=kOutput, calls=%fused_computation.363 | convolution fusion | flops 8636069888 | bytes 25178112 | tf_op jit(solution)/shard_map/dot_general | solution.py:39
  403.1 12.2 convolution_convert_fusion.3
  415.3 16.0 %convolution_convert_fusion.4 = bf16[1024,2048]{1,0:T(8,128)(2,1)} fusion(bf16[2048,2048]{1,0:T(8,128)(2,1)} %param.71, f32[1024,2048]{1,0:T(8,128)} %fusion.277, f32[2048]{0:T(1024)S(1)} %copy-done.60), kind=kOutput, calls=%fused_computation.306 | convolution fusion | flops 8613003264 | bytes 20979712 | tf_op jit(solution)/shard_map/dot_general | solution.py:152
  431.4 69.7 %all-reduce.9.cloned.1.call-done = bf16[1024,2048]{1,0:T(8,128)(2,1)} async-done(((bf16[1024,2048]{1,0:T(8,128)(2,1)}), bf16[1024,2048]{1,0:T(8,128)(2,1)}) %all-reduce.9.cloned.1.call-update) | async-done | bytes 4194320 | tf_op jit(solution)/shard_map/psum | solution.py:163
  501.0 7.4 fusion.232
  509.4 6.1 fusion.233
  515.5 11.3 fusion.284
  526.8 5.9 fusion.257
  532.8 5.6 convolution_bitcast_fusion.15
  543.8 8.7 fusion.218
  568.1 6.4 conditional.38
  575.8 6.2 conditional.39
  583.3 6.2 conditional.40
  590.3 7.6 conditional.41
  598.7 6.3 fusion.285
  606.6 30.9 %collective-permute-done.8 = bf16[1024,256]{0,1:T(8,128)(2,1)} collective-permute-done((bf16[1024,256]{0,1:T(8,128)(2,1)}, bf16[1024,256]{0,1:T(8,128)(2,1)}, u32[]{:S(2)}, u32[]{:S(2)}) %collective-permute-start.8) | collective-permute-done | bytes 524320 | tf_op jit(solution)/shard_map/ppermute | solution.py:18
  639.0 6.3 convolution_bitcast_fusion.16
  649.6 21.3 %collective-permute-done.9 = bf16[1024,256]{0,1:T(8,128)(2,1)} collective-permute-done((bf16[1024,256]{0,1:T(8,128)(2,1)}, bf16[1024,256]{0,1:T(8,128)(2,1)}, u32[]{:S(2)}, u32[]{:S(2)}) %collective-permute-start.9) | collective-permute-done | bytes 524320 | tf_op jit(solution)/shard_map/ppermute | solution.py:18
  670.9 45.3 %collective-permute-done.10 = bf16[1024,256]{0,1:T(8,128)(2,1)} collective-permute-done((bf16[1024,256]{0,1:T(8,128)(2,1)}, bf16[1024,256]{0,1:T(8,128)(2,1)}, u32[]{:S(2)}, u32[]{:S(2)}) %collective-permute-start.10) | collective-permute-done | bytes 524320 | tf_op jit(solution)/shard_map/ppermute | solution.py:18
  716.3 33.6 %collective-permute-done.11 = bf16[1024,256]{0,1:T(8,128)(2,1)} collective-permute-done((bf16[1024,256]{0,1:T(8,128)(2,1)}, bf16[1024,256]{0,1:T(8,128)(2,1)}, u32[]{:S(2)}, u32[]{:S(2)}) %collective-permute-start.11) | collective-permute-done | bytes 524320 | tf_op jit(solution)/shard_map/ppermute | solution.py:18
  749.9 31.8 %collective-permute-done.12 = bf16[1024,256]{0,1:T(8,128)(2,1)S(1)} collective-permute-done((bf16[1024,256]{0,1:T(8,128)(2,1)S(1)}, bf16[1024,256]{0,1:T(8,128)(2,1)S(1)}, u32[]{:S(2)}, u32[]{:S(2)}) %collective-permute-start.12) | collective-permute-done | bytes 524320 | tf_op jit(solution)/shard_map/ppermute | solution.py:18
  781.6 43.0 %collective-permute-done.13 = bf16[1024,256]{0,1:T(8,128)(2,1)S(1)} collective-permute-done((bf16[1024,256]{0,1:T(8,128)(2,1)S(1)}, bf16[1024,256]{0,1:T(8,128)(2,1)S(1)}, u32[]{:S(2)}, u32[]{:S(2)}) %collective-permute-start.13) | collective-permute-done | bytes 524320 | tf_op jit(solution)/shard_map/ppermute | solution.py:18
  828.0 7.9 convolution_convert_fusion.6
  836.1 6.0 convolution_convert_fusion.7
  842.1 144.8 %all-reduce.11.cloned.1.call-done = (bf16[1024,2048]{1,0:T(8,128)(2,1)}, bf16[1024,2048]{1,0:T(8,128)(2,1)}, bf16[1024,256]{0,1:T(8,128)(2,1)}) async-done(((bf16[1024,2048]{1,0:T(8,128)(2,1)}, bf16[1024,2048]{1,0:T(8,128)(2,1)}, bf16[1024,256]{0,1:T(8,128)(2,1)}), (bf16[1024,2048]{1,0:T(8,128)(2,1)}, bf16[1024,2048]{1,0:T(8,128)(2,1)}, bf16[1024,256]{0,1:T(8,128)(2,1)})) %all-reduce.11.cloned.1.call-update) | async-done | bytes 8912912 | tf_op jit(solution)/shard_map/psum | solution.py:154
  991.9 15.9 %convolution_convert_fusion = bf16[2048,2048]{1,0:T(8,128)(2,1)} fusion(bf16[1024,2048]{1,0:T(8,128)(2,1)} %param.73, f32[1024,2048]{1,0:T(8,128)} %fusion.277, f32[2048]{0:T(1024)S(1)} %copy-done.61), kind=kOutput, calls=%fused_computation.299 | convolution fusion | flops 8615100416 | bytes 20979712 | tf_op jit(solution)/shard_map/dot_general | solution.py:33
  1008.6 15.5 %convolution_convert_fusion.1 = bf16[2048,2048]{1,0:T(8,128)(2,1)} fusion(bf16[1024,2048]{1,0:T(8,128)(2,1)} %get-tuple-element.562, f32[2048]{0:T(1024)S(1)} %copy-done.63, f32[2048]{0:T(1024)S(1)} %copy-done.43, f32[1024]{0:T(1024)S(1)} %copy-done.49, bf16[1024,2048]{1,0:T(8,128)(2,1)} %all-reduce.7.cloned.1.call-done, bf16[1024,2048]{1,0:T(8,128)(2,1)} %param.58, ...), kind=kOutput, calls=%fused_computation.300 | convolution fusion | flops 8613003264 | bytes 21004288 | tf_op jit(solution)/shard_map/dot_general | solution.py:33
  1029.9 29.5 %reduce-scatter.10.cloned.1.call-done = bf16[512,256]{1,0:T(8,128)(2,1)} async-done(((bf16[512,2048]{1,0:T(8,128)(2,1)}), bf16[512,256]{1,0:T(8,128)(2,1)}) %reduce-scatter.10.cloned.1.call-update) | async-done | bytes 262160 | tf_op jit(solution)/shard_map/reduce_scatter | solution.py:241
  1061.2 69.0 %reduce-scatter.6.cloned.1.call-done = bf16[256,512]{1,0:T(8,128)(2,1)} async-done(((bf16[2048,512]{1,0:T(8,128)(2,1)}), bf16[256,512]{1,0:T(8,128)(2,1)}) %reduce-scatter.6.cloned.1.call-update) | async-done | bytes 262160 | tf_op jit(solution)/shard_map/reduce_scatter | solution.py:235
  1132.3 5.7 fusion.281
  1142.0 35.5 %all-reduce.1 = (bf16[2048]{0:T(1024)(128)(2,1)S(1)}, bf16[2048]{0:T(1024)(128)(2,1)S(1)}, bf16[512]{0:T(512)(128)(2,1)S(1)}, bf16[128]{0:T(256)(128)(2,1)S(1)},...) all-reduce(bf16[2048]{0:T(1024)(128)(2,1)S(1)} %get-tuple-element.5, ...), channel_id=1, replica_groups=mesh['dp'=8,'tensor'=4] {'dp'}, use_global_device_ids=true, to_apply=%region_72.73 | all-reduce | flops 14976 | bytes 59904 | tf_op jit(solution)/shard_map/psum | solution.py:252
  1182.8 16.1 %add_add_fusion.2 = (f32[1024,2048]{1,0:T(8,128)}, bf16[1024,2048]{1,0:T(8,128)(2,1)}) fusion(f32[1024,2048]{1,0:T(8,128)} %get-tuple-element.564, f32[1024]{0:T(1024)S(1)} %negate_multiply_fusion, f32[1024]{0:T(1024)S(1)} %multiply_multiply_fusion.2, f32[1024]{0:T(1024)S(1)} %copy-done.37, bf16[1024,2048]{1,0:T(8,128)(2,1)} %param.58, ...), kind=kLoop, calls=%fused_computation.292 | loop fusion | flops 33554432 | bytes 41984000 | tf_op jit(solution)/shard_map/add | solution.py:233
  1200.5 148.0 %reduce-scatter.14.cloned.1.call-done = bf16[2048,256]{1,0:T(8,128)(2,1)} async-done(((bf16[2048,2048]{1,0:T(8,128)(2,1)}), bf16[2048,256]{1,0:T(8,128)(2,1)}) %reduce-scatter.14.cloned.1.call-update) | async-done | bytes 1048592 | tf_op jit(solution)/shard_map/reduce_scatter | solution.py:247
  1351.1 149.0 %reduce-scatter.12.cloned.1.call-done = bf16[256,2048]{1,0:T(8,128)(2,1)} async-done(((bf16[2048,2048]{1,0:T(8,128)(2,1)}), bf16[256,2048]{1,0:T(8,128)(2,1)}) %reduce-scatter.12.cloned.1.call-update) | async-done | bytes 1048592 | tf_op jit(solution)/shard_map/reduce_scatter | solution.py:244
  (238 shorter events, 125.6 us)
Async XLA Ops:
  7.2 152.0 %copy-start = (bf16[512,2048]{1,0:T(8,128)(2,1)S(1)}, bf16[512,2048]{1,0:T(8,128)(2,1)}, u32[]{:S(2)}) copy-start(bf16[512,2048]{1,0:T(8,128)(2,1)} %param.65) | copy-start | bytes 6291460
  7.2 352.4 %all-reduce.7.cloned.1.call-start = ((), (), s32[]{:S(2)}) async-start(), calls=%async_computation.5 | async-start | bytes 8388608 | tf_op jit(solution)/shard_map/psum | solution.py:144
  13.8 21.7 %copy-start.46 = (f32[1024]{0:T(1024)}, f32[1024]{0:T(1024)S(1)}, u32[]{:S(2)}) copy-start(f32[1024]{0:T(1024)S(1)} %fusion.241) | copy-start | bytes 12292
  13.8 21.6 %copy-start.44 = (f32[1024]{0:T(1024)}, f32[1024]{0:T(1024)S(1)}, u32[]{:S(2)}) copy-start(f32[1024]{0:T(1024)S(1)} %fusion.272) | copy-start | bytes 12292
  13.9 21.9 %copy-start.56 = (bf16[2048,512]{1,0:T(8,128)(2,1)S(1)}, bf16[2048,512]{1,0:T(8,128)(2,1)}, u32[]{:S(2)}) copy-start(bf16[2048,512]{1,0:T(8,128)(2,1)} %param.61) | copy-start | bytes 6291460
  13.9 21.9 %copy-start.64 = (f32[512]{0:T(512)S(1)}, f32[512]{0:T(512)}, u32[]{:S(2)}) copy-start(f32[512]{0:T(512)} %param.62) | copy-start | bytes 6148
  15.8 22.4 %copy-start.24 = (bf16[1024,2048]{1,0:T(8,128)(2,1)}, bf16[1024,2048]{1,0:T(8,128)(2,1)S(1)}, u32[]{:S(2)}) copy-start(bf16[1024,2048]{1,0:T(8,128)(2,1)S(1)} %fusion.230) | copy-start | bytes 12582916
  18.0 100.0 %collective-permute-start.6 = (bf16[1024,256]{1,0:T(8,128)(2,1)}, bf16[1024,256]{1,0:T(8,128)(2,1)}, u32[]{:S(2)}, u32[]{:S(2)}) collective-permute-start(bf16[1024,256]{1,0:T(8,128)(2,1)} %fusion.260), channel_id=1, source_target_pairs={{0,28},{1,29},{2,30},{3,31}} | collective-permute-start | bytes 1572872 | tf_op jit(solution)/shard_map/ppermute | solution.py:18
  26.6 84.4 %collective-permute-start.5 = (bf16[1024,256]{1,0:T(8,128)(2,1)}, bf16[1024,256]{1,0:T(8,128)(2,1)}, u32[]{:S(2)}, u32[]{:S(2)}) collective-permute-start(bf16[1024,256]{1,0:T(8,128)(2,1)} %fusion.260), channel_id=1, source_target_pairs={{0,24},{4,28},{1,25},{5,29},{2,26},{6,30},{3,27},{7,31}} | collective-permute-start | bytes 1572872 | tf_op jit(solution)/shard_map/ppermute | solution.py:18
  28.7 82.3 %collective-permute-start.4 = (bf16[1024,256]{1,0:T(8,128)(2,1)}, bf16[1024,256]{1,0:T(8,128)(2,1)}, u32[]{:S(2)}, u32[]{:S(2)}) collective-permute-start(bf16[1024,256]{1,0:T(8,128)(2,1)} %fusion.260), channel_id=1, source_target_pairs={{0,20},{4,24},{8,28},{1,21},{5,25},{9,29},{2,22},{6,26},{10,30},{3... | collective-permute-start | bytes 1572872 | tf_op jit(solution)/shard_map/ppermute | solution.py:18
  30.8 40.4 %collective-permute-start.1 = (bf16[1024,256]{1,0:T(8,128)(2,1)}, bf16[1024,256]{1,0:T(8,128)(2,1)}, u32[]{:S(2)}, u32[]{:S(2)}) collective-permute-start(bf16[1024,256]{1,0:T(8,128)(2,1)} %fusion.260), channel_id=1, source_target_pairs={{0,8},{4,12},{8,16},{12,20},{16,24},{20,28},{1,9},{5,13},{9,17},{1... | collective-permute-start | bytes 1572872 | tf_op jit(solution)/shard_map/ppermute | solution.py:18
  32.9 55.5 %collective-permute-start = (bf16[1024,256]{1,0:T(8,128)(2,1)}, bf16[1024,256]{1,0:T(8,128)(2,1)}, u32[]{:S(2)}, u32[]{:S(2)}) collective-permute-start(bf16[1024,256]{1,0:T(8,128)(2,1)} %fusion.260), channel_id=1, source_target_pairs={{0,4},{4,8},{8,12},{12,16},{16,20},{20,24},{24,28},{1,5},{5,9},{9,... | collective-permute-start | bytes 1572872 | tf_op jit(solution)/shard_map/ppermute | solution.py:18
  71.2 39.4 %collective-permute-start.3 = (bf16[1024,256]{1,0:T(8,128)(2,1)}, bf16[1024,256]{1,0:T(8,128)(2,1)}, u32[]{:S(2)}, u32[]{:S(2)}) collective-permute-start(bf16[1024,256]{1,0:T(8,128)(2,1)} %fusion.260), channel_id=1, source_target_pairs={{0,16},{4,20},{8,24},{12,28},{1,17},{5,21},{9,25},{13,29},{2,18},{... | collective-permute-start | bytes 1572872 | tf_op jit(solution)/shard_map/ppermute | solution.py:18
  88.4 22.1 %collective-permute-start.2 = (bf16[1024,256]{1,0:T(8,128)(2,1)}, bf16[1024,256]{1,0:T(8,128)(2,1)}, u32[]{:S(2)}, u32[]{:S(2)}) collective-permute-start(bf16[1024,256]{1,0:T(8,128)(2,1)} %fusion.260), channel_id=1, source_target_pairs={{0,12},{4,16},{8,20},{12,24},{16,28},{1,13},{5,17},{9,21},{13,25},... | collective-permute-start | bytes 1572872 | tf_op jit(solution)/shard_map/ppermute | solution.py:18
  159.1 200.5 %copy-start.33 = (f32[2048]{0:T(1024)S(1)}, f32[2048]{0:T(1024)}, u32[]{:S(2)}) copy-start(f32[2048]{0:T(1024)} %param.66) | copy-start | bytes 24580
  164.8 336.2 %all-reduce.9.cloned.1.call-start = ((), (), s32[]{:S(2)}) async-start(), calls=%async_computation.6 | async-start | bytes 8388608 | tf_op jit(solution)/shard_map/psum | solution.py:163
  164.9 203.7 %copy-start.42 = (f32[2048]{0:T(1024)S(1)}, f32[2048]{0:T(1024)}, u32[]{:S(2)}) copy-start(f32[2048]{0:T(1024)} %param.67) | copy-start | bytes 24580
  164.9 203.7 %copy-start.62 = (f32[2048]{0:T(1024)S(1)}, f32[2048]{0:T(1024)}, u32[]{:S(2)}) copy-start(f32[2048]{0:T(1024)} %param.68) | copy-start | bytes 24580
  365.6 149.9 %copy-start.38 = (f32[1024]{0:T(1024)}, f32[1024]{0:T(1024)S(1)}, u32[]{:S(2)}) copy-start(f32[1024]{0:T(1024)S(1)} %broadcast_multiply_fusion) | copy-start | bytes 12292
  368.5 146.9 %copy-start.48 = (f32[1024]{0:T(1024)}, f32[1024]{0:T(1024)S(1)}, u32[]{:S(2)}) copy-start(f32[1024]{0:T(1024)S(1)} %fusion.273) | copy-start | bytes 12292
  368.6 34.5 %slice-start.4 = ((s8[8388608]{0:T(1024)(128)(4,1)}), s8[4194304]{0:T(1024)(128)(4,1)S(1)}, s32[]{:S(2)}) async-start(s8[8388608]{0:T(1024)(128)(4,1)} %bitcast.624), calls=%async_computation.17 | async-start | bytes 8388608
  382.5 20.6 %slice-start.5 = ((s8[8388608]{0:T(1024)(128)(4,1)}), s8[4194304]{0:T(1024)(128)(4,1)S(1)}, s32[]{:S(2)}) async-start(s8[8388608]{0:T(1024)(128)(4,1)} %bitcast.624), calls=%async_computation.18 | async-start | bytes 8388608
  415.3 571.7 %all-reduce.11.cloned.1.call-start = ((), (), s32[]{:S(2)}) async-start(), calls=%async_computation.12 | async-start | bytes 17825792 | tf_op jit(solution)/shard_map/psum | solution.py:154
  515.5 17.2 %slice-start.1 = ((s8[16777216]{0:T(1024)(128)(4,1)}), s8[4194304]{0:T(1024)(128)(4,1)S(1)}, s32[]{:S(2)}) async-start(s8[16777216]{0:T(1024)(128)(4,1)} %bitcast.617), calls=%async_computation.14 | async-start | bytes 8388608
  559.0 46.0 %collective-permute-start.7 = (bf16[1024,256]{0,1:T(8,128)(2,1)}, bf16[1024,256]{0,1:T(8,128)(2,1)}, u32[]{:S(2)}, u32[]{:S(2)}) collective-permute-start(bf16[1024,256]{0,1:T(8,128)(2,1)} %get-tuple-element.410), channel_id=1, source_target_pairs={{4,0},{8,4},{12,8},{16,12},{20,16},{24,20},{28,24},{5,1},{9,5},{13... | collective-permute-start | bytes 1572872 | tf_op jit(solution)/shard_map/ppermute | solution.py:18
  562.8 74.8 %collective-permute-start.8 = (bf16[1024,256]{0,1:T(8,128)(2,1)}, bf16[1024,256]{0,1:T(8,128)(2,1)}, u32[]{:S(2)}, u32[]{:S(2)}) collective-permute-start(bf16[1024,256]{0,1:T(8,128)(2,1)} %get-tuple-element.411), channel_id=1, source_target_pairs={{8,0},{12,4},{16,8},{20,12},{24,16},{28,20},{9,1},{13,5},{17,9},{2... | collective-permute-start | bytes 1572872 | tf_op jit(solution)/shard_map/ppermute | solution.py:18
  566.8 104.2 %collective-permute-start.9 = (bf16[1024,256]{0,1:T(8,128)(2,1)}, bf16[1024,256]{0,1:T(8,128)(2,1)}, u32[]{:S(2)}, u32[]{:S(2)}) collective-permute-start(bf16[1024,256]{0,1:T(8,128)(2,1)} %get-tuple-element.412), channel_id=1, source_target_pairs={{12,0},{16,4},{20,8},{24,12},{28,16},{13,1},{17,5},{21,9},{25,13},... | collective-permute-start | bytes 1572872 | tf_op jit(solution)/shard_map/ppermute | solution.py:18
  574.5 141.8 %collective-permute-start.10 = (bf16[1024,256]{0,1:T(8,128)(2,1)}, bf16[1024,256]{0,1:T(8,128)(2,1)}, u32[]{:S(2)}, u32[]{:S(2)}) collective-permute-start(bf16[1024,256]{0,1:T(8,128)(2,1)} %get-tuple-element.413), channel_id=1, source_target_pairs={{16,0},{20,4},{24,8},{28,12},{17,1},{21,5},{25,9},{29,13},{18,2},{... | collective-permute-start | bytes 1572872 | tf_op jit(solution)/shard_map/ppermute | solution.py:18
  582.0 167.9 %collective-permute-start.11 = (bf16[1024,256]{0,1:T(8,128)(2,1)}, bf16[1024,256]{0,1:T(8,128)(2,1)}, u32[]{:S(2)}, u32[]{:S(2)}) collective-permute-start(bf16[1024,256]{0,1:T(8,128)(2,1)} %get-tuple-element.414), channel_id=1, source_target_pairs={{20,0},{24,4},{28,8},{21,1},{25,5},{29,9},{22,2},{26,6},{30,10},{2... | collective-permute-start | bytes 1572872 | tf_op jit(solution)/shard_map/ppermute | solution.py:18
  598.7 38.9 %copy-start.32 = (bf16[1024,256]{0,1:T(8,128)(2,1)S(1)}, bf16[1024,256]{0,1:T(8,128)(2,1)}, u32[]{:S(2)}) copy-start(bf16[1024,256]{0,1:T(8,128)(2,1)} %copy-done.31) | copy-start | bytes 1572868
  605.0 44.7 %copy-start.26 = (bf16[1024,4,128]{0,2,1:T(8,128)(2,1)}, bf16[1024,4,128]{0,2,1:T(8,128)(2,1)S(1)}, u32[]{:S(2)}) copy-start(bf16[1024,4,128]{0,2,1:T(8,128)(2,1)S(1)} %get-tuple-element.566) | copy-start | bytes 3145732
  605.0 40.3 %copy-start.57 = (bf16[2048,512]{1,0:T(8,128)(2,1)S(1)}, bf16[2048,512]{1,0:T(8,128)(2,1)}, u32[]{:S(2)}) copy-start(bf16[2048,512]{1,0:T(8,128)(2,1)} %param.61) | copy-start | bytes 6291460
  605.0 176.6 %collective-permute-start.12 = (bf16[1024,256]{0,1:T(8,128)(2,1)S(1)}, bf16[1024,256]{0,1:T(8,128)(2,1)S(1)}, u32[]{:S(2)}, u32[]{:S(2)}) collective-permute-start(bf16[1024,256]{0,1:T(8,128)(2,1)S(1)} %copy-done.30), channel_id=1, source_target_pairs={{24,0},{28,4},{25,1},{29,5},{26,2},{30,6},{27,3},{31,7}} | collective-permute-start | bytes 1572872 | tf_op jit(solution)/shard_map/ppermute | solution.py:18
  637.5 187.1 %collective-permute-start.13 = (bf16[1024,256]{0,1:T(8,128)(2,1)S(1)}, bf16[1024,256]{0,1:T(8,128)(2,1)S(1)}, u32[]{:S(2)}, u32[]{:S(2)}) collective-permute-start(bf16[1024,256]{0,1:T(8,128)(2,1)S(1)} %copy-done.32), channel_id=1, source_target_pairs={{28,0},{29,1},{30,2},{31,3}} | collective-permute-start | bytes 1572872 | tf_op jit(solution)/shard_map/ppermute | solution.py:18
  645.3 179.4 %copy-start.28 = (f32[1024,128]{0,1:T(8,128)S(1)}, f32[1024,128]{0,1:T(8,128)}, u32[]{:S(2)}) copy-start(f32[1024,128]{0,1:T(8,128)} %convolution_bitcast_fusion.15) | copy-start | bytes 1572868
  649.6 178.4 %copy-start.25 = (bf16[1024,4,128]{0,2,1:T(8,128)(2,1)S(1)}, bf16[1024,4,128]{0,2,1:T(8,128)(2,1)}, u32[]{:S(2)}) copy-start(bf16[1024,4,128]{0,2,1:T(8,128)(2,1)} %copy.152) | copy-start | bytes 3145732
  828.0 231.5 %reduce-scatter.10.cloned.1.call-start = ((), (), s32[]{:S(2)}) async-start(), calls=%async_computation.9 | async-start | bytes 2359296 | tf_op jit(solution)/shard_map/reduce_scatter | solution.py:241
  836.0 294.3 %reduce-scatter.6.cloned.1.call-start = ((), (), s32[]{:S(2)}) async-start(), calls=%async_computation.7 | async-start | bytes 2359296 | tf_op jit(solution)/shard_map/reduce_scatter | solution.py:235
  842.1 149.8 %copy-start.61 = (f32[2048]{0:T(1024)S(1)}, f32[2048]{0:T(1024)}, u32[]{:S(2)}) copy-start(f32[2048]{0:T(1024)} %param.70) | copy-start | bytes 24580
  842.1 356.7 %reduce-scatter.8.cloned.1.call-start = ((), (), s32[]{:S(2)}) async-start(), calls=%async_computation.8 | async-start | bytes 1179648 | tf_op jit(solution)/shard_map/reduce_scatter | solution.py:238
  991.6 356.8 %reduce-scatter.14.cloned.1.call-start = ((), (), s32[]{:S(2)}) async-start(), calls=%async_computation.11 | async-start | bytes 9437184 | tf_op jit(solution)/shard_map/reduce_scatter | solution.py:247
  1007.9 492.2 %reduce-scatter.12.cloned.1.call-start = ((), (), s32[]{:S(2)}) async-start(), calls=%async_computation.10 | async-start | bytes 9437184 | tf_op jit(solution)/shard_map/reduce_scatter | solution.py:244
  1024.1 108.0 %copy-start.35 = (bf16[1024,256]{0,1:T(8,128)(2,1)S(1)}, bf16[1024,256]{0,1:T(8,128)(2,1)}, u32[]{:S(2)}) copy-start(bf16[1024,256]{0,1:T(8,128)(2,1)} %get-tuple-element.560) | copy-start | bytes 1572868
  1024.1 108.1 %copy-start.37 = (f32[1024]{0:T(1024)S(1)}, f32[1024]{0:T(1024)}, u32[]{:S(2)}) copy-start(f32[1024]{0:T(1024)} %copy-done.36) | copy-start | bytes 12292
  1024.1 108.1 %copy-start.41 = (f32[2048]{0:T(1024)S(1)}, f32[2048]{0:T(1024)}, u32[]{:S(2)}) copy-start(f32[2048]{0:T(1024)} %param.59) | copy-start | bytes 24580
  1024.1 108.1 %copy-start.59 = (bf16[2048,256]{1,0:T(8,128)(2,1)S(1)}, bf16[2048,256]{1,0:T(8,128)(2,1)}, u32[]{:S(2)}) copy-start(bf16[2048,256]{1,0:T(8,128)(2,1)} %param.63) | copy-start | bytes 3145732
  1138.0 44.8 %copy-start.53 = (f32[2048]{0:T(1024)S(1)}, f32[2048]{0:T(1024)}, u32[]{:S(2)}) copy-start(f32[2048]{0:T(1024)} %param.72) | copy-start | bytes 24580
  1182.8 320.1 %copy-start.1 = (bf16[512,2048]{1,0:T(8,128)(2,1)S(1)}, bf16[512,2048]{1,0:T(8,128)(2,1)}, u32[]{:S(2)}) copy-start(bf16[512,2048]{1,0:T(8,128)(2,1)} %param.65) | copy-start | bytes 6291460
  (38 other events, 231.2 us)
Sparse Core Ops, SparseCore 0:
  164.9 194.6 all-reduce.6
  415.4 85.6 all-reduce.8
  828.1 158.8 all-reduce.10
  990.9 68.4 reduce-scatter.9
  1063.4 66.8 reduce-scatter.5
  1133.5 62.3 reduce-scatter.7
  1200.0 148.4 reduce-scatter.13
  1352.1 148.0 reduce-scatter.11
where the time goes:
time: 1520 us; the launch traced here: 1510 us
  waiting for transfers between devices  1050 us (69%)
  matrix products  183 us (12%)
  other arithmetic  105 us (7%)
  loops' own time  51.6 us (3%)
  starting transfers between devices  47 us (3%)
  blocking collectives  35.5 us (2%)
  local copies, waits for them, and re-layouts  26.4 us (2%)
  between operations  15.7 us (1%)
    ppermute x14, waiting for transfers between devices, shifted(): lax.ppermute(value, axis, [(source, source + steps) for source in range(f...  241 us
    psum x1, waiting for transfers between devices, per_device(): lax.psum(attn_part.astype(jnp.bfloat16), 'tensor').astype(jnp.float32)  195 us
    reduce_scatter x1, waiting for transfers between devices, per_device(): lax.psum_scatter(grad_up_part.astype(jnp.bfloat16), 'dp', scatter_dimensi...  149 us
    reduce_scatter x1, waiting for transfers between devices, per_device(): lax.psum_scatter(grad_down_part.astype(jnp.bfloat16), 'dp', scatter_dimen...  148 us
    psum x1, waiting for transfers between devices, per_device(): lax.psum(mlp_part.astype(jnp.bfloat16), 'tensor').astype(jnp.float32)  145 us
    psum x1, waiting for transfers between devices, per_device(): lax.psum(over_cols(d_pre, up_weight).astype(jnp.bfloat16), 'tensor')  69.7 us
    reduce_scatter x1, waiting for transfers between devices, per_device(): lax.psum_scatter(grad_query_part.astype(jnp.bfloat16), 'dp', scatter_dime...  69 us
    dot_general x5, matrix products, over_rows(): lax.dot_general(left, right, (((0,), (0,)), ((), ())), preferred_element_...  50 us
  transfers between devices with their start and end apart: 22, of which 15 were waited for; matrix products, arithmetic and copies ran while one was open for 11% of the time, Pallas kernels for 0%

commit v1 on v0

v1 whole, which is shorter than its diff:
```python
import functools

import jax
import jax.numpy as jnp
from jax import lax
from jax.experimental import pallas as pl
from jax.experimental.pallas import tpu as pltpu
from jax.sharding import PartitionSpec as P

SPAN = 8
EPSILON = 1e-05
NEG_LARGE = -1e30
MESH = pl.DeviceIdType.MESH
VMEM = pl.BlockSpec(memory_space=pltpu.VMEM)
F32 = jnp.float32
BF16 = jnp.bfloat16


def contract(left, right, left_dim, right_dim):
    return lax.dot_general(
        left, right, (((left_dim,), (right_dim,)), ((), ())), preferred_element_type=F32
    )


def remote(source, target, send_sem, recv_sem, device):
    return pltpu.make_async_remote_copy(
        src_ref=source,
        dst_ref=target,
        send_sem=send_sem,
        recv_sem=recv_sem,
        device_id=device,
        device_id_type=MESH,
    )


def greet(devices):
    barrier = pltpu.get_barrier_semaphore()
    for device in devices:
        pl.semaphore_signal(barrier, inc=1, device_id=device, device_id_type=MESH)
    pl.semaphore_wait(barrier, len(devices))


def tensor_sum_kernel(
    chunks, part_ref, out_ref, from_core, summed, from_y, core_send, core_recv, y_send, y_recv,
    back_send, back_recv,
):
    block = lax.axis_index("dp")
    lane = lax.axis_index("tensor")
    core_peer = (block, lane + 1 - 2 * lax.rem(lane, 2))
    y_peer = (block, lax.rem(lane + 2, 4))
    rows, width = part_ref.shape
    half = width // 2
    step = rows // chunks
    mine = pl.ds(pl.multiple_of(lax.rem(lane, 2) * half, half), half)
    other = pl.ds(pl.multiple_of((1 - lax.rem(lane, 2)) * half, half), half)
    greet([core_peer, y_peer])

    def span(k):
        return pl.ds(pl.multiple_of(k * step, step), step)

    def to_core(k):
        return remote(
            part_ref.at[span(k), other], from_core.at[span(k)], core_send.at[k], core_recv.at[k],
            core_peer,
        )

    def to_y(k):
        return remote(
            summed.at[span(k)], from_y.at[span(k)], y_send.at[k], y_recv.at[k], y_peer
        )

    def back(k):
        return remote(
            out_ref.at[span(k), mine], out_ref.at[span(k), mine], back_send.at[k],
            back_recv.at[k], core_peer,
        )

    @pl.loop(0, chunks)
    def _(k):
        to_core(k).start()

    @pl.loop(0, chunks)
    def _(k):
        to_core(k).wait_recv()
        summed[span(k)] = (
            part_ref[span(k), mine].astype(F32) + from_core[span(k)].astype(F32)
        ).astype(BF16)
        to_y(k).start()

    @pl.loop(0, chunks)
    def _(k):
        to_y(k).wait_recv()
        out_ref[span(k), mine] = (
            summed[span(k)].astype(F32) + from_y[span(k)].astype(F32)
        ).astype(BF16)
        back(k).start()

    @pl.loop(0, chunks)
    def _(k):
        back(k).wait_recv()
        back(k).wait_send()
        to_core(k).wait_send()
        to_y(k).wait_send()


def tensor_sum(part, chunks=8):
    rows, width = part.shape
    half = pltpu.VMEM((rows, width // 2), BF16)
    return pl.pallas_call(
        functools.partial(tensor_sum_kernel, chunks),
        out_shape=jax.ShapeDtypeStruct((rows, width), BF16),
        in_specs=[VMEM],
        out_specs=VMEM,
        scratch_shapes=[half, half, half] + [pltpu.SemaphoreType.DMA((chunks,))] * 6,
        compiler_params=pltpu.CompilerParams(
            collective_id=0, has_side_effects=True, vmem_limit_bytes=32 << 20
        ),
        name="tensor_sum",
    )(part)


def gather_kernel(own_ref, out_ref, local_sem, x_send, x_recv, z_send, z_recv, c_send, c_recv):
    block = lax.axis_index("dp")
    lane = lax.axis_index("tensor")
    place = lax.rem(block, SPAN)
    level = place // 2
    levels = SPAN // 2
    core_peer = (block, lane + 1 - 2 * lax.rem(lane, 2))
    x_peer = (block + 1 - 2 * lax.rem(place, 2), lane)
    upper = (jnp.where(level < levels - 1, block + 2, block + 2 - SPAN), lane)
    lower = (jnp.where(level > 0, block - 2, block - 2 + SPAN), lane)
    rows = own_ref.shape[0]
    half = rows // 2
    part = pl.ds(pl.multiple_of(lax.rem(lane, 2) * half, half), half)
    greet([core_peer, x_peer, upper, lower])
    keep = pltpu.make_async_copy(own_ref, out_ref.at[place], local_sem)
    keep.start()
    to_x = remote(own_ref.at[part], out_ref.at[place, part], x_send, x_recv, x_peer)
    to_x.start()
    keep.wait()
    to_x.wait_recv()
    partner = place + 1 - 2 * lax.rem(place, 2)
    share = remote(
        out_ref.at[partner, part], out_ref.at[partner, part], c_send.at[levels - 1],
        c_recv.at[levels - 1], core_peer,
    )
    share.start()

    def pair(lev):
        return pl.ds(2 * lev, 2)

    def up(s):
        return remote(
            out_ref.at[pair(level - s), part], out_ref.at[pair(level - s), part], z_send.at[s],
            z_recv.at[s], upper,
        )

    def across(s):
        return remote(
            out_ref.at[pair(level - 1 - s), part], out_ref.at[pair(level - 1 - s), part],
            c_send.at[s], c_recv.at[s], core_peer,
        )

    for s in range(levels - 1):
        @pl.when((level < levels - 1) & (level >= s))
        def _(s=s):
            up(s).start()

        @pl.when(level > s)
        def _(s=s):
            up(s).wait_recv()
            across(s).start()

    share.wait()
    to_x.wait_send()
    for s in range(levels - 1):
        @pl.when((level < levels - 1) & (level >= s))
        def _(s=s):
            up(s).wait_send()

        @pl.when(level > s)
        def _(s=s):
            across(s).wait()


def gather_keyval(keyval):
    rows, width = keyval.shape
    levels = SPAN // 2
    dma = pltpu.SemaphoreType.DMA
    hbm = pl.BlockSpec(memory_space=pl.ANY)
    out = pl.pallas_call(
        gather_kernel,
        out_shape=jax.ShapeDtypeStruct((SPAN, rows, width), BF16),
        in_specs=[hbm],
        out_specs=hbm,
        scratch_shapes=[dma, dma, dma, dma((levels,)), dma((levels,)), dma((levels,)), dma((levels,))],
        compiler_params=pltpu.CompilerParams(collective_id=1, has_side_effects=True),
        name="gather_keyval",
    )(keyval)
    return out.reshape(SPAN * rows, width)


def small_sum_kernel(count, own_ref, out_ref, slots, send, recv):
    block = lax.axis_index("dp")
    lane = lax.axis_index("tensor")
    others = [(lax.rem(block + k, count), lane) for k in range(1, count)]
    greet(others)
    copies = []
    for k in range(1, count):
        copy = remote(own_ref, slots.at[k - 1], send.at[k - 1], recv.at[k - 1], others[k - 1])
        copy.start()
        copies.append(copy)
    total = own_ref[...]
    for k in range(1, count):
        copies[k - 1].wait()
        total = total + slots[k - 1]
    out_ref[...] = total


def small_sum(values, count):
    flat = jnp.concatenate(values)
    size = flat.shape[0]
    rows = -(-size // 1024) * 8
    packed = jnp.pad(flat, (0, rows * 128 - size)).reshape(rows, 128)
    total = pl.pallas_call(
        functools.partial(small_sum_kernel, count),
        out_shape=jax.ShapeDtypeStruct((rows, 128), F32),
        in_specs=[VMEM],
        out_specs=VMEM,
        scratch_shapes=[pltpu.VMEM((count - 1, rows, 128), F32)]
        + [pltpu.SemaphoreType.DMA((count - 1,))] * 2,
        compiler_params=pltpu.CompilerParams(collective_id=2, has_side_effects=True),
        name="small_sum",
    )(packed).reshape(-1)
    pieces = []
    start = 0
    for value in values:
        pieces.append(total[start : start + value.shape[0]])
        start += value.shape[0]
    return pieces


def scatter_sum(own, other, group):
    count = lax.axis_size("dp")
    length = group // 2
    block = lax.axis_index("dp")
    level = lax.rem(block, group) // 2

    def shifted(value, sources, step):
        pairs = [
            (base + 2 * source + side, base + 2 * (source + step) + side)
            for base in range(0, count, group)
            for source in sources
            for side in range(2)
        ]
        return lax.ppermute(value, "dp", pairs)

    received = lax.ppermute(other, "dp", [(p, p ^ 1) for p in range(count)])
    total = (own.astype(F32) + received.astype(F32)).astype(BF16)

    def slot(index):
        index = jnp.clip(index, 0, length - 1)
        return lax.dynamic_index_in_dim(total, index, 0, keepdims=False)

    up, down = slot(level + length - 1), slot(level - length + 1)
    for s in range(1, length):
        up = shifted(up, range(0, s), 1)
        down = shifted(down, range(length - s, length), -1)
        kept_up = slot(level + length - 1 - s).astype(F32)
        kept_down = slot(level - length + 1 + s).astype(F32)
        if s < length - 1:
            up = (kept_up + up.astype(F32)).astype(BF16)
            down = (kept_down + down.astype(F32)).astype(BF16)
        else:
            return kept_up + up.astype(F32) + down.astype(F32)


def split_sides(part, group):
    rows = part.shape[0] // group
    side = lax.rem(lax.axis_index("dp"), 2)
    parts = part.reshape(group // 2, 2, rows, part.shape[1])
    own = lax.dynamic_index_in_dim(parts, side, 1, keepdims=False)
    other = lax.dynamic_index_in_dim(parts, 1 - side, 1, keepdims=False)
    return own, other


def attend_kernel(q_rows, k_rows, q_ref, kv_ref, ctx_ref, lse_ref, acc, peak, total):
    rows = q_ref.shape[0]
    head = kv_ref.shape[1] // 2
    heads = q_ref.shape[1] // head
    place = lax.rem(lax.axis_index("dp"), SPAN)
    for i in range(rows // q_rows):
        span = slice(i * q_rows, (i + 1) * q_rows)
        peak[...] = jnp.full_like(peak, NEG_LARGE)
        total[...] = jnp.zeros_like(total)
        acc[...] = jnp.zeros_like(acc)

        def step(j, diagonal):
            at = pl.ds(pl.multiple_of(j * k_rows, k_rows), k_rows)
            keys = kv_ref[at, 0:head]
            values = kv_ref[at, head : 2 * head]
            for h in range(heads):
                query = q_ref[span, h * head : (h + 1) * head]
                scores = contract(keys, query, 1, 1)
                if diagonal is not None:
                    key_at = lax.broadcasted_iota(jnp.int32, scores.shape, 0) + diagonal
                    query_at = lax.broadcasted_iota(jnp.int32, scores.shape, 1)
                    scores = jnp.where(key_at <= query_at, scores, NEG_LARGE)
                old = peak[h]
                new = jnp.maximum(old, jnp.max(scores, axis=0, keepdims=True))
                probs = jnp.exp(scores - new)
                fade = jnp.exp(old - new)
                total[h] = total[h] * fade + jnp.sum(probs, axis=0, keepdims=True)
                peak[h] = new
                acc[h] = acc[h] * fade + contract(values, probs.astype(BF16), 0, 0)

        full = (place * rows + i * q_rows) // k_rows

        @pl.loop(0, full)
        def _(j):
            step(j, None)

        for d in range(q_rows // k_rows):
            step(full + d, d * k_rows)
        for h in range(heads):
            context = acc[h] / total[h]
            ctx_ref[span, h * head : (h + 1) * head] = context.T.astype(BF16)
            lse_ref[h : h + 1, span] = peak[h] + jnp.log(total[h])


def attend(queries, keyval, q_rows=512, k_rows=512):
    rows, width = queries.shape
    head = keyval.shape[1] // 2
    heads = width // head
    stat = pltpu.VMEM((heads, 1, q_rows), F32)
    return pl.pallas_call(
        functools.partial(attend_kernel, q_rows, k_rows),
        out_shape=(
            jax.ShapeDtypeStruct((rows, width), BF16),
            jax.ShapeDtypeStruct((heads, rows), F32),
        ),
        in_specs=[VMEM, VMEM],
        out_specs=(VMEM, VMEM),
        scratch_shapes=[pltpu.VMEM((heads, head, q_rows), F32), stat, stat],
        compiler_params=pltpu.CompilerParams(vmem_limit_bytes=48 << 20),
        cost_estimate=pl.CostEstimate(
            flops=16 * rows * rows * width, bytes_accessed=8 << 20, transcendentals=0
        ),
        name="attend",
    )(queries, keyval)


def attend_back_kernel(
    q_rows, k_rows, q_ref, kv_ref, do_ref, ctx_ref, lse_ref, dq_ref, dkv_ref, dq_acc, dkv_acc, delta
):
    rows = q_ref.shape[0]
    head = kv_ref.shape[1] // 2
    heads = q_ref.shape[1] // head
    place = lax.rem(lax.axis_index("dp"), SPAN)
    dkv_acc[...] = jnp.zeros_like(dkv_acc)
    for i in range(rows // q_rows):
        span = slice(i * q_rows, (i + 1) * q_rows)
        for h in range(heads):
            cols = slice(h * head, (h + 1) * head)
            product = do_ref[span, cols].astype(F32) * ctx_ref[span, cols].astype(F32)
            delta[h] = jnp.sum(product.T, axis=0, keepdims=True)
        dq_acc[...] = jnp.zeros_like(dq_acc)

        def step(j, diagonal):
            at = pl.ds(pl.multiple_of(j * k_rows, k_rows), k_rows)
            keys = kv_ref[at, 0:head]
            values = kv_ref[at, head : 2 * head]
            d_keys = jnp.zeros((k_rows, head), F32)
            d_values = jnp.zeros((k_rows, head), F32)
            for h in range(heads):
                cols = slice(h * head, (h + 1) * head)
                query = q_ref[span, cols]
                d_ctx = do_ref[span, cols]
                scores = contract(keys, query, 1, 1)
                if diagonal is not None:
                    key_at = lax.broadcasted_iota(jnp.int32, scores.shape, 0) + diagonal
                    query_at = lax.broadcasted_iota(jnp.int32, scores.shape, 1)
                    scores = jnp.where(key_at <= query_at, scores, NEG_LARGE)
                probs = jnp.exp(scores - lse_ref[h : h + 1, span])
                d_probs = contract(values, d_ctx, 1, 1)
                d_scores = (probs * (d_probs - delta[h])).astype(BF16)
                d_values += contract(probs.astype(BF16), d_ctx, 1, 0)
                d_keys += contract(d_scores, query, 1, 0)
                dq_acc[h] += contract(keys, d_scores, 0, 0)
            dkv_acc[at, 0:head] += d_keys
            dkv_acc[at, head : 2 * head] += d_values

        full = (place * rows + i * q_rows) // k_rows

        @pl.loop(0, full)
        def _(j):
            step(j, None)

        for d in range(q_rows // k_rows):
            step(full + d, d * k_rows)
        for h in range(heads):
            dq_ref[span, h * head : (h + 1) * head] = (dq_acc[h] * head**-0.5).T.astype(BF16)
    dkv_ref[...] = dkv_acc[...].astype(BF16)


def attend_back(queries, keyval, d_context, context, lse, q_rows=512, k_rows=512):
    rows, width = queries.shape
    head = keyval.shape[1] // 2
    heads = width // head
    return pl.pallas_call(
        functools.partial(attend_back_kernel, q_rows, k_rows),
        out_shape=(
            jax.ShapeDtypeStruct((rows, width), BF16),
            jax.ShapeDtypeStruct(keyval.shape, BF16),
        ),
        in_specs=[VMEM] * 5,
        out_specs=(VMEM, VMEM),
        scratch_shapes=[
            pltpu.VMEM((heads, head, q_rows), F32),
            pltpu.VMEM(keyval.shape, F32),
            pltpu.VMEM((heads, 1, q_rows), F32),
        ],
        compiler_params=pltpu.CompilerParams(vmem_limit_bytes=56 << 20),
        cost_estimate=pl.CostEstimate(
            flops=40 * rows * rows * width, bytes_accessed=12 << 20, transcendentals=0
        ),
        name="attend_back",
    )(queries, keyval, d_context, context, lse)


def layer_norm(values, norm_gain, norm_bias):
    average = jnp.mean(values, axis=-1, keepdims=True)
    centred = values - average
    variance = jnp.mean(centred * centred, axis=-1, keepdims=True)
    return centred * lax.rsqrt(variance + EPSILON) * norm_gain + norm_bias


def gelu_tanh(values):
    return jax.nn.gelu(values, approximate=True)


def per_device(
    inputs,
    first_gain,
    first_bias,
    query_weight,
    query_bias,
    keyval_weight,
    value_bias,
    output_weight,
    output_bias,
    second_gain,
    second_bias,
    up_weight,
    up_bias,
    down_weight,
    down_bias,
    cotangent,
):
    count = lax.axis_size("dp")
    head_size = value_bias.shape[0]
    score_scale = head_size ** (-0.5)
    x_full = inputs.astype(F32)
    normed1_full, first_pull = jax.vjp(layer_norm, x_full, first_gain, first_bias)
    normed1 = normed1_full.astype(BF16)
    query_pre = jnp.dot(normed1, query_weight, preferred_element_type=F32) + query_bias
    queries = (query_pre * score_scale).astype(BF16)
    kv_bias = jnp.concatenate([jnp.zeros_like(value_bias), value_bias])
    keyval = (jnp.dot(normed1, keyval_weight, preferred_element_type=F32) + kv_bias).astype(BF16)
    keyval_all = gather_keyval(keyval)
    context_low, lse = attend(queries, keyval_all)
    attn_part = jnp.dot(context_low, output_weight, preferred_element_type=F32).astype(BF16)
    middle = x_full + tensor_sum(attn_part).astype(F32) + output_bias
    normed2_full, second_pull = jax.vjp(layer_norm, middle, second_gain, second_bias)
    normed2 = normed2_full.astype(BF16)
    pre_act = jnp.dot(normed2, up_weight, preferred_element_type=F32) + up_bias
    act_full, gelu_pull = jax.vjp(gelu_tanh, pre_act)
    activ = act_full.astype(BF16)
    grad_full = cotangent.astype(F32)
    d_down_bias = jnp.sum(grad_full, axis=0)
    d_pre = gelu_pull(contract(cotangent, down_weight, 1, 1))[0].astype(BF16)
    d_normed2_part = contract(d_pre, up_weight, 1, 1).astype(BF16)
    d_normed2 = tensor_sum(d_normed2_part).astype(F32)
    grad_down_part = contract(cotangent, activ, 0, 0).astype(BF16)
    sent_down = scatter_sum(*split_sides(grad_down_part, count), count)
    grad_up_part = contract(normed2, d_pre, 0, 0).astype(BF16)
    sent_up = scatter_sum(*split_sides(grad_up_part, count), count)
    d_up_bias = jnp.sum(d_pre.astype(F32), axis=0)
    mlp_part = jnp.dot(activ, down_weight, preferred_element_type=F32).astype(BF16)
    result = middle + tensor_sum(mlp_part).astype(F32) + down_bias
    layer_out = result.astype(BF16)
    d_middle_norm, d_second_gain, d_second_bias = second_pull(d_normed2)
    d_middle = grad_full + d_middle_norm
    d_output_bias = jnp.sum(d_middle, axis=0)
    d_middle_low = d_middle.astype(BF16)
    grad_out_part = contract(d_middle_low, context_low, 0, 0).astype(BF16)
    d_context = contract(d_middle_low, output_weight, 1, 1).astype(BF16)
    d_queries, d_kv_part = attend_back(queries, keyval_all, d_context, context_low, lse)
    grad_query_part = contract(normed1, d_queries, 0, 0).astype(BF16)
    d_query_bias = jnp.sum(d_queries.astype(F32), axis=0)
    d_normed1_query = contract(d_queries, query_weight, 1, 1).astype(BF16)
    d_kv_own = scatter_sum(*split_sides(d_kv_part, SPAN), SPAN)
    d_normed1_sum = tensor_sum(d_normed1_query).astype(F32)
    d_keyval = lax.psum(d_kv_own.astype(BF16), "tensor")
    grad_kv_part = contract(normed1, d_keyval, 0, 0).astype(BF16)
    d_value_bias = jnp.sum(d_keyval[:, head_size:].astype(F32), axis=0)
    d_normed1 = d_normed1_sum + contract(d_keyval, keyval_weight, 1, 1)
    d_x_norm, d_first_gain, d_first_bias = first_pull(d_normed1)
    grad_inputs = d_middle + d_x_norm
    local = query_weight.shape[1]
    rest_part = jnp.concatenate([grad_query_part, grad_out_part, grad_kv_part], axis=1)
    sent_rest = scatter_sum(*split_sides(rest_part, count), count)
    sums = small_sum(
        [
            d_first_gain,
            d_first_bias,
            d_query_bias,
            d_value_bias,
            d_output_bias,
            d_second_gain,
            d_second_bias,
            d_up_bias,
            d_down_bias,
        ],
        count,
    )
    return (
        layer_out,
        grad_inputs,
        sums[0],
        sums[1],
        sent_rest[:, :local],
        sums[2],
        sent_rest[:, 2 * local :],
        sums[3],
        sent_rest[:, local : 2 * local].T,
        sums[4],
        sums[5],
        sums[6],
        sent_up,
        sums[7],
        sent_down.T,
        sums[8],
    )


def solution(mesh):
    in_specs = (
        P("dp", None),
        P(),
        P(),
        P(None, "tensor"),
        P("tensor"),
        P(),
        P(),
        P("tensor", None),
        P(),
        P(),
        P(),
        P(None, "tensor"),
        P("tensor"),
        P("tensor", None),
        P(),
        P("dp", None),
    )
    out_specs = (
        P("dp", None),
        P("dp", None),
        P(),
        P(),
        P("dp", "tensor"),
        P("tensor"),
        P("dp", None),
        P(),
        P("tensor", "dp"),
        P(),
        P(),
        P(),
        P("dp", "tensor"),
        P("tensor"),
        P("tensor", "dp"),
        P(),
    )
    return jax.shard_map(
        per_device, mesh=mesh, in_specs=in_specs, out_specs=out_specs, check_vma=False
    )
```

time: 1520 us -> 1010 us (0.66)
  the two profiles are of different devices: /device:TPU:0 before, /device:TPU:14 now
where the time goes in v1:
time: 1010 us; the launch traced here: 997 us
  Pallas kernels  389 us (39%)
  waiting for transfers between devices  174 us (17%)
  starting transfers between devices  148 us (15%)
  matrix products  119 us (12%)
  other arithmetic  83.8 us (8%)
  local copies, waits for them, and re-layouts  67.4 us (7%)
  between operations  15.6 us (2%)
    pallas_call x4, Pallas kernels, tensor_sum(): pl.pallas_call(functools.partial(tensor_sum_kernel, chunks), out_shape=ja...  203 us
    ppermute x24, starting transfers between devices, shifted(): return lax.ppermute(value, 'dp', pairs)  146 us
    ppermute x24, waiting for transfers between devices, shifted(): return lax.ppermute(value, 'dp', pairs)  131 us
    dot_general x10, matrix products, contract(): lax.dot_general(left, right, (((left_dim,), (right_dim,)), ((), ())), pre...  79.1 us
    pallas_call x1, Pallas kernels, small_sum(): pl.pallas_call(functools.partial(small_sum_kernel, count), out_shape=jax....  55.9 us
    pallas_call x1, Pallas kernels, attend_back(): pl.pallas_call(functools.partial(attend_back_kernel, q_rows, k_rows), out...  49.9 us
    pallas_call x1, Pallas kernels, gather_keyval(): pl.pallas_call(gather_kernel, out_shape=jax.ShapeDtypeStruct((SPAN, rows,...  44.1 us
    pallas_call x1, Pallas kernels, attend(): pl.pallas_call(functools.partial(attend_kernel, q_rows, k_rows), out_shap...  35.7 us
  transfers between devices with their start and end apart: 29, of which 12 were waited for; matrix products, arithmetic and copies ran while one was open for 20% of the time, Pallas kernels for 26%

profile of v1, /device:TPU:14, one launch (start us, length us, event | category | flops | bytes accessed | tf_op | source)
XLA Modules:
  0.0 996.9 jit_solution(14645741543761646638)
XLA Ops:
  10.3 3.5 fusion.19
  19.9 44.1 %gather_keyval.1 = bf16[8,1024,256]{2,1,0:T(8,128)(2,1)} custom-call(bf16[1024,256]{1,0:T(8,128)(2,1)} %fusion.51.own_ref), custom_call_target="tpu_custom_call" | custom-call | tf_op jit(solution)/shard_map/gather_keyval/pallas_call | solution.py:191
  64.0 5.2 multiply_convert_fusion.1.q_ref
  69.2 35.7 %attend.1 = (bf16[1024,512]{1,0:T(8,128)(2,1)S(1)}, f32[4,1024]{1,0:T(4,128)S(1)}) custom-call(bf16[1024,512]{1,0:T(8,128)(2,1)S(1)} %multiply_convert_fusion.1.q_ref, bf16[8192,256]{1,0:T(8,128)(2,1)} %bitcast.165), custom_call_target="tpu_custom_call" | custom-call | flops 8589934592 | bytes 8388608 | tf_op jit(solution)/shard_map/attend/pallas_call | solution.py:336
  107.4 50.0 %tensor_sum.4 = bf16[1024,2048]{1,0:T(8,128)(2,1)S(1)} custom-call(bf16[1024,2048]{1,0:T(8,128)(2,1)S(1)} %convolution_convert_fusion.5.part_ref), custom_call_target="tpu_custom_call" | custom-call | tf_op jit(solution)/shard_map/tensor_sum/pallas_call | solution.py:109
  161.4 16.4 %fusion.61 = f32[1024,2048]{1,0:T(8,128)} fusion(bf16[2048,2048]{1,0:T(8,128)(2,1)} %param.27, f32[2048]{0:T(1024)S(1)} %copy-done.47, f32[2048]{0:T(1024)S(1)} %copy-done.32, f32[1024]{0:T(1024)S(1)} %fusion.59, bf16[1024,2048]{1,0:T(8,128)(2,1)} %copy-done.2, bf16[1024,2048]{1,0:T(8,128)(2,1)} %param.16, f32[1024]{0:T(1024)S(1)} %broadcast_multiply_fusion, ...), kind=kOutput, calls=%fused_computation.160 | convolution fusion | flops 8608808960 | bytes 25198592 | tf_op jit(solution)/shard_map/dot_general | solution.py:476
  177.8 12.1 %convolution_convert_fusion = bf16[2048,2048]{0,1:T(8,128)(2,1)S(1)} fusion(bf16[1024,2048]{1,0:T(8,128)(2,1)S(1)} %copy-done.21, f32[1024,2048]{1,0:T(8,128)} %fusion.61, f32[2048]{0:T(1024)S(1)} %copy-done.46), kind=kOutput, calls=%fused_computation.46 | convolution fusion | flops 8615100416 | bytes 20979712 | tf_op jit(solution)/shard_map/dot_general | solution.py:20
  189.9 4.2 constant_dynamic-slice_fusion.1
  194.1 6.2 copy.36
  200.3 19.4 %convert_reduce_fusion.3 = (f32[2048]{0:T(1024)}, bf16[1024,2048]{1,0:T(8,128)(2,1)S(1)}) fusion(f32[1024,2048]{1,0:T(8,128)} %fusion.61, f32[2048]{0:T(1024)S(1)} %copy-done.46, bf16[1024,2048]{1,0:T(8,128)(2,1)} %param.31, bf16[2048,2048]{1,0:T(8,128)(2,1)} %param.29), kind=kOutput, calls=%fused_computation.39 | convolution fusion | flops 8638167040 | bytes 25182208 | tf_op jit(solution)/shard_map/dot_general | solution.py:20
  219.7 13.9 %convolution_convert_fusion.4.part_ref = bf16[1024,2048]{1,0:T(8,128)(2,1)S(1)} fusion(bf16[2048,2048]{1,0:T(8,128)(2,1)S(1)} %bitcast.169, f32[1024,2048]{1,0:T(8,128)} %fusion.61, f32[2048]{0:T(1024)S(1)} %copy-done.46), kind=kOutput, calls=%fused_computation.58 | convolution fusion | flops 8613003264 | bytes 20979712 | tf_op jit(solution)/shard_map/dot_general | solution.py:489
  233.6 11.7 %convolution_convert_fusion.3.part_ref = bf16[1024,2048]{1,0:T(8,128)(2,1)S(1)} fusion(bf16[1024,2048]{1,0:T(8,128)(2,1)S(1)} %get-tuple-element.49, bf16[2048,2048]{1,0:T(8,128)(2,1)} %param.27), kind=kOutput, calls=%fused_computation.57 | convolution fusion | flops 8592031744 | bytes 16777216 | tf_op jit(solution)/shard_map/dot_general | solution.py:20
  245.3 51.1 %tensor_sum.6 = bf16[1024,2048]{1,0:T(8,128)(2,1)S(1)} custom-call(bf16[1024,2048]{1,0:T(8,128)(2,1)S(1)} %convolution_convert_fusion.3.part_ref), custom_call_target="tpu_custom_call" | custom-call | tf_op jit(solution)/shard_map/tensor_sum/pallas_call | solution.py:109
  296.5 3.5 convert_reduce_fusion
  300.0 5.5 fusion.22
  305.5 51.1 %tensor_sum.5 = bf16[1024,2048]{1,0:T(8,128)(2,1)S(1)} custom-call(bf16[1024,2048]{1,0:T(8,128)(2,1)S(1)} %convolution_convert_fusion.4.part_ref), custom_call_target="tpu_custom_call" | custom-call | tf_op jit(solution)/shard_map/tensor_sum/pallas_call | solution.py:109
  356.7 9.7 fusion.67
  366.3 6.7 fusion.43.do_ref
  373.1 49.9 %attend_back.1 = (bf16[1024,512]{1,0:T(8,128)(2,1)}, bf16[8192,256]{1,0:T(8,128)(2,1)}) custom-call(bf16[1024,512]{1,0:T(8,128)(2,1)} %copy-done.8, bf16[8192,256]{1,0:T(8,128)(2,1)} %bitcast.166, bf16[1024,512]{1,0:T(8,128)(2,1)} %fusion.43.do_ref, bf16[1024,512]{1,0:T(8,128)(2,1)} %copy-done.6, f32[4,1024]{1,0:T(4,128)} %copy-done.9), custom_call_target="tpu_custom_call" | custom-call | flops 21474836480 | bytes 12582912 | tf_op jit(solution)/shard_map/attend_back/pallas_call | solution.py:410
  426.0 12.8 %convolution_convert_fusion.1 = bf16[2048,2048]{1,0:T(8,128)(2,1)S(1)} fusion(bf16[1024,2048]{1,0:T(8,128)(2,1)} %copy-done.49, f32[2048]{0:T(1024)S(1)} %copy-done.47, f32[2048]{0:T(1024)S(1)} %copy-done.32, f32[1024]{0:T(1024)S(1)} %fusion.59, bf16[1024,2048]{1,0:T(8,128)(2,1)S(1)} %copy-done.3, bf16[1024,2048]{1,0:T(8,128)(2,1)} %param.16, ...), kind=kOutput, calls=%fused_computation.47 | convolution fusion | flops 8613003264 | bytes 21004288 | tf_op jit(solution)/shard_map/dot_general | solution.py:20
  446.5 6.3 copy.41
  452.8 21.8 %collective-permute-done = bf16[4,1024,256]{2,1,0:T(8,128)(2,1)S(1)} collective-permute-done((bf16[4,1024,256]{2,1,0:T(8,128)(2,1)}, bf16[4,1024,256]{2,1,0:T(8,128)(2,1)S(1)}, u32[]{:S(2)}, u32[]{:S(2)}) %collective-permute-start) | collective-permute-done | bytes 2097184 | tf_op jit(solution)/shard_map/ppermute | solution.py:258
  480.7 51.1 %tensor_sum.7 = bf16[1024,2048]{1,0:T(8,128)(2,1)S(1)} custom-call(bf16[1024,2048]{1,0:T(8,128)(2,1)S(1)} %convolution_convert_fusion.2.part_ref), custom_call_target="tpu_custom_call" | custom-call | tf_op jit(solution)/shard_map/tensor_sum/pallas_call | solution.py:109
  533.1 55.6 %collective-permute-start.2 = (bf16[1024,256]{1,0:T(8,128)(2,1)S(1)}, bf16[1024,256]{1,0:T(8,128)(2,1)S(1)}, u32[]{:S(2)}, u32[]{:S(2)}) collective-permute-start(bf16[1024,256]{1,0:T(8,128)(2,1)S(1)} %fusion.54), channel_id=1, source_target_pairs={{0,8},{4,12},{8,16},{12,20},{1,9},{5,13},{9,17},{13,21},{2,10},{6,... | collective-permute-start | bytes 1572872 | tf_op jit(solution)/shard_map/ppermute | solution.py:256
  588.8 3.7 convolution_convert_fusion.6
  592.5 7.9 collective-permute-done.2
  602.3 3.7 convolution_convert_fusion.7
  606.0 46.1 %collective-permute-start.3 = (bf16[1024,256]{1,0:T(8,128)(2,1)S(1)}, bf16[1024,256]{1,0:T(8,128)(2,1)S(1)}, u32[]{:S(2)}, u32[]{:S(2)}) collective-permute-start(bf16[1024,256]{1,0:T(8,128)(2,1)S(1)} %get-tuple-element.70), channel_id=1, source_target_pairs={{0,8},{4,12},{8,16},{12,20},{16,24},{20,28},{1,9},{5,13},{9,17},{1... | collective-permute-start | bytes 1572872 | tf_op jit(solution)/shard_map/ppermute | solution.py:256
  652.1 6.1 collective-permute-done.5
  674.1 5.4 fusion.24
  686.3 21.0 %all-reduce.4.cloned.1.call-done = bf16[1024,256]{1,0:T(8,128)(2,1)} async-done(((bf16[1024,256]{1,0:T(8,128)(2,1)}), bf16[1024,256]{1,0:T(8,128)(2,1)}) %all-reduce.4.cloned.1.call-update) | async-done | bytes 524304 | tf_op jit(solution)/shard_map/psum | solution.py:504
  707.4 3.7 convolution_convert_fusion.8
  711.1 9.1 pad_maximum_fusion
  720.2 9.5 reshape.180
  729.7 13.4 %constant_dynamic-slice_fusion.3 = (bf16[4,1,256,1280]{2,1,0,3:T(2,128)(2,1)}, bf16[4,1,256,1280]{2,1,0,3:T(2,128)(2,1)S(1)}) fusion(bf16[4,2,256,1280]{2,1,0,3:T(2,128)(2,1)} %reshape.180, s32[]{:T(128)S(6)} %select_n.54, s32[]{:T(128)S(6)} %select_n.55), kind=kLoop, calls=%fused_computation.130 | loop fusion | bytes 10485768 | tf_op jit(solution)/shard_map/jit(dynamic_index_in_dim)/dynamic_slice | solution.py:282
  748.9 3.9 fusion.10
  753.8 55.9 %small_sum.1 = f32[120,128]{1,0:T(8,128)} custom-call(f32[120,128]{1,0:T(8,128)} %pad_bitcast_fusion.own_ref), custom_call_target="tpu_custom_call" | custom-call | tf_op jit(solution)/shard_map/small_sum/pallas_call | solution.py:225
  812.3 11.7 %add_add_fusion.2 = f32[1024,2048]{1,0:T(8,128)} fusion(f32[1024,2048]{1,0:T(8,128)} %get-tuple-element.51, f32[1024]{0:T(1024)S(1)} %negate_multiply_fusion, f32[1024]{0:T(1024)S(1)} %multiply_multiply_fusion.2, f32[1024]{0:T(1024)S(1)} %copy-done.31, bf16[1024,2048]{1,0:T(8,128)(2,1)} %param.16, f32[1024]{0:T(1024)S(1)} %copy-done.36, ...), kind=kLoop, calls=%fused_computation.40 | loop fusion | flops 18874368 | bytes 29384704 | tf_op jit(solution)/shard_map/add | solution.py:509
  825.7 3.4 collective-permute-start.23
  836.9 16.8 %collective-permute-done.23 = bf16[256,2048]{0,1:T(8,128)(2,1)S(1)} collective-permute-done((bf16[256,2048]{0,1:T(8,128)(2,1)S(1)}, bf16[256,2048]{0,1:T(8,128)(2,1)S(1)}, u32[]{:S(2)}, u32[]{:S(2)}) %collective-permute-start.23) | collective-permute-done | bytes 1048608 | tf_op jit(solution)/shard_map/ppermute | solution.py:256
  856.7 4.6 collective-permute-start.24
  861.3 6.4 collective-permute-done.8
  870.6 19.6 %collective-permute-done.16 = bf16[256,2048]{1,0:T(8,128)(2,1)S(1)} collective-permute-done((bf16[256,2048]{1,0:T(8,128)(2,1)S(1)}, bf16[256,2048]{1,0:T(8,128)(2,1)S(1)}, u32[]{:S(2)}, u32[]{:S(2)}) %collective-permute-start.16) | collective-permute-done | bytes 1048608 | tf_op jit(solution)/shard_map/ppermute | solution.py:256
  895.8 28.2 %collective-permute-done.9 = bf16[256,1280]{0,1:T(8,128)(2,1)S(1)} collective-permute-done((bf16[256,1280]{0,1:T(8,128)(2,1)S(1)}, bf16[256,1280]{0,1:T(8,128)(2,1)S(1)}, u32[]{:S(2)}, u32[]{:S(2)}) %collective-permute-start.9) | collective-permute-done | bytes 655392 | tf_op jit(solution)/shard_map/ppermute | solution.py:256
  926.9 4.5 collective-permute-start.17
  933.8 23.0 %collective-permute-done.12 = bf16[256,1280]{0,1:T(8,128)(2,1)S(1)} collective-permute-done((bf16[256,1280]{0,1:T(8,128)(2,1)S(1)}, bf16[256,1280]{0,1:T(8,128)(2,1)S(1)}, u32[]{:S(2)}, u32[]{:S(2)}) %collective-permute-start.12) | collective-permute-done | bytes 655392 | tf_op jit(solution)/shard_map/ppermute | solution.py:256
  964.7 14.5 %collective-permute-done.20 = bf16[256,2048]{1,0:T(8,128)(2,1)S(1)} collective-permute-done((bf16[256,2048]{1,0:T(8,128)(2,1)S(1)}, bf16[256,2048]{1,0:T(8,128)(2,1)S(1)}, u32[]{:S(2)}, u32[]{:S(2)}) %collective-permute-start.20) | collective-permute-done | bytes 1048608 | tf_op jit(solution)/shard_map/ppermute | solution.py:256
  981.1 5.8 collective-permute-done.13
  (220 shorter events, 106.0 us)
Async XLA Ops:
  7.2 97.8 %copy-start = (bf16[512,2048]{1,0:T(8,128)(2,1)S(1)}, bf16[512,2048]{1,0:T(8,128)(2,1)}, u32[]{:S(2)}) copy-start(bf16[512,2048]{1,0:T(8,128)(2,1)} %param.23) | copy-start | bytes 6291460
  7.2 700.1 %all-reduce.4.cloned.1.call-start = ((), (), s32[]{:S(2)}) async-start(), calls=%async_computation | async-start | bytes 1048576 | tf_op jit(solution)/shard_map/psum | solution.py:504
  17.9 46.1 %copy-start.48 = (f32[512]{0:T(512)S(1)}, f32[512]{0:T(512)}, u32[]{:S(2)}) copy-start(f32[512]{0:T(512)} %param.20) | copy-start | bytes 6148
  69.2 35.8 %copy-start.8 = (bf16[1024,512]{1,0:T(8,128)(2,1)}, bf16[1024,512]{1,0:T(8,128)(2,1)S(1)}, u32[]{:S(2)}) copy-start(bf16[1024,512]{1,0:T(8,128)(2,1)S(1)} %multiply_convert_fusion.1.q_ref) | copy-start | bytes 3145732
  105.0 52.4 %copy-start.6 = (bf16[1024,512]{1,0:T(8,128)(2,1)}, bf16[1024,512]{1,0:T(8,128)(2,1)S(1)}, u32[]{:S(2)}) copy-start(bf16[1024,512]{1,0:T(8,128)(2,1)S(1)} %get-tuple-element.20.ctx_ref) | copy-start | bytes 3145732
  105.0 52.4 %copy-start.9 = (f32[4,1024]{1,0:T(4,128)}, f32[4,1024]{1,0:T(4,128)S(1)}, u32[]{:S(2)}) copy-start(f32[4,1024]{1,0:T(4,128)S(1)} %get-tuple-element.21.lse_ref) | copy-start | bytes 49156
  105.0 52.4 %copy-start.11 = (bf16[1024,2048]{1,0:T(8,128)(2,1)S(1)}, bf16[1024,2048]{1,0:T(8,128)(2,1)}, u32[]{:S(2)}) copy-start(bf16[1024,2048]{1,0:T(8,128)(2,1)} %param.16) | copy-start | bytes 12582916
  105.0 52.4 %copy-start.28 = (f32[2048]{0:T(1024)S(1)}, f32[2048]{0:T(1024)}, u32[]{:S(2)}) copy-start(f32[2048]{0:T(1024)} %param.24) | copy-start | bytes 24580
  200.3 459.9 %collective-permute-start.21 = (bf16[4,256,2048]{1,2,0:T(8,128)(2,1)}, bf16[4,256,2048]{1,2,0:T(8,128)(2,1)}, u32[]{:S(2)}, u32[]{:S(2)}) collective-permute-start(bf16[4,256,2048]{1,2,0:T(8,128)(2,1)} %bitcast.167), channel_id=1, source_target_pairs={{0,4},{4,0},{8,12},{12,8},{16,20},{20,16},{24,28},{28,24},{1,5},{5... | collective-permute-start | bytes 12582920 | tf_op jit(solution)/shard_map/ppermute | solution.py:258
  245.3 51.1 %copy-start.3 = (bf16[1024,2048]{1,0:T(8,128)(2,1)S(1)}, bf16[1024,2048]{1,0:T(8,128)(2,1)}, u32[]{:S(2)}) copy-start(bf16[1024,2048]{1,0:T(8,128)(2,1)} %copy-done.2) | copy-start | bytes 12582916
  245.3 51.1 %copy-start.12 = (bf16[1024,2048]{1,0:T(8,128)(2,1)S(1)}, bf16[1024,2048]{1,0:T(8,128)(2,1)}, u32[]{:S(2)}) copy-start(bf16[1024,2048]{1,0:T(8,128)(2,1)} %param.16) | copy-start | bytes 12582916
  300.0 56.6 %copy-start.22 = (bf16[1024,2048]{1,0:T(8,128)(2,1)S(1)}, bf16[1024,2048]{1,0:T(8,128)(2,1)}, u32[]{:S(2)}) copy-start(bf16[1024,2048]{1,0:T(8,128)(2,1)} %param.31) | copy-start | bytes 12582916
  300.0 56.6 %copy-start.40 = (f32[2048]{0:T(1024)S(1)}, f32[2048]{0:T(1024)}, u32[]{:S(2)}) copy-start(f32[2048]{0:T(1024)} %param.30) | copy-start | bytes 24580
  426.0 48.7 %collective-permute-start = (bf16[4,1024,256]{2,1,0:T(8,128)(2,1)}, bf16[4,1024,256]{2,1,0:T(8,128)(2,1)S(1)}, u32[]{:S(2)}, u32[]{:S(2)}) collective-permute-start(bf16[4,1024,256]{2,1,0:T(8,128)(2,1)} %dynamic-slice_bitcast_fusion.1), channel_id=1, source_target_pairs={{0,4},{4,0},{8,12},{12,8},{16,20},{20,16},{24,28},{28,24},{1,5},{5... | collective-permute-start | bytes 6291464 | tf_op jit(solution)/shard_map/ppermute | solution.py:258
  444.5 229.7 %collective-permute-start.14 = (bf16[4,256,2048]{2,1,0:T(8,128)(2,1)}, bf16[4,256,2048]{2,1,0:T(8,128)(2,1)}, u32[]{:S(2)}, u32[]{:S(2)}) collective-permute-start(bf16[4,256,2048]{2,1,0:T(8,128)(2,1)} %dynamic-slice_bitcast_fusion), channel_id=1, source_target_pairs={{0,4},{4,0},{8,12},{12,8},{16,20},{20,16},{24,28},{28,24},{1,5},{5... | collective-permute-start | bytes 12582920 | tf_op jit(solution)/shard_map/ppermute | solution.py:258
  446.5 31.8 %copy-start.27 = (bf16[1024,512]{1,0:T(8,128)(2,1)S(1)}, bf16[1024,512]{1,0:T(8,128)(2,1)}, u32[]{:S(2)}) copy-start(bf16[1024,512]{1,0:T(8,128)(2,1)} %get-tuple-element.22) | copy-start | bytes 3145732
  474.7 114.1 %slice-start = ((s8[8388608]{0:T(1024)(128)(4,1)}), s8[4194304]{0:T(1024)(128)(4,1)S(1)}, s32[]{:S(2)}) async-start(s8[8388608]{0:T(1024)(128)(4,1)} %bitcast.156), calls=%async_computation.1 | async-start | bytes 8388608
  477.0 56.0 %collective-permute-start.1 = (bf16[1024,256]{1,0:T(8,128)(2,1)S(1)}, bf16[1024,256]{1,0:T(8,128)(2,1)S(1)}, u32[]{:S(2)}, u32[]{:S(2)}) collective-permute-start(bf16[1024,256]{1,0:T(8,128)(2,1)S(1)} %get-tuple-element.72), channel_id=1, source_target_pairs={{0,8},{4,12},{1,9},{5,13},{2,10},{6,14},{3,11},{7,15}} | collective-permute-start | bytes 1572872 | tf_op jit(solution)/shard_map/ppermute | solution.py:256
  478.3 110.4 %slice-start.1 = ((s8[8388608]{0:T(1024)(128)(4,1)}), s8[4194304]{0:T(1024)(128)(4,1)S(1)}, s32[]{:S(2)}) async-start(s8[8388608]{0:T(1024)(128)(4,1)} %bitcast.156), calls=%async_computation.2 | async-start | bytes 8388608
  480.7 108.0 %copy-start.7 = (bf16[1024,512]{1,0:T(8,128)(2,1)S(1)}, bf16[1024,512]{1,0:T(8,128)(2,1)}, u32[]{:S(2)}) copy-start(bf16[1024,512]{1,0:T(8,128)(2,1)} %copy-done.6) | copy-start | bytes 3145732
  531.8 60.6 %copy-start.4 = (bf16[1024,2048]{1,0:T(8,128)(2,1)}, bf16[1024,2048]{1,0:T(8,128)(2,1)S(1)}, u32[]{:S(2)}) copy-start(bf16[1024,2048]{1,0:T(8,128)(2,1)S(1)} %tensor_sum.7) | copy-start | bytes 12582916
  532.1 60.4 %collective-permute-start.4 = (bf16[1024,256]{1,0:T(8,128)(2,1)S(1)}, bf16[1024,256]{1,0:T(8,128)(2,1)S(1)}, u32[]{:S(2)}, u32[]{:S(2)}) collective-permute-start(bf16[1024,256]{1,0:T(8,128)(2,1)S(1)} %get-tuple-element.73), channel_id=1, source_target_pairs={{24,16},{28,20},{25,17},{29,21},{26,18},{30,22},{27,19},{31,23}} | collective-permute-start | bytes 1572872 | tf_op jit(solution)/shard_map/ppermute | solution.py:256
  533.1 69.2 %copy-start.24 = (bf16[1024,2048]{1,0:T(8,128)(2,1)S(1)}, bf16[1024,2048]{1,0:T(8,128)(2,1)}, u32[]{:S(2)}) copy-start(bf16[1024,2048]{1,0:T(8,128)(2,1)} %copy-done.23) | copy-start | bytes 12582916
  533.1 67.3 %collective-permute-start.2 = (bf16[1024,256]{1,0:T(8,128)(2,1)S(1)}, bf16[1024,256]{1,0:T(8,128)(2,1)S(1)}, u32[]{:S(2)}, u32[]{:S(2)}) collective-permute-start(bf16[1024,256]{1,0:T(8,128)(2,1)S(1)} %fusion.54), channel_id=1, source_target_pairs={{0,8},{4,12},{8,16},{12,20},{1,9},{5,13},{9,17},{13,21},{2,10},{6,... | collective-permute-start | bytes 1572872 | tf_op jit(solution)/shard_map/ppermute | solution.py:256
  600.7 59.5 %copy-start.19 = (bf16[4,1,256,2048]{2,3,0,1:T(8,128)(2,1)S(1)}, bf16[4,1,256,2048]{2,3,0,1:T(8,128)(2,1)}, u32[]{:S(2)}) copy-start(bf16[4,1,256,2048]{2,3,0,1:T(8,128)(2,1)} %copy.41) | copy-start | bytes 12582916
  600.7 57.4 %collective-permute-start.5 = (bf16[1024,256]{1,0:T(8,128)(2,1)S(1)}, bf16[1024,256]{1,0:T(8,128)(2,1)S(1)}, u32[]{:S(2)}, u32[]{:S(2)}) collective-permute-start(bf16[1024,256]{1,0:T(8,128)(2,1)S(1)} %get-tuple-element.71), channel_id=1, source_target_pairs={{16,8},{20,12},{24,16},{28,20},{17,9},{21,13},{25,17},{29,21},{18,... | collective-permute-start | bytes 1572872 | tf_op jit(solution)/shard_map/ppermute | solution.py:256
  606.0 64.1 %collective-permute-start.3 = (bf16[1024,256]{1,0:T(8,128)(2,1)S(1)}, bf16[1024,256]{1,0:T(8,128)(2,1)S(1)}, u32[]{:S(2)}, u32[]{:S(2)}) collective-permute-start(bf16[1024,256]{1,0:T(8,128)(2,1)S(1)} %get-tuple-element.70), channel_id=1, source_target_pairs={{0,8},{4,12},{8,16},{12,20},{16,24},{20,28},{1,9},{5,13},{9,17},{1... | collective-permute-start | bytes 1572872 | tf_op jit(solution)/shard_map/ppermute | solution.py:256
  658.3 14.8 %collective-permute-start.6 = (bf16[1024,256]{1,0:T(8,128)(2,1)S(1)}, bf16[1024,256]{1,0:T(8,128)(2,1)S(1)}, u32[]{:S(2)}, u32[]{:S(2)}) collective-permute-start(bf16[1024,256]{1,0:T(8,128)(2,1)S(1)} %fusion.53), channel_id=1, source_target_pairs={{8,0},{12,4},{16,8},{20,12},{24,16},{28,20},{9,1},{13,5},{17,9},{2... | collective-permute-start | bytes 1572872 | tf_op jit(solution)/shard_map/ppermute | solution.py:256
  667.2 156.9 %collective-permute-start.22 = (bf16[256,2048]{0,1:T(8,128)(2,1)}, bf16[256,2048]{0,1:T(8,128)(2,1)}, u32[]{:S(2)}, u32[]{:S(2)}) collective-permute-start(bf16[256,2048]{0,1:T(8,128)(2,1)} %get-tuple-element.59), channel_id=1, source_target_pairs={{0,8},{4,12},{1,9},{5,13},{2,10},{6,14},{3,11},{7,15}} | collective-permute-start | bytes 3145736 | tf_op jit(solution)/shard_map/ppermute | solution.py:256
  668.4 168.4 %collective-permute-start.25 = (bf16[256,2048]{0,1:T(8,128)(2,1)}, bf16[256,2048]{0,1:T(8,128)(2,1)}, u32[]{:S(2)}, u32[]{:S(2)}) collective-permute-start(bf16[256,2048]{0,1:T(8,128)(2,1)} %get-tuple-element.60), channel_id=1, source_target_pairs={{24,16},{28,20},{25,17},{29,21},{26,18},{30,22},{27,19},{31,23}} | collective-permute-start | bytes 3145736 | tf_op jit(solution)/shard_map/ppermute | solution.py:256
  683.0 150.3 %collective-permute-start.15 = (bf16[256,2048]{1,0:T(8,128)(2,1)}, bf16[256,2048]{1,0:T(8,128)(2,1)}, u32[]{:S(2)}, u32[]{:S(2)}) collective-permute-start(bf16[256,2048]{1,0:T(8,128)(2,1)} %get-tuple-element.63), channel_id=1, source_target_pairs={{0,8},{4,12},{1,9},{5,13},{2,10},{6,14},{3,11},{7,15}} | collective-permute-start | bytes 3145736 | tf_op jit(solution)/shard_map/ppermute | solution.py:256
  684.3 184.3 %collective-permute-start.18 = (bf16[256,2048]{1,0:T(8,128)(2,1)}, bf16[256,2048]{1,0:T(8,128)(2,1)}, u32[]{:S(2)}, u32[]{:S(2)}) collective-permute-start(bf16[256,2048]{1,0:T(8,128)(2,1)} %get-tuple-element.64), channel_id=1, source_target_pairs={{24,16},{28,20},{25,17},{29,21},{26,18},{30,22},{27,19},{31,23}} | collective-permute-start | bytes 3145736 | tf_op jit(solution)/shard_map/ppermute | solution.py:256
  745.5 83.6 %collective-permute-start.7 = (bf16[4,256,1280]{1,2,0:T(8,128)(2,1)}, bf16[4,256,1280]{1,2,0:T(8,128)(2,1)}, u32[]{:S(2)}, u32[]{:S(2)}) collective-permute-start(bf16[4,256,1280]{1,2,0:T(8,128)(2,1)} %bitcast.155), channel_id=1, source_target_pairs={{0,4},{4,0},{8,12},{12,8},{16,20},{20,16},{24,28},{28,24},{1,5},{5... | collective-permute-start | bytes 7864328 | tf_op jit(solution)/shard_map/ppermute | solution.py:258
  752.9 76.2 %slice-start.2 = ((s8[5242880]{0:T(1024)(128)(4,1)}), s8[1048576]{0:T(1024)(128)(4,1)S(1)}, s32[]{:S(2)}) async-start(s8[5242880]{0:T(1024)(128)(4,1)} %bitcast.158), calls=%async_computation.3 | async-start | bytes 2097152
  825.7 28.0 %collective-permute-start.23 = (bf16[256,2048]{0,1:T(8,128)(2,1)S(1)}, bf16[256,2048]{0,1:T(8,128)(2,1)S(1)}, u32[]{:S(2)}, u32[]{:S(2)}) collective-permute-start(bf16[256,2048]{0,1:T(8,128)(2,1)S(1)} %fusion.31), channel_id=1, source_target_pairs={{0,8},{4,12},{8,16},{12,20},{1,9},{5,13},{9,17},{13,21},{2,10},{6,... | collective-permute-start | bytes 3145736 | tf_op jit(solution)/shard_map/ppermute | solution.py:256
  832.0 35.7 %collective-permute-start.8 = (bf16[256,1280]{0,1:T(8,128)(2,1)S(1)}, bf16[256,1280]{0,1:T(8,128)(2,1)S(1)}, u32[]{:S(2)}, u32[]{:S(2)}) collective-permute-start(bf16[256,1280]{0,1:T(8,128)(2,1)S(1)} %get-tuple-element.68), channel_id=1, source_target_pairs={{0,8},{4,12},{1,9},{5,13},{2,10},{6,14},{3,11},{7,15}} | collective-permute-start | bytes 1966088 | tf_op jit(solution)/shard_map/ppermute | solution.py:256
  834.9 55.3 %collective-permute-start.16 = (bf16[256,2048]{1,0:T(8,128)(2,1)S(1)}, bf16[256,2048]{1,0:T(8,128)(2,1)S(1)}, u32[]{:S(2)}, u32[]{:S(2)}) collective-permute-start(bf16[256,2048]{1,0:T(8,128)(2,1)S(1)} %fusion.37), channel_id=1, source_target_pairs={{0,8},{4,12},{8,16},{12,20},{1,9},{5,13},{9,17},{13,21},{2,10},{6,... | collective-permute-start | bytes 3145736 | tf_op jit(solution)/shard_map/ppermute | solution.py:256
  855.4 38.1 %collective-permute-start.26 = (bf16[256,2048]{0,1:T(8,128)(2,1)S(1)}, bf16[256,2048]{0,1:T(8,128)(2,1)S(1)}, u32[]{:S(2)}, u32[]{:S(2)}) collective-permute-start(bf16[256,2048]{0,1:T(8,128)(2,1)S(1)} %get-tuple-element.58), channel_id=1, source_target_pairs={{16,8},{20,12},{24,16},{28,20},{17,9},{21,13},{25,17},{29,21},{18,... | collective-permute-start | bytes 3145736 | tf_op jit(solution)/shard_map/ppermute | solution.py:256
  856.7 103.3 %collective-permute-start.24 = (bf16[256,2048]{0,1:T(8,128)(2,1)S(1)}, bf16[256,2048]{0,1:T(8,128)(2,1)S(1)}, u32[]{:S(2)}, u32[]{:S(2)}) collective-permute-start(bf16[256,2048]{0,1:T(8,128)(2,1)S(1)} %get-tuple-element.57), channel_id=1, source_target_pairs={{0,8},{4,12},{8,16},{12,20},{16,24},{20,28},{1,9},{5,13},{9,17},{1... | collective-permute-start | bytes 3145736 | tf_op jit(solution)/shard_map/ppermute | solution.py:256
  867.7 28.0 %collective-permute-start.11 = (bf16[256,1280]{0,1:T(8,128)(2,1)S(1)}, bf16[256,1280]{0,1:T(8,128)(2,1)S(1)}, u32[]{:S(2)}, u32[]{:S(2)}) collective-permute-start(bf16[256,1280]{0,1:T(8,128)(2,1)S(1)} %get-tuple-element.69), channel_id=1, source_target_pairs={{24,16},{28,20},{25,17},{29,21},{26,18},{30,22},{27,19},{31,23}} | collective-permute-start | bytes 1966088 | tf_op jit(solution)/shard_map/ppermute | solution.py:256
  868.6 55.3 %collective-permute-start.9 = (bf16[256,1280]{0,1:T(8,128)(2,1)S(1)}, bf16[256,1280]{0,1:T(8,128)(2,1)S(1)}, u32[]{:S(2)}, u32[]{:S(2)}) collective-permute-start(bf16[256,1280]{0,1:T(8,128)(2,1)S(1)} %fusion.48), channel_id=1, source_target_pairs={{0,8},{4,12},{8,16},{12,20},{1,9},{5,13},{9,17},{13,21},{2,10},{6,... | collective-permute-start | bytes 1966088 | tf_op jit(solution)/shard_map/ppermute | solution.py:256
  892.2 39.2 %collective-permute-start.19 = (bf16[256,2048]{1,0:T(8,128)(2,1)S(1)}, bf16[256,2048]{1,0:T(8,128)(2,1)S(1)}, u32[]{:S(2)}, u32[]{:S(2)}) collective-permute-start(bf16[256,2048]{1,0:T(8,128)(2,1)S(1)} %get-tuple-element.62), channel_id=1, source_target_pairs={{16,8},{20,12},{24,16},{28,20},{17,9},{21,13},{25,17},{29,21},{18,... | collective-permute-start | bytes 3145736 | tf_op jit(solution)/shard_map/ppermute | solution.py:256
  893.8 69.2 %collective-permute-start.27 = (bf16[256,2048]{0,1:T(8,128)(2,1)S(1)}, bf16[256,2048]{0,1:T(8,128)(2,1)S(1)}, u32[]{:S(2)}, u32[]{:S(2)}) collective-permute-start(bf16[256,2048]{0,1:T(8,128)(2,1)S(1)} %fusion.30), channel_id=1, source_target_pairs={{8,0},{12,4},{16,8},{20,12},{24,16},{28,20},{9,1},{13,5},{17,9},{2... | collective-permute-start | bytes 3145736 | tf_op jit(solution)/shard_map/ppermute | solution.py:256
  924.4 32.4 %collective-permute-start.12 = (bf16[256,1280]{0,1:T(8,128)(2,1)S(1)}, bf16[256,1280]{0,1:T(8,128)(2,1)S(1)}, u32[]{:S(2)}, u32[]{:S(2)}) collective-permute-start(bf16[256,1280]{0,1:T(8,128)(2,1)S(1)} %get-tuple-element.67), channel_id=1, source_target_pairs={{16,8},{20,12},{24,16},{28,20},{17,9},{21,13},{25,17},{29,21},{18,... | collective-permute-start | bytes 1966088 | tf_op jit(solution)/shard_map/ppermute | solution.py:256
  926.9 37.9 %collective-permute-start.17 = (bf16[256,2048]{1,0:T(8,128)(2,1)S(1)}, bf16[256,2048]{1,0:T(8,128)(2,1)S(1)}, u32[]{:S(2)}, u32[]{:S(2)}) collective-permute-start(bf16[256,2048]{1,0:T(8,128)(2,1)S(1)} %get-tuple-element.61), channel_id=1, source_target_pairs={{0,8},{4,12},{8,16},{12,20},{16,24},{20,28},{1,9},{5,13},{9,17},{1... | collective-permute-start | bytes 3145736 | tf_op jit(solution)/shard_map/ppermute | solution.py:256
  931.8 47.4 %collective-permute-start.20 = (bf16[256,2048]{1,0:T(8,128)(2,1)S(1)}, bf16[256,2048]{1,0:T(8,128)(2,1)S(1)}, u32[]{:S(2)}, u32[]{:S(2)}) collective-permute-start(bf16[256,2048]{1,0:T(8,128)(2,1)S(1)} %fusion.36), channel_id=1, source_target_pairs={{8,0},{12,4},{16,8},{20,12},{24,16},{28,20},{9,1},{13,5},{17,9},{2... | collective-permute-start | bytes 3145736 | tf_op jit(solution)/shard_map/ppermute | solution.py:256
  956.8 24.3 %collective-permute-start.10 = (bf16[256,1280]{0,1:T(8,128)(2,1)S(1)}, bf16[256,1280]{0,1:T(8,128)(2,1)S(1)}, u32[]{:S(2)}, u32[]{:S(2)}) collective-permute-start(bf16[256,1280]{0,1:T(8,128)(2,1)S(1)} %get-tuple-element.66), channel_id=1, source_target_pairs={{0,8},{4,12},{8,16},{12,20},{16,24},{20,28},{1,9},{5,13},{9,17},{1... | collective-permute-start | bytes 1966088 | tf_op jit(solution)/shard_map/ppermute | solution.py:256
  960.1 26.8 %collective-permute-start.13 = (bf16[256,1280]{0,1:T(8,128)(2,1)S(1)}, bf16[256,1280]{0,1:T(8,128)(2,1)S(1)}, u32[]{:S(2)}, u32[]{:S(2)}) collective-permute-start(bf16[256,1280]{0,1:T(8,128)(2,1)S(1)} %fusion.47), channel_id=1, source_target_pairs={{8,0},{12,4},{16,8},{20,12},{24,16},{28,20},{9,1},{13,5},{17,9},{2... | collective-permute-start | bytes 1966088 | tf_op jit(solution)/shard_map/ppermute | solution.py:256
  (37 other events, 393.3 us)
Sparse Core Ops, SparseCore 0:
  674.2 33.0 all-reduce.3

commit v2 on v1

v2 whole, which is shorter than its diff:
```python
import functools

import jax
import jax.numpy as jnp
from jax import lax
from jax.experimental import pallas as pl
from jax.experimental.pallas import tpu as pltpu
from jax.sharding import PartitionSpec as P

SPAN = 8
EPSILON = 1e-05
NEG_LARGE = -1e30
MESH = pl.DeviceIdType.MESH
VMEM = pl.BlockSpec(memory_space=pltpu.VMEM)
F32 = jnp.float32
BF16 = jnp.bfloat16


def contract(left, right, left_dim, right_dim):
    return lax.dot_general(
        left, right, (((left_dim,), (right_dim,)), ((), ())), preferred_element_type=F32
    )


def remote(source, target, send_sem, recv_sem, device):
    return pltpu.make_async_remote_copy(
        src_ref=source,
        dst_ref=target,
        send_sem=send_sem,
        recv_sem=recv_sem,
        device_id=device,
        device_id_type=MESH,
    )


def greet(devices):
    barrier = pltpu.get_barrier_semaphore()
    for device in devices:
        pl.semaphore_signal(barrier, inc=1, device_id=device, device_id_type=MESH)
    pl.semaphore_wait(barrier, len(devices))


class TensorSum:
    def __init__(self, chunks, part, result, from_core, summed, from_y, sems):
        block = lax.axis_index("dp")
        lane = lax.axis_index("tensor")
        core = lax.rem(lane, 2)
        self.core_peer = (block, lane + 1 - 2 * core)
        self.y_peer = (block, lax.rem(lane + 2, 4))
        rows, width = part.shape
        half = width // 2
        self.step = rows // chunks
        self.mine = pl.ds(pl.multiple_of(core * half, half), half)
        self.other = pl.ds(pl.multiple_of((1 - core) * half, half), half)
        self.part, self.result = part, result
        self.from_core, self.summed, self.from_y = from_core, summed, from_y
        self.sems = sems

    def span(self, k):
        return pl.ds(pl.multiple_of(k * self.step, self.step), self.step)

    def to_core(self, k):
        at = self.span(k)
        return remote(
            self.part.at[at, self.other], self.from_core.at[at], self.sems[0].at[k],
            self.sems[1].at[k], self.core_peer,
        )

    def to_y(self, k):
        at = self.span(k)
        return remote(
            self.summed.at[at], self.from_y.at[at], self.sems[2].at[k], self.sems[3].at[k],
            self.y_peer,
        )

    def back(self, k):
        at = self.span(k)
        return remote(
            self.result.at[at, self.mine], self.result.at[at, self.mine], self.sems[4].at[k],
            self.sems[5].at[k], self.core_peer,
        )

    def first(self, k):
        self.to_core(k).start()

    def second(self, k):
        at = self.span(k)
        self.to_core(k).wait_recv()
        total = self.part[at, self.mine].astype(F32) + self.from_core[at].astype(F32)
        self.summed[at] = total.astype(BF16)
        self.to_y(k).start()

    def third(self, k):
        at = self.span(k)
        self.to_y(k).wait_recv()
        total = self.summed[at].astype(F32) + self.from_y[at].astype(F32)
        self.result[at, self.mine] = total.astype(BF16)
        self.back(k).start()

    def finish(self, chunks):
        @pl.loop(0, chunks)
        def _(k):
            self.back(k).wait_recv()
            self.back(k).wait_send()
            self.to_core(k).wait_send()
            self.to_y(k).wait_send()


def sum_scratch(chunks, rows, width):
    half = pltpu.VMEM((rows, width // 2), BF16)
    return [pltpu.VMEM((rows, width), BF16), half, half, half] + [
        pltpu.SemaphoreType.DMA((chunks,))
    ] * 6


def grad_rows(left_ref, right, target, which):
    levels, rows = target.shape[0], target.shape[1]

    @pl.loop(0, levels)
    def _(lev):
        if rows % 128 == 0:
            cols = pl.ds(pl.multiple_of((2 * lev + which) * rows, rows), rows)
            target[lev] = contract(left_ref[:, cols], right[...], 0, 0).astype(BF16)
        else:
            cols = pl.ds(pl.multiple_of(2 * lev * rows, 2 * rows), 2 * rows)
            both = contract(left_ref[:, cols], right[...], 0, 0)
            target[lev] = jnp.where(which == 0, both[:rows], both[rows:]).astype(BF16)


def project_kernel(
    chunks, ctx_ref, wo_ref, cot_ref, wd_ref, out_ref, g_ref, part, from_core, summed, from_y, *sems
):
    ts = TensorSum(chunks, part, out_ref, from_core, summed, from_y, sems)
    greet([ts.core_peer, ts.y_peer])

    @pl.loop(0, chunks)
    def _(k):
        at = ts.span(k)
        part[at, :] = jnp.dot(
            ctx_ref[at, :], wo_ref[...], preferred_element_type=F32
        ).astype(BF16)
        ts.first(k)

        @pl.when(k >= 1)
        def _():
            ts.second(k - 1)

    ts.second(chunks - 1)
    tile = g_ref.shape[1] // 8

    @pl.loop(0, 8)
    def _(j):
        cols = pl.ds(pl.multiple_of(j * tile, tile), tile)
        g_ref[:, cols] = contract(cot_ref[...], wd_ref[cols, :], 1, 1).astype(BF16)

    @pl.loop(0, chunks)
    def _(k):
        ts.third(k)

    ts.finish(chunks)


def project(context, output_weight, cotangent, down_weight, chunks=8):
    rows, width = context.shape[0], output_weight.shape[1]
    return pl.pallas_call(
        functools.partial(project_kernel, chunks),
        out_shape=(
            jax.ShapeDtypeStruct((rows, width), BF16),
            jax.ShapeDtypeStruct((rows, down_weight.shape[0]), BF16),
        ),
        in_specs=[VMEM] * 4,
        out_specs=(VMEM, VMEM),
        scratch_shapes=sum_scratch(chunks, rows, width),
        compiler_params=pltpu.CompilerParams(
            collective_id=3, has_side_effects=True, vmem_limit_bytes=56 << 20
        ),
        name="project",
    )(context, output_weight, cotangent, down_weight)


def hidden_back_kernel(
    chunks, dpre_ref, wu_ref, n2_ref, sent_ref, dn_ref, own_ref, other_ref, got_ref, x_send, x_recv,
    part, from_core, summed, from_y, *sems,
):
    ts = TensorSum(chunks, part, dn_ref, from_core, summed, from_y, sems)
    side = lax.rem(lax.axis_index("dp"), 2)
    x_peer = (lax.axis_index("dp") + 1 - 2 * side, lax.axis_index("tensor"))
    greet([ts.core_peer, ts.y_peer, x_peer])
    levels, rows = own_ref.shape[0], own_ref.shape[1]
    to_x = remote(sent_ref.at[pl.ds(0, got_ref.shape[0])], got_ref, x_send, x_recv, x_peer)
    to_x.start()

    @pl.loop(0, chunks)
    def _(k):
        at = ts.span(k)
        part[at, :] = contract(dpre_ref[at, :], wu_ref[...], 1, 1).astype(BF16)
        ts.first(k)

        @pl.when(k >= 1)
        def _():
            ts.second(k - 1)

    ts.second(chunks - 1)

    def grad(target, which):
        grad_rows(n2_ref, dpre_ref, target, which)

    grad(other_ref, 1 - side)
    grad(own_ref, side)

    @pl.loop(0, chunks)
    def _(k):
        ts.third(k)

    ts.finish(chunks)
    to_x.wait()


def hidden_back(d_pre, up_weight, normed2, sent, count, chunks=4):
    rows, width = d_pre.shape[0], up_weight.shape[0]
    half = jax.ShapeDtypeStruct((count // 2, width // count, up_weight.shape[1]), BF16)
    got = jax.ShapeDtypeStruct((sent.shape[0] * 3 // 4,) + sent.shape[1:], BF16)
    hbm = pl.BlockSpec(memory_space=pl.ANY)
    return pl.pallas_call(
        functools.partial(hidden_back_kernel, chunks),
        out_shape=(jax.ShapeDtypeStruct((rows, width), BF16), half, half, got),
        in_specs=[VMEM] * 3 + [hbm],
        out_specs=(VMEM,) * 3 + (hbm,),
        scratch_shapes=[pltpu.SemaphoreType.DMA, pltpu.SemaphoreType.DMA]
        + sum_scratch(chunks, rows, width),
        compiler_params=pltpu.CompilerParams(
            collective_id=4, has_side_effects=True, vmem_limit_bytes=58 << 20
        ),
        name="hidden_back",
    )(d_pre, up_weight, normed2, sent)


class Chain:
    def __init__(self, length, level, upper, lower, pair, bufs, sems):
        self.length, self.level = length, level
        self.peers = (upper, lower)
        self.pair = pair
        self.bufs = bufs
        self.sems = sems

    def copy(self, way, s):
        inward, outward = self.bufs[2 * way], self.bufs[2 * way + 1]
        send, recv = self.sems[2 * way], self.sems[2 * way + 1]
        return remote(
            outward.at[s - 1], inward.at[s - 1], send.at[s - 1], recv.at[s - 1], self.peers[way]
        )

    def rank(self, way):
        return self.level if way == 0 else self.length - 1 - self.level

    def start(self, s):
        for way in range(2):
            rank = self.rank(way)
            slot = rank + self.length - s
            slot = jnp.clip(slot if way == 0 else self.length - 1 - slot, 0, self.length - 1)
            inward, outward = self.bufs[2 * way], self.bufs[2 * way + 1]

            @pl.when(rank <= s - 1)
            def _(way=way, rank=rank, slot=slot, inward=inward, outward=outward):
                outward[s - 1] = self.pair[slot]
                if s > 1:
                    @pl.when(rank >= 1)
                    def _():
                        outward[s - 1] = (
                            self.pair[slot].astype(F32) + inward[s - 2].astype(F32)
                        ).astype(BF16)

                self.copy(way, s).start()

    def arrive(self, s):
        for way in range(2):
            rank = self.rank(way)

            @pl.when((rank >= 1) & (rank <= s))
            def _(way=way):
                self.copy(way, s).wait_recv()

    def result(self, target):
        last = self.length - 2
        target[...] = self.pair[self.level].astype(F32)
        for way in range(2):
            @pl.when(self.rank(way) >= 1)
            def _(way=way):
                target[...] += self.bufs[2 * way][last].astype(F32)

    def drain(self):
        for s in range(1, self.length):
            for way in range(2):
                rank = self.rank(way)

                @pl.when(rank <= s - 1)
                def _(way=way, s=s):
                    self.copy(way, s).wait_send()


def chain_scratch(length, shape):
    return [pltpu.VMEM((length - 1,) + shape, BF16)] * 4 + [
        pltpu.SemaphoreType.DMA((length - 1,))
    ] * 4


def chain_peers():
    count = lax.axis_size("dp")
    block = lax.axis_index("dp")
    lane = lax.axis_index("tensor")
    level = block // 2
    upper = (jnp.where(level < count // 2 - 1, block + 2, block + 2 - count), lane)
    lower = (jnp.where(level > 0, block - 2, block - 2 + count), lane)
    return count // 2, level, upper, lower


def query_back_kernel(
    chunks, dq_ref, wq_ref, n1_ref, dkv0, dkv1, dkv2, dkv3, dn_ref, grad_ref, tot_ref, part,
    from_core, summed, from_y, kv_core, kv_sum, kv_x, kv_pair, kv_z, kv_up, kv_y, kv_sems, own_ref,
    other_ref, got_ref, q_send, q_recv, *rest,
):
    chain_bufs, chain_sems, sems = rest[:4], rest[4:8], rest[8:]
    ts = TensorSum(chunks, part, dn_ref, from_core, summed, from_y, sems)
    block = lax.axis_index("dp")
    lane = lax.axis_index("tensor")
    place = lax.rem(block, SPAN)
    side = lax.rem(place, 2)
    level = place // 2
    levels = SPAN // 2
    x_peer = (block + 1 - 2 * side, lane)
    upper = (jnp.where(level < levels - 1, block + 2, block + 2 - SPAN), lane)
    lower = (jnp.where(level > 0, block - 2, block - 2 + SPAN), lane)
    length, chain_level, chain_upper, chain_lower = chain_peers()
    if length == levels:
        greet([ts.core_peer, ts.y_peer, x_peer, upper, lower])
    else:
        greet([ts.core_peer, ts.y_peer, x_peer, upper, lower, chain_upper, chain_lower])
    chain = Chain(length, chain_level, chain_upper, chain_lower, own_ref, chain_bufs, chain_sems)
    core = lax.rem(lane, 2)
    seq_rows = tot_ref.shape[0]
    half = seq_rows // 2
    mine = pl.ds(pl.multiple_of(core * half, half), half)
    other = pl.ds(pl.multiple_of((1 - core) * half, half), half)

    def kv_copy(source, target, index, device):
        return remote(source, target, kv_sems.at[0, index], kv_sems.at[1, index], device)

    dkv_refs = (dkv0, dkv1, dkv2, dkv3)
    to_core = [
        kv_copy(ref.at[:, other], kv_core.at[lev], 3 + levels + lev, ts.core_peer)
        for lev, ref in enumerate(dkv_refs)
    ]
    for copy in to_core:
        copy.start()
    grad_levels, rows = own_ref.shape[0], own_ref.shape[1]

    @pl.loop(0, chunks)
    def _(k):
        at = ts.span(k)
        part[at, :] = contract(dq_ref[at, :], wq_ref[...], 1, 1).astype(BF16)
        ts.first(k)

        @pl.when(k >= 1)
        def _():
            ts.second(k - 1)

    ts.second(chunks - 1)
    for lev, ref in enumerate(dkv_refs):
        to_core[lev].wait_recv()
        kv_sum[lev] = (ref[:, mine].astype(F32) + kv_core[lev].astype(F32)).astype(BF16)

    to_x = kv_copy(kv_sum.at[:, 1 - side], kv_x, 1, x_peer)
    to_x.start()

    def grad(target, which):
        grad_rows(n1_ref, dq_ref, target, which)

    grad(other_ref, 1 - side)
    q_to_x = remote(other_ref, got_ref, q_send, q_recv, x_peer)
    q_to_x.start()
    grad(own_ref, side)
    to_x.wait_recv()

    @pl.loop(0, levels)
    def _(lev):
        kv_pair[lev] = (kv_sum[lev, side].astype(F32) + kv_x[lev].astype(F32)).astype(BF16)

    def down(s):
        slot = jnp.maximum(level - levels + s, 0)
        return kv_copy(kv_up.at[s - 1], kv_z.at[s - 1], 1 + s, lower), slot

    for s in range(1, levels):
        copy, slot = down(s)

        @pl.when(level >= levels - s)
        def _(copy=copy, slot=slot, s=s):
            kv_up[s - 1] = kv_pair[slot]
            if s > 1:
                @pl.when(level < levels - 1)
                def _():
                    kv_up[s - 1] = (
                        kv_pair[slot].astype(F32) + kv_z[s - 2].astype(F32)
                    ).astype(BF16)

            copy.start()

        @pl.when((level >= levels - 1 - s) & (level < levels - 1))
        def _(copy=copy):
            copy.wait_recv()

    kv_up[levels - 1] = kv_pair[level]

    @pl.when(level < levels - 1)
    def _():
        kv_up[levels - 1] = (
            kv_pair[level].astype(F32) + kv_z[levels - 2].astype(F32)
        ).astype(BF16)

    to_y = kv_copy(kv_up.at[levels - 1], kv_y, 1 + levels, ts.y_peer)
    to_y.start()
    q_to_x.wait_recv()

    @pl.loop(0, grad_levels)
    def _(lev):
        own_ref[lev] = (own_ref[lev].astype(F32) + got_ref[lev].astype(F32)).astype(BF16)

    chain.start(1)
    to_y.wait_recv()
    tot_ref[mine] = (kv_up[levels - 1].astype(F32) + kv_y[...].astype(F32)).astype(BF16)
    back = kv_copy(tot_ref.at[mine], tot_ref.at[mine], 2 + levels, ts.core_peer)
    back.start()
    half_way = chunks // 2
    for s in range(1, length):
        if s == 2:
            @pl.loop(0, half_way)
            def _(k):
                ts.third(k)

        chain.arrive(s)
        if s + 1 < length:
            chain.start(s + 1)

    @pl.loop(half_way, chunks)
    def _(k):
        ts.third(k)

    chain.result(grad_ref)
    chain.drain()
    q_to_x.wait_send()
    back.wait()
    for copy in to_core:
        copy.wait_send()
    to_x.wait_send()
    to_y.wait_send()
    for s in range(1, levels):
        copy, _slot = down(s)

        @pl.when(level >= levels - s)
        def _(copy=copy):
            copy.wait_send()

    ts.finish(chunks)


def query_back(d_queries, query_weight, normed1, d_kv_parts, count, chunks=4):
    rows, width = d_queries.shape[0], query_weight.shape[0]
    kv_width = d_kv_parts[0].shape[1]
    levels = SPAN // 2
    parts = [part.reshape(2, rows, kv_width) for part in d_kv_parts]
    shape = (width // count, query_weight.shape[1])
    half = pltpu.VMEM((count // 2,) + shape, BF16)
    piece = (rows // 2, kv_width)
    return pl.pallas_call(
        functools.partial(query_back_kernel, chunks),
        out_shape=(
            jax.ShapeDtypeStruct((rows, width), BF16),
            jax.ShapeDtypeStruct(shape, F32),
            jax.ShapeDtypeStruct((rows, kv_width), BF16),
        ),
        in_specs=[VMEM] * (3 + levels),
        out_specs=(VMEM,) * 3,
        scratch_shapes=sum_scratch(chunks, rows, width)[:4]
        + [
            pltpu.VMEM((levels, 2) + piece, BF16),
            pltpu.VMEM((levels, 2) + piece, BF16),
            pltpu.VMEM((levels,) + piece, BF16),
            pltpu.VMEM((levels,) + piece, BF16),
            pltpu.VMEM((levels - 1,) + piece, BF16),
            pltpu.VMEM((levels,) + piece, BF16),
            pltpu.VMEM(piece, BF16),
            pltpu.SemaphoreType.DMA((2, 3 + 2 * levels)),
            half,
            half,
            half,
            pltpu.SemaphoreType.DMA,
            pltpu.SemaphoreType.DMA,
        ]
        + chain_scratch(count // 2, shape)
        + [pltpu.SemaphoreType.DMA((chunks,))] * 6,
        compiler_params=pltpu.CompilerParams(
            collective_id=5, has_side_effects=True, vmem_limit_bytes=58 << 20
        ),
        name="query_back",
    )(d_queries, query_weight, normed1, *parts)


def gather_kernel(own_ref, out_ref, local_sem, x_send, x_recv, z_send, z_recv, s_send, s_recv):
    block = lax.axis_index("dp")
    lane = lax.axis_index("tensor")
    place = lax.rem(block, SPAN)
    side = lax.rem(place, 2)
    level = place // 2
    levels = SPAN // 2
    core = lax.rem(lane, 2)
    core_lane = lane + 1 - 2 * core
    y_lane = lax.rem(lane + 2, 4)
    core_peer = (block, core_lane)
    y_peer = (block, y_lane)
    x_peer = (block + 1 - 2 * side, lane)
    upper = (jnp.where(level < levels - 1, block + 2, block + 2 - SPAN), lane)
    lower = (jnp.where(level > 0, block - 2, block - 2 + SPAN), lane)
    piece = own_ref.shape[0] // 4

    def rows(which):
        return pl.ds(pl.multiple_of(which * piece, piece), piece)

    greet([core_peer, y_peer, x_peer, upper, lower])
    keep = pltpu.make_async_copy(own_ref, out_ref.at[place], local_sem)
    keep.start()
    to_x = remote(own_ref.at[rows(lane)], out_ref.at[place, rows(lane)], x_send, x_recv, x_peer)
    to_x.start()
    keep.wait()
    to_x.wait_recv()

    def share(s, kind):
        blocks = pl.ds(place + 1 - 2 * side, 1) if s == 0 else pl.ds(2 * (level - s), 2)
        at = rows(y_lane if kind == 2 else lane)
        ref = out_ref.at[blocks, at]
        return remote(
            ref, ref, s_send.at[s, kind], s_recv.at[s, kind], y_peer if kind == 0 else core_peer
        )

    def up(s):
        ref = out_ref.at[pl.ds(2 * (level - s), 2), rows(lane)]
        return remote(ref, ref, z_send.at[s], z_recv.at[s], upper)

    def from_below(s):
        ref = out_ref.at[pl.ds(2 * (level - 1 - s), 2), rows(lane)]
        return remote(ref, ref, z_send.at[s], z_recv.at[s], upper)

    for s in range(levels):
        @pl.when(level >= s)
        def _(s=s):
            if s > 0:
                from_below(s - 1).wait_recv()
            if s < levels - 1:
                @pl.when(level < levels - 1)
                def _():
                    up(s).start()

            share(s, 0).start()
            share(s, 1).start()

    for s in range(levels):
        @pl.when(level >= s)
        def _(s=s):
            share(s, 0).wait_recv()
            share(s, 2).start()

    for s in range(levels):
        @pl.when(level >= s)
        def _(s=s):
            share(s, 0).wait_send()
            share(s, 1).wait()
            share(s, 2).wait()
            if s < levels - 1:
                @pl.when(level < levels - 1)
                def _():
                    up(s).wait_send()

    to_x.wait_send()


def gather_keyval(keyval):
    rows, width = keyval.shape
    levels = SPAN // 2
    dma = pltpu.SemaphoreType.DMA
    hbm = pl.BlockSpec(memory_space=pl.ANY)
    out = pl.pallas_call(
        gather_kernel,
        out_shape=jax.ShapeDtypeStruct((SPAN, rows, width), BF16),
        in_specs=[hbm],
        out_specs=hbm,
        scratch_shapes=[dma, dma, dma]
        + [dma((levels - 1,))] * 2
        + [dma((levels, 3))] * 2,
        compiler_params=pltpu.CompilerParams(collective_id=1, has_side_effects=True),
        name="gather_keyval",
    )(keyval)
    return out.reshape(SPAN * rows, width)


def last_sums_kernel(
    n1_ref, dkv_ref, own_vec, grad_ref, vec_ref, own_ref, other_ref, got_ref, x_send, x_recv, slots,
    send, recv, *chain_refs,
):
    block = lax.axis_index("dp")
    lane = lax.axis_index("tensor")
    count = lax.axis_size("dp")
    side = lax.rem(block, 2)
    others = [(lax.rem(block + k, count), lane) for k in range(1, count)]
    x_peer = (block + 1 - 2 * side, lane)
    greet(others)
    copies = []
    for k in range(1, count):
        copy = remote(own_vec, slots.at[k - 1], send.at[k - 1], recv.at[k - 1], others[k - 1])
        copy.start()
        copies.append(copy)
    levels, rows = own_ref.shape[0], own_ref.shape[1]

    def grad(target, which):
        grad_rows(n1_ref, dkv_ref, target, which)

    grad(other_ref, 1 - side)
    to_x = remote(other_ref, got_ref, x_send, x_recv, x_peer)
    to_x.start()
    grad(own_ref, side)
    length, level, upper, lower = chain_peers()
    chain = Chain(length, level, upper, lower, own_ref, chain_refs[:4], chain_refs[4:8])
    to_x.wait_recv()
    own_ref[...] = (own_ref[...].astype(F32) + got_ref[...].astype(F32)).astype(BF16)
    chain.start(1)
    for s in range(1, length):
        chain.arrive(s)
        if s + 1 < length:
            chain.start(s + 1)
    chain.result(grad_ref)
    total = own_vec[...]
    for k in range(1, count):
        copies[k - 1].wait()
        total = total + slots[k - 1]
    vec_ref[...] = total
    chain.drain()
    to_x.wait_send()


def last_sums(normed1, d_keyval, values, count):
    flat = jnp.concatenate(values)
    size = flat.shape[0]
    rows = -(-size // 1024) * 8
    packed = jnp.pad(flat, (0, rows * 128 - size)).reshape(rows, 128)
    shape = (normed1.shape[1] // count, d_keyval.shape[1])
    half = pltpu.VMEM((count // 2,) + shape, BF16)
    dma = pltpu.SemaphoreType.DMA
    grad, total = pl.pallas_call(
        last_sums_kernel,
        out_shape=(jax.ShapeDtypeStruct(shape, F32), jax.ShapeDtypeStruct((rows, 128), F32)),
        in_specs=[VMEM] * 3,
        out_specs=(VMEM, VMEM),
        scratch_shapes=[
            half,
            half,
            half,
            dma,
            dma,
            pltpu.VMEM((count - 1, rows, 128), F32),
            dma((count - 1,)),
            dma((count - 1,)),
        ]
        + chain_scratch(count // 2, shape),
        compiler_params=pltpu.CompilerParams(
            collective_id=2, has_side_effects=True, vmem_limit_bytes=32 << 20
        ),
        name="last_sums",
    )(normed1, d_keyval, packed)
    total = total.reshape(-1)
    pieces = []
    start = 0
    for value in values:
        pieces.append(total[start : start + value.shape[0]])
        start += value.shape[0]
    return grad, pieces


def layer_sum(part):
    lane = lax.axis_index("tensor")
    core = lax.rem(lane, 2)
    half = part.shape[1] // 2
    mine = lax.dynamic_slice_in_dim(part, core * half, half, 1)
    other = lax.dynamic_slice_in_dim(part, (1 - core) * half, half, 1)
    core_pairs = [(0, 1), (1, 0), (2, 3), (3, 2)]
    y_pairs = [(0, 2), (2, 0), (1, 3), (3, 1)]
    got = lax.ppermute(other, "tensor", core_pairs)
    summed = (mine.astype(F32) + got.astype(F32)).astype(BF16)
    return summed, lax.ppermute(summed, "tensor", y_pairs)


def layer_join(summed, got):
    core = lax.rem(lax.axis_index("tensor"), 2)
    total = (summed.astype(F32) + got.astype(F32)).astype(BF16)
    peer = lax.ppermute(total, "tensor", [(0, 1), (1, 0), (2, 3), (3, 2)])
    return jnp.concatenate(
        [jnp.where(core == 0, total, peer), jnp.where(core == 0, peer, total)], axis=1
    )


def together(*values):
    return lax.optimization_barrier(values)


class ScatterSum:
    def __init__(self, own, other, arrived=None):
        self.count = lax.axis_size("dp")
        self.length = self.count // 2
        self.level = lax.axis_index("dp") // 2
        self.own = own
        if arrived is not None:
            other = other[arrived.shape[0] :]
        got = lax.ppermute(other, "dp", [(p, p ^ 1) for p in range(self.count)])
        if arrived is not None:
            got = jnp.concatenate([arrived, got], axis=0)
        self.flying = (got,)
        self.s = 0

    def shifted(self, value, sources, step):
        pairs = [
            (2 * source + side, 2 * (source + step) + side)
            for source in sources
            for side in range(2)
        ]
        return lax.ppermute(value, "dp", pairs)

    def slot(self, index):
        index = jnp.clip(index, 0, self.length - 1)
        return lax.dynamic_index_in_dim(self.total, index, 0, keepdims=False)

    def step(self, *values):
        length, level = self.length, self.level
        self.s += 1
        s = self.s
        if s == 1:
            self.total = (self.own.astype(F32) + self.flying[0].astype(F32)).astype(BF16)
            up, down = self.slot(level + length - 1), self.slot(level - length + 1)
        else:
            up, down = self.flying
            up = self.slot(level + length - s).astype(F32) + up.astype(F32)
            if s == length:
                self.result = up + down.astype(F32)
                return values
            down = self.slot(level - length + s).astype(F32) + down.astype(F32)
            up, down = up.astype(BF16), down.astype(BF16)
        up, down, *values = together(up, down, *values)
        self.flying = (
            self.shifted(up, range(0, s), 1),
            self.shifted(down, range(length - s, length), -1),
        )
        return values

    def finish(self):
        while self.s < self.length:
            self.step()
        return self.result


def weight_grad_kernel(left_ref, right_ref, own_ref, other_ref):
    side = lax.rem(lax.axis_index("dp"), 2)
    grad_rows(left_ref, right_ref, other_ref, 1 - side)
    grad_rows(left_ref, right_ref, own_ref, side)


def weight_grad(left, right, count):
    half = jax.ShapeDtypeStruct((count // 2, left.shape[1] // count, right.shape[1]), BF16)
    return pl.pallas_call(
        weight_grad_kernel,
        out_shape=(half, half),
        in_specs=[VMEM] * 2,
        out_specs=(VMEM,) * 2,
        compiler_params=pltpu.CompilerParams(vmem_limit_bytes=40 << 20),
        cost_estimate=pl.CostEstimate(
            flops=2 * left.shape[0] * left.shape[1] * right.shape[1],
            bytes_accessed=16 << 20,
            transcendentals=0,
        ),
        name="weight_grad",
    )(left, right)


def attend_kernel(q_rows, k_rows, q_ref, kv_ref, ctx_ref, lse_ref, acc, peak, total):
    rows = q_ref.shape[0]
    head = kv_ref.shape[1] // 2
    heads = q_ref.shape[1] // head
    place = lax.rem(lax.axis_index("dp"), SPAN)
    for i in range(rows // q_rows):
        span = slice(i * q_rows, (i + 1) * q_rows)
        peak[...] = jnp.full_like(peak, NEG_LARGE)
        total[...] = jnp.zeros_like(total)
        acc[...] = jnp.zeros_like(acc)

        def step(j, diagonal):
            at = pl.ds(pl.multiple_of(j * k_rows, k_rows), k_rows)
            keys = kv_ref[at, 0:head]
            values = kv_ref[at, head : 2 * head]
            for h in range(heads):
                query = q_ref[span, h * head : (h + 1) * head]
                scores = contract(keys, query, 1, 1)
                if diagonal is not None:
                    key_at = lax.broadcasted_iota(jnp.int32, scores.shape, 0) + diagonal
                    query_at = lax.broadcasted_iota(jnp.int32, scores.shape, 1)
                    scores = jnp.where(key_at <= query_at, scores, NEG_LARGE)
                old = peak[h]
                new = jnp.maximum(old, jnp.max(scores, axis=0, keepdims=True))
                probs = jnp.exp(scores - new)
                fade = jnp.exp(old - new)
                total[h] = total[h] * fade + jnp.sum(probs, axis=0, keepdims=True)
                peak[h] = new
                acc[h] = acc[h] * fade + contract(values, probs.astype(BF16), 0, 0)

        full = (place * rows + i * q_rows) // k_rows

        @pl.loop(0, full)
        def _(j):
            step(j, None)

        for d in range(q_rows // k_rows):
            step(full + d, d * k_rows)
        for h in range(heads):
            context = acc[h] / total[h]
            ctx_ref[span, h * head : (h + 1) * head] = context.T.astype(BF16)
            lse_ref[h : h + 1, span] = peak[h] + jnp.log(total[h])


def attend(queries, keyval, q_rows=512, k_rows=512):
    rows, width = queries.shape
    head = keyval.shape[1] // 2
    heads = width // head
    stat = pltpu.VMEM((heads, 1, q_rows), F32)
    return pl.pallas_call(
        functools.partial(attend_kernel, q_rows, k_rows),
        out_shape=(
            jax.ShapeDtypeStruct((rows, width), BF16),
            jax.ShapeDtypeStruct((heads, rows), F32),
        ),
        in_specs=[VMEM, VMEM],
        out_specs=(VMEM, VMEM),
        scratch_shapes=[pltpu.VMEM((heads, head, q_rows), F32), stat, stat],
        compiler_params=pltpu.CompilerParams(vmem_limit_bytes=48 << 20),
        cost_estimate=pl.CostEstimate(
            flops=16 * rows * rows * width, bytes_accessed=8 << 20, transcendentals=0
        ),
        name="attend",
    )(queries, keyval)


def attend_back_kernel(
    target, q_rows, k_rows, first, last, q_ref, kv_ref, do_ref, lse_ref, *refs
):
    refs = list(refs)
    if first:
        ctx_ref = refs.pop(0)
    else:
        delta, dq_in = refs.pop(0), refs.pop(0)
    dkv_ref = refs.pop(0)
    if first:
        delta = refs.pop(0)
    if last:
        dq_ref = refs.pop(0)
    else:
        dq_out = refs.pop(0)
    dq_acc, dkv_acc = refs
    rows = q_ref.shape[0]
    head = kv_ref.shape[1] // 2
    heads = q_ref.shape[1] // head
    place = lax.rem(lax.axis_index("dp"), SPAN)
    dkv_acc[...] = jnp.zeros_like(dkv_acc)
    for i in range(rows // q_rows):
        span = slice(i * q_rows, (i + 1) * q_rows)
        if first:
            for h in range(heads):
                cols = slice(h * head, (h + 1) * head)
                product = do_ref[span, cols].astype(F32) * ctx_ref[span, cols].astype(F32)
                delta[h : h + 1, span] = jnp.sum(product.T, axis=0, keepdims=True)
            dq_acc[...] = jnp.zeros_like(dq_acc)
        else:
            dq_acc[...] = dq_in[i]

        def step(j, diagonal):
            at = pl.ds(pl.multiple_of(j * k_rows, k_rows), k_rows)
            keys = kv_ref[at, 0:head]
            values = kv_ref[at, head : 2 * head]
            d_keys = jnp.zeros((k_rows, head), F32)
            d_values = jnp.zeros((k_rows, head), F32)
            for h in range(heads):
                cols = slice(h * head, (h + 1) * head)
                query = q_ref[span, cols]
                d_ctx = do_ref[span, cols]
                scores = contract(keys, query, 1, 1)
                if diagonal:
                    key_at = lax.broadcasted_iota(jnp.int32, scores.shape, 0)
                    query_at = lax.broadcasted_iota(jnp.int32, scores.shape, 1)
                    scores = jnp.where(key_at <= query_at, scores, NEG_LARGE)
                probs = jnp.exp(scores - lse_ref[h : h + 1, span])
                d_probs = contract(values, d_ctx, 1, 1)
                d_scores = (probs * (d_probs - delta[h : h + 1, span])).astype(BF16)
                d_values += contract(probs.astype(BF16), d_ctx, 1, 0)
                d_keys += contract(d_scores, query, 1, 0)
                dq_acc[h] += contract(keys, d_scores, 0, 0)
            dkv_acc[at, 0:head] += d_keys
            dkv_acc[at, head : 2 * head] += d_values

        parts = kv_ref.shape[0] // k_rows
        full = (place * rows + i * q_rows) // k_rows - target * parts

        @pl.loop(0, jnp.clip(full, 0, parts))
        def _(j):
            step(j, False)

        @pl.when((full >= 0) & (full < parts))
        def _():
            step(full, True)

        if last:
            for h in range(heads):
                dq_ref[span, h * head : (h + 1) * head] = (
                    (dq_acc[h] * head**-0.5).T.astype(BF16)
                )
        else:
            dq_out[i] = dq_acc[...]
    dkv_ref[...] = dkv_acc[...].astype(BF16)


def attend_back(target, queries, keyval, d_context, lse, context, carried, block=512):
    rows, width = queries.shape
    head = keyval.shape[1] // 2
    heads = width // head
    first, last = target == 0, target == SPAN // 2 - 1
    span = 2 * rows
    kv_spec = pl.BlockSpec((span, 2 * head), lambda i: (target, 0))
    dq_shape = (rows // block, heads, head, block)
    whole = lambda shape: pl.BlockSpec(shape, lambda i: (0,) * len(shape))
    outs = [jax.ShapeDtypeStruct((span, 2 * head), BF16)]
    args = [queries, keyval, d_context, lse]
    if first:
        args.append(context)
        outs.append(jax.ShapeDtypeStruct((heads, rows), F32))
    else:
        args += carried
    if last:
        outs.append(jax.ShapeDtypeStruct((rows, width), BF16))
    else:
        outs.append(jax.ShapeDtypeStruct(dq_shape, F32))
    specs = [whole(a.shape) for a in args]
    specs[1] = kv_spec
    return pl.pallas_call(
        functools.partial(attend_back_kernel, target, block, block, first, last),
        grid=(1,),
        out_shape=tuple(outs),
        in_specs=specs,
        out_specs=tuple(whole(o.shape) for o in outs),
        scratch_shapes=[pltpu.VMEM(dq_shape[1:], F32), pltpu.VMEM((span, 2 * head), F32)],
        compiler_params=pltpu.CompilerParams(vmem_limit_bytes=48 << 20),
        cost_estimate=pl.CostEstimate(
            flops=20 * rows * rows * width, bytes_accessed=12 << 20, transcendentals=0
        ),
        name=f"attend_back{target}",
    )(*args)


def layer_norm(values, norm_gain, norm_bias):
    average = jnp.mean(values, axis=-1, keepdims=True)
    centred = values - average
    variance = jnp.mean(centred * centred, axis=-1, keepdims=True)
    return centred * lax.rsqrt(variance + EPSILON) * norm_gain + norm_bias


def gelu_tanh(values):
    return jax.nn.gelu(values, approximate=True)


def per_device(
    inputs,
    first_gain,
    first_bias,
    query_weight,
    query_bias,
    keyval_weight,
    value_bias,
    output_weight,
    output_bias,
    second_gain,
    second_bias,
    up_weight,
    up_bias,
    down_weight,
    down_bias,
    cotangent,
):
    count = lax.axis_size("dp")
    head_size = value_bias.shape[0]
    score_scale = head_size ** (-0.5)
    x_full = inputs.astype(F32)
    normed1_full, first_pull = jax.vjp(layer_norm, x_full, first_gain, first_bias)
    normed1 = normed1_full.astype(BF16)
    query_pre = jnp.dot(normed1, query_weight, preferred_element_type=F32) + query_bias
    queries = (query_pre * score_scale).astype(BF16)
    kv_bias = jnp.concatenate([jnp.zeros_like(value_bias), value_bias])
    keyval = (jnp.dot(normed1, keyval_weight, preferred_element_type=F32) + kv_bias).astype(BF16)
    keyval_all = gather_keyval(keyval)
    context_low, lse = attend(queries, keyval_all)
    attn_sum, d_activ = project(context_low, output_weight, cotangent, down_weight)
    middle = x_full + attn_sum.astype(F32) + output_bias
    normed2_full, second_pull = jax.vjp(layer_norm, middle, second_gain, second_bias)
    normed2 = normed2_full.astype(BF16)
    pre_act = jnp.dot(normed2, up_weight, preferred_element_type=F32) + up_bias
    act_full, gelu_pull = jax.vjp(gelu_tanh, pre_act)
    activ = act_full.astype(BF16)
    grad_full = cotangent.astype(F32)
    d_pre = gelu_pull(d_activ.astype(F32))[0].astype(BF16)
    own, other = weight_grad(cotangent, activ, count)
    d_normed2, up_own, up_other, arrived = hidden_back(d_pre, up_weight, normed2, other, count)
    scatter_down = ScatterSum(own, other, arrived)
    up_other, d_normed2 = together(up_other, d_normed2)
    scatter_up = ScatterSum(up_own, up_other)
    d_up_bias = jnp.sum(d_pre.astype(F32), axis=0)
    d_down_bias = jnp.sum(grad_full, axis=0)
    d_middle_norm, d_second_gain, d_second_bias = second_pull(d_normed2.astype(F32))
    d_middle = grad_full + d_middle_norm
    d_output_bias = jnp.sum(d_middle, axis=0)
    d_middle_low = d_middle.astype(BF16)
    d_context = contract(d_middle_low, output_weight, 1, 1).astype(BF16)
    mlp_part = jnp.dot(activ, down_weight, preferred_element_type=F32).astype(BF16)
    mlp_part, d_context = together(mlp_part, d_context)
    mlp_sum, mlp_y = layer_sum(mlp_part)
    grad_out_own, grad_out_other = weight_grad(d_middle_low, context_low, count)
    grad_out_other, d_context = together(grad_out_other, d_context)
    scatter_out = ScatterSum(grad_out_own, grad_out_other)

    d_kv_parts = []
    carried = None
    levels = SPAN // 2
    for target in range(levels):
        (d_context,) = scatter_down.step(d_context)
        if target >= 1:
            (d_context,) = scatter_out.step(d_context)
        results = attend_back(target, queries, keyval_all, d_context, lse, context_low, carried)
        if target == 0:
            d_kv, delta, dq = results
        else:
            d_kv, dq = results
        d_kv_parts.append(d_kv)
        carried = [delta, dq]
        dq, d_context = together(dq, d_context)
        carried = [delta, dq]
    d_queries = dq
    scatter_down.finish()
    scatter_out.finish()
    (d_queries,) = scatter_up.step(d_queries)
    d_query_bias = jnp.sum(d_queries.astype(F32), axis=0)
    d_normed1_sum, sent_query, d_keyval = query_back(
        d_queries, query_weight, normed1, d_kv_parts, count
    )
    (d_keyval,) = scatter_up.step(d_keyval)
    layer_out = (
        middle + layer_join(mlp_sum, mlp_y).astype(F32) + down_bias
    ).astype(BF16)
    d_value_bias = jnp.sum(d_keyval[:, head_size:].astype(F32), axis=0)
    d_normed1 = d_normed1_sum.astype(F32) + contract(d_keyval, keyval_weight, 1, 1)
    d_x_norm, d_first_gain, d_first_bias = first_pull(d_normed1)
    grad_inputs = d_middle + d_x_norm
    scatter_up.finish()
    sent_kv, sums = last_sums(
        normed1,
        d_keyval,
        [
            d_first_gain,
            d_first_bias,
            d_query_bias,
            d_value_bias,
            d_output_bias,
            d_second_gain,
            d_second_bias,
            d_up_bias,
            d_down_bias,
        ],
        count,
    )
    return (
        layer_out,
        grad_inputs,
        sums[0],
        sums[1],
        sent_query,
        sums[2],
        sent_kv,
        sums[3],
        scatter_out.result.T,
        sums[4],
        sums[5],
        sums[6],
        scatter_up.result,
        sums[7],
        scatter_down.result.T,
        sums[8],
    )


def solution(mesh):
    in_specs = (
        P("dp", None),
        P(),
        P(),
        P(None, "tensor"),
        P("tensor"),
        P(),
        P(),
        P("tensor", None),
        P(),
        P(),
        P(),
        P(None, "tensor"),
        P("tensor"),
        P("tensor", None),
        P(),
        P("dp", None),
    )
    out_specs = (
        P("dp", None),
        P("dp", None),
        P(),
        P(),
        P("dp", "tensor"),
        P("tensor"),
        P("dp", None),
        P(),
        P("tensor", "dp"),
        P(),
        P(),
        P(),
        P("dp", "tensor"),
        P("tensor"),
        P("tensor", "dp"),
        P(),
    )
    return jax.shard_map(
        per_device, mesh=mesh, in_specs=in_specs, out_specs=out_specs, check_vma=False
    )
```

time: 1010 us -> 816 us (0.81)
  the two profiles are of different devices: /device:TPU:14 before, /device:TPU:0 now
where the time goes in v2:
time: 816 us; the launch traced here: 807 us
  Pallas kernels  364 us (45%)
  starting transfers between devices  156 us (19%)
  waiting for transfers between devices  103 us (13%)
  other arithmetic  98.2 us (12%)
  matrix products  48.2 us (6%)
  local copies, waits for them, and re-layouts  35.8 us (4%)
    ppermute x18, starting transfers between devices, shifted(): return lax.ppermute(value, 'dp', pairs)  152 us
    pallas_call x1, Pallas kernels, query_back(): pl.pallas_call(functools.partial(query_back_kernel, chunks), out_shape=(j...  104 us
    pallas_call x1, Pallas kernels, hidden_back(): pl.pallas_call(functools.partial(hidden_back_kernel, chunks), out_shape=(...  90 us
    ppermute x3, waiting for transfers between devices, __init__(): got = lax.ppermute(other, 'dp', [(p, p ^ 1) for p in range(self.count)])  72.3 us
    pallas_call x1, Pallas kernels, project(): pl.pallas_call(functools.partial(project_kernel, chunks), out_shape=(jax....  60.5 us
    pallas_call x1, Pallas kernels, last_sums(): pl.pallas_call(last_sums_kernel, out_shape=(jax.ShapeDtypeStruct(shape, F...  33.8 us
    ppermute x18, waiting for transfers between devices, shifted(): return lax.ppermute(value, 'dp', pairs)  30.7 us
    pallas_call x1, Pallas kernels, gather_keyval(): pl.pallas_call(gather_kernel, out_shape=jax.ShapeDtypeStruct((SPAN, rows,...  28.7 us
  transfers between devices with their start and end apart: 24, of which 6 were waited for; matrix products, arithmetic and copies ran while one was open for 13% of the time, Pallas kernels for 20%

profile of v2, /device:TPU:0, one launch (start us, length us, event | category | flops | bytes accessed | tf_op | source)
XLA Modules:
  0.0 807.4 jit_solution(2670224213750924161)
XLA Ops:
  0.7 3.0 convert_reduce_fusion.1
  3.7 3.4 fusion.22
  13.1 28.7 %gather_keyval.1 = bf16[8,1024,256]{2,1,0:T(8,128)(2,1)} custom-call(bf16[1024,256]{1,0:T(8,128)(2,1)} %fusion.39.own_ref), custom_call_target="tpu_custom_call" | custom-call | tf_op jit(solution)/shard_map/gather_keyval/pallas_call | solution.py:589
  41.9 4.5 multiply_convert_fusion.1.q_ref
  46.4 9.4 %attend.1 = (bf16[1024,512]{1,0:T(8,128)(2,1)S(1)}, f32[4,1024]{1,0:T(4,128)S(1)}) custom-call(bf16[1024,512]{1,0:T(8,128)(2,1)S(1)} %multiply_convert_fusion.1.q_ref, bf16[8192,256]{1,0:T(8,128)(2,1)} %bitcast.106), custom_call_target="tpu_custom_call" | custom-call | flops 8589934592 | bytes 8388608 | tf_op jit(solution)/shard_map/attend/pallas_call | solution.py:837
  56.8 60.5 %project.1 = (bf16[1024,2048]{1,0:T(8,128)(2,1)}, bf16[1024,2048]{1,0:T(8,128)(2,1)}) custom-call(bf16[1024,512]{1,0:T(8,128)(2,1)} %copy-done.17, bf16[512,2048]{1,0:T(8,128)(2,1)} %wo_ref.1, bf16[1024,2048]{1,0:T(8,128)(2,1)} %left_ref.1, bf16[2048,2048]{1,0:T(8,128)(2,1)} %wd_ref.1), custom_call_target="tpu_custom_call" | custom-call | tf_op jit(solution)/shard_map/project/pallas_call | solution.py:165
  117.4 3.8 fusion.27
  123.7 2.9 add_convert_fusion.3.n2_ref
  126.7 19.1 %convert_reduce_fusion.3 = (f32[2048]{0:T(1024)S(1)}, bf16[1024,2048]{1,0:T(8,128)(2,1)}, bf16[1024,2048]{1,0:T(8,128)(2,1)}) fusion(f32[2048]{0:T(1024)S(1)} %copy-done.55, bf16[1024,2048]{1,0:T(8,128)(2,1)} %get-tuple-element.83, bf16[1024,2048]{1,0:T(8,128)(2,1)S(1)} %add_convert_fusion.3.n2_ref, bf16[2048,2048]{1,0:T(8,128)(2,1)S(1)} %bitcast.105), kind=kOutput, calls=%fused_computation.40 | convolution fusion | flops 8644458496 | bytes 25182208 | tf_op jit(solution)/shard_map/dot_general | solution.py:1013
  145.7 12.6 %weight_grad.2 = (bf16[4,256,2048]{2,1,0:T(8,128)(2,1)S(1)}, bf16[4,256,2048]{2,1,0:T(8,128)(2,1)S(1)}) custom-call(bf16[1024,2048]{1,0:T(8,128)(2,1)S(1)} %copy-done.3, bf16[1024,2048]{1,0:T(8,128)(2,1)} %get-tuple-element.174.right_ref), custom_call_target="tpu_custom_call" | custom-call | flops 8589934592 | bytes 16777216 | tf_op jit(solution)/shard_map/weight_grad/pallas_call | solution.py:773
  162.4 90.0 %hidden_back.1 = (bf16[1024,2048]{1,0:T(8,128)(2,1)}, bf16[4,256,2048]{2,1,0:T(8,128)(2,1)}, bf16[4,256,2048]{2,1,0:T(8,128)(2,1)}, bf16[3,256,2048]{2,1,0:T(8,128)(2,1)}) custom-call(bf16[1024,2048]{1,0:T(8,128)(2,1)} %get-tuple-element.171.dpre_ref, bf16[2048,2048]{1,0:T(8,128)(2,1)} %wu_ref.1, bf16[1024,2048]{1,0:T(8,128)(2,1)} %copy-done.36, ...), custom_call_target="tpu_custom_call" | custom-call | tf_op jit(solution)/shard_map/hidden_back/pallas_call | solution.py:224
  254.0 13.8 %convolution_convert_fusion = bf16[1024,2048]{1,0:T(8,128)(2,1)} fusion(bf16[1024,2048]{1,0:T(8,128)(2,1)} %get-tuple-element.174.right_ref, bf16[2048,2048]{1,0:T(8,128)(2,1)} %wd_ref.1), kind=kOutput, calls=%fused_computation.53 | convolution fusion | flops 8592031744 | bytes 16777216 | tf_op jit(solution)/shard_map/dot_general | solution.py:1030
  267.8 7.7 convert_reduce_fusion
  276.1 5.5 fusion.25
  281.6 6.7 fusion.52
  288.4 3.5 copy-done.31
  292.6 3.4 convolution_convert_fusion.1.do_ref
  297.9 3.1 constant_dynamic-slice_fusion
  303.2 4.4 weight_grad.3
  312.0 3.4 add_convert_fusion.5
  316.0 52.8 %collective-permute-done.4 = bf16[4,256,512]{2,1,0:T(8,128)(2,1)} collective-permute-done((bf16[4,256,512]{2,1,0:T(8,128)(2,1)}, bf16[4,256,512]{2,1,0:T(8,128)(2,1)}, u32[]{:S(2)}, u32[]{:S(2)}) %collective-permute-start.4) | collective-permute-done | bytes 1048608 | tf_op jit(solution)/shard_map/ppermute | solution.py:719
  370.3 19.4 %collective-permute-done.5 = bf16[1,256,2048]{2,1,0:T(8,128)(2,1)} collective-permute-done((bf16[1,256,2048]{2,1,0:T(8,128)(2,1)}, bf16[1,256,2048]{2,1,0:T(8,128)(2,1)}, u32[]{:S(2)}, u32[]{:S(2)}) %collective-permute-start.5) | collective-permute-done | bytes 1048608 | tf_op jit(solution)/shard_map/ppermute | solution.py:719
  392.6 6.9 add_convert_fusion.1
  401.0 31.4 %collective-permute-start.6 = (bf16[256,2048]{1,0:T(8,128)(2,1)S(1)}, bf16[256,2048]{1,0:T(8,128)(2,1)}, u32[]{:S(2)}, u32[]{:S(2)}) collective-permute-start(bf16[256,2048]{1,0:T(8,128)(2,1)S(1)} %get-tuple-element.98), channel_id=1, source_target_pairs={{0,8},{4,12},{1,9},{5,13},{2,10},{6,14},{3,11},{7,15}} | collective-permute-start | bytes 3145736 | tf_op jit(solution)/shard_map/ppermute | solution.py:731
  434.1 3.9 add_convert_fusion.4
  438.0 12.6 %attend_back0.1 = (bf16[2048,256]{1,0:T(8,128)(2,1)S(1)}, f32[4,1024]{1,0:T(4,128)S(1)}, f32[2,4,128,512]{3,2,1,0:T(8,128)}) custom-call(bf16[1024,512]{1,0:T(8,128)(2,1)S(1)} %copy-done.21, bf16[8192,256]{1,0:T(8,128)(2,1)} %bitcast.107, bf16[1024,512]{1,0:T(8,128)(2,1)S(1)} %copy-done.19, f32[4,1024]{1,0:T(4,128)S(1)} %get-tuple-element.101.lse_ref, ...), custom_call_target="tpu_custom_call" | custom-call | flops 10737418240 | bytes 12582912 | tf_op jit(solution)/shard_map/attend_back0/pallas_call | solution.py:953
  455.0 13.3 %collective-permute-start.8 = (bf16[256,512]{1,0:T(8,128)(2,1)S(1)}, bf16[256,512]{1,0:T(8,128)(2,1)S(1)}, u32[]{:S(2)}, u32[]{:S(2)}) collective-permute-start(bf16[256,512]{1,0:T(8,128)(2,1)S(1)} %get-tuple-element.105), channel_id=1, source_target_pairs={{0,8},{4,12},{1,9},{5,13},{2,10},{6,14},{3,11},{7,15}} | collective-permute-start | bytes 786440 | tf_op jit(solution)/shard_map/ppermute | solution.py:731
  476.7 20.2 %collective-permute-done.10 = bf16[256,2048]{1,0:T(8,128)(2,1)} collective-permute-done((bf16[256,2048]{1,0:T(8,128)(2,1)S(1)}, bf16[256,2048]{1,0:T(8,128)(2,1)}, u32[]{:S(2)}, u32[]{:S(2)}) %collective-permute-start.10) | collective-permute-done | bytes 1048608 | tf_op jit(solution)/shard_map/ppermute | solution.py:731
  496.9 3.6 fusion.35
  500.6 39.6 %collective-permute-start.12 = (bf16[256,512]{1,0:T(8,128)(2,1)S(1)}, bf16[256,512]{1,0:T(8,128)(2,1)S(1)}, u32[]{:S(2)}, u32[]{:S(2)}) collective-permute-start(bf16[256,512]{1,0:T(8,128)(2,1)S(1)} %get-tuple-element.115), channel_id=1, source_target_pairs={{0,8},{4,12},{8,16},{12,20},{1,9},{5,13},{9,17},{13,21},{2,10},{6,... | collective-permute-start | bytes 786440 | tf_op jit(solution)/shard_map/ppermute | solution.py:731
  540.9 2.8 attend_back2.1
  545.1 16.9 %collective-permute-start.22 = (bf16[256,2048]{1,0:T(8,128)(2,1)}, bf16[256,2048]{1,0:T(8,128)(2,1)}, u32[]{:S(2)}, u32[]{:S(2)}) collective-permute-start(bf16[256,2048]{1,0:T(8,128)(2,1)} %get-tuple-element.144), channel_id=1, source_target_pairs={{0,8},{4,12},{8,16},{12,20},{16,24},{20,28},{1,9},{5,13},{9,17},{1... | collective-permute-start | bytes 3145736 | tf_op jit(solution)/shard_map/ppermute | solution.py:731
  563.4 12.6 %collective-permute-start.16 = (bf16[256,512]{1,0:T(8,128)(2,1)S(1)}, bf16[256,512]{1,0:T(8,128)(2,1)S(1)}, u32[]{:S(2)}, u32[]{:S(2)}) collective-permute-start(bf16[256,512]{1,0:T(8,128)(2,1)S(1)} %get-tuple-element.138), channel_id=1, source_target_pairs={{0,8},{4,12},{8,16},{12,20},{16,24},{20,28},{1,9},{5,13},{9,17},{1... | collective-permute-start | bytes 786440 | tf_op jit(solution)/shard_map/ppermute | solution.py:731
  576.0 2.8 attend_back3.1
  582.2 17.0 %collective-permute-start.14 = (bf16[256,2048]{1,0:T(8,128)(2,1)}, bf16[256,2048]{1,0:T(8,128)(2,1)}, u32[]{:S(2)}, u32[]{:S(2)}) collective-permute-start(bf16[256,2048]{1,0:T(8,128)(2,1)} %get-tuple-element.131), channel_id=1, source_target_pairs={{0,8},{4,12},{1,9},{5,13},{2,10},{6,14},{3,11},{7,15}} | collective-permute-start | bytes 3145736 | tf_op jit(solution)/shard_map/ppermute | solution.py:731
  600.9 4.5 broadcast_select_fusion.1
  605.4 103.9 %query_back.1 = (bf16[1024,2048]{1,0:T(8,128)(2,1)}, f32[256,512]{1,0:T(8,128)}, bf16[1024,256]{1,0:T(8,128)(2,1)}) custom-call(bf16[1024,512]{1,0:T(8,128)(2,1)} %copy-done.10, bf16[2048,512]{1,0:T(8,128)(2,1)} %wq_ref.1, bf16[1024,2048]{1,0:T(8,128)(2,1)} %copy-done.1, bf16[2,1024,256]{2,1,0:T(8,128)(2,1)} %bitcast.98, bf16[2,1024,256]{2,1,0:T(8,128)(2,1)} %bitcast.99, ...), custom_call_target="tpu_custom_call" | custom-call | tf_op jit(solution)/shard_map/query_back/pallas_call | solution.py:473
  710.7 3.8 fusion.29
  714.4 2.9 copy.33
  717.3 3.9 fusion.33
  721.4 4.6 collective-permute-start.18
  727.7 5.4 fusion.50
  733.2 4.0 fusion.10
  738.3 33.8 %last_sums.1 = (f32[256,256]{1,0:T(8,128)S(1)}, f32[120,128]{1,0:T(8,128)S(1)}) custom-call(bf16[1024,2048]{1,0:T(8,128)(2,1)S(1)} %copy-done.2, bf16[1024,256]{1,0:T(8,128)(2,1)S(1)} %copy-done.12, f32[120,128]{1,0:T(8,128)S(1)} %pad_bitcast_fusion.own_vec), custom_call_target="tpu_custom_call" | custom-call | tf_op jit(solution)/shard_map/last_sums/pallas_call | solution.py:655
  780.1 13.2 %add_add_fusion.2 = (f32[1024,2048]{1,0:T(8,128)}, bf16[1024,2048]{1,0:T(8,128)(2,1)}) fusion(f32[1024,2048]{1,0:T(8,128)S(1)} %bitcast.103, f32[1024]{0:T(1024)S(1)} %negate_multiply_fusion, f32[1024]{0:T(1024)S(1)} %multiply_multiply_fusion.2, f32[1024]{0:T(1024)S(1)} %copy-done.44, bf16[1024,2048]{1,0:T(8,128)(2,1)S(1)} %copy-done.27, ...), kind=kLoop, calls=%fused_computation.41 | loop fusion | flops 39845888 | bytes 41984000 | tf_op jit(solution)/shard_map/add | solution.py:1068
  793.3 5.2 collective-permute-done.20
  798.5 4.2 collective-permute-done.21
  802.6 3.1 fusion.32
  (201 shorter events, 67.9 us)
Async XLA Ops:
  7.1 34.8 %copy-start.47 = (f32[1024]{0:T(1024)}, f32[1024]{0:T(1024)S(1)}, u32[]{:S(2)}) copy-start(f32[1024]{0:T(1024)S(1)} %fusion.46) | copy-start | bytes 12292
  11.1 30.8 %copy-start.39 = (bf16[2048,512]{1,0:T(8,128)(2,1)S(1)}, bf16[2048,512]{1,0:T(8,128)(2,1)}, u32[]{:S(2)}) copy-start(bf16[2048,512]{1,0:T(8,128)(2,1)} %wq_ref.1) | copy-start | bytes 6291460
  11.1 30.8 %copy-start.56 = (f32[512]{0:T(512)S(1)}, f32[512]{0:T(512)}, u32[]{:S(2)}) copy-start(f32[512]{0:T(512)} %param.20) | copy-start | bytes 6148
  56.8 60.5 %copy-start.25 = (bf16[1024,2048]{1,0:T(8,128)(2,1)S(1)}, bf16[1024,2048]{1,0:T(8,128)(2,1)}, u32[]{:S(2)}) copy-start(bf16[1024,2048]{1,0:T(8,128)(2,1)} %param.16) | copy-start | bytes 12582916
  56.8 60.5 %copy-start.41 = (f32[2048]{0:T(1024)S(1)}, f32[2048]{0:T(1024)}, u32[]{:S(2)}) copy-start(f32[2048]{0:T(1024)} %param.24) | copy-start | bytes 24580
  126.6 19.1 %copy-start.36 = (bf16[1024,2048]{1,0:T(8,128)(2,1)}, bf16[1024,2048]{1,0:T(8,128)(2,1)S(1)}, u32[]{:S(2)}) copy-start(bf16[1024,2048]{1,0:T(8,128)(2,1)S(1)} %add_convert_fusion.3.n2_ref) | copy-start | bytes 12582916
  126.7 19.1 %copy-start.3 = (bf16[1024,2048]{1,0:T(8,128)(2,1)S(1)}, bf16[1024,2048]{1,0:T(8,128)(2,1)}, u32[]{:S(2)}) copy-start(bf16[1024,2048]{1,0:T(8,128)(2,1)} %left_ref.1) | copy-start | bytes 12582916
  252.4 140.2 %collective-permute-start.3 = (bf16[4,256,2048]{2,1,0:T(8,128)(2,1)}, bf16[4,256,2048]{2,1,0:T(8,128)(2,1)}, u32[]{:S(2)}, u32[]{:S(2)}) collective-permute-start(bf16[4,256,2048]{2,1,0:T(8,128)(2,1)} %get-tuple-element.90), channel_id=1, source_target_pairs={{0,4},{4,0},{8,12},{12,8},{16,20},{20,16},{24,28},{28,24},{1,5},{5... | collective-permute-start | bytes 12582920 | tf_op jit(solution)/shard_map/ppermute | solution.py:719
  301.0 11.0 %collective-permute-start = (bf16[1024,1024]{1,0:T(8,128)(2,1)}, bf16[1024,1024]{1,0:T(8,128)(2,1)}, u32[]{:S(2)}, u32[]{:S(2)}) collective-permute-start(bf16[1024,1024]{1,0:T(8,128)(2,1)} %constant_dynamic-slice_fusion), channel_id=1, source_target_pairs={{0,1},{1,0},{2,3},{3,2},{4,5},{5,4},{6,7},{7,6},{8,9},{9,8},{10,11... | collective-permute-start | bytes 6291464 | tf_op jit(solution)/shard_map/ppermute | solution.py:693
  307.6 61.1 %collective-permute-start.4 = (bf16[4,256,512]{2,1,0:T(8,128)(2,1)}, bf16[4,256,512]{2,1,0:T(8,128)(2,1)}, u32[]{:S(2)}, u32[]{:S(2)}) collective-permute-start(bf16[4,256,512]{2,1,0:T(8,128)(2,1)} %get-tuple-element.94), channel_id=1, source_target_pairs={{0,4},{4,0},{8,12},{12,8},{16,20},{20,16},{24,28},{28,24},{1,5},{5... | collective-permute-start | bytes 3145736 | tf_op jit(solution)/shard_map/ppermute | solution.py:719
  310.5 79.3 %collective-permute-start.5 = (bf16[1,256,2048]{2,1,0:T(8,128)(2,1)}, bf16[1,256,2048]{2,1,0:T(8,128)(2,1)}, u32[]{:S(2)}, u32[]{:S(2)}) collective-permute-start(bf16[1,256,2048]{2,1,0:T(8,128)(2,1)} %slice.60), channel_id=1, source_target_pairs={{0,4},{4,0},{8,12},{12,8},{16,20},{20,16},{24,28},{28,24},{1,5},{5... | collective-permute-start | bytes 3145736 | tf_op jit(solution)/shard_map/ppermute | solution.py:719
  312.0 77.8 %copy-start.7 = (bf16[4,256,2048]{2,1,0:T(8,128)(2,1)S(1)}, bf16[4,256,2048]{2,1,0:T(8,128)(2,1)}, u32[]{:S(2)}) copy-start(bf16[4,256,2048]{2,1,0:T(8,128)(2,1)} %copy-done.6) | copy-start | bytes 12582916
  312.0 77.8 %copy-start.37 = (bf16[3,256,2048]{2,1,0:T(8,128)(2,1)S(1)}, bf16[3,256,2048]{2,1,0:T(8,128)(2,1)}, u32[]{:S(2)}) copy-start(bf16[3,256,2048]{2,1,0:T(8,128)(2,1)} %get-tuple-element.96) | copy-start | bytes 9437188
  315.4 118.7 %collective-permute-start.1 = (bf16[1024,1024]{1,0:T(8,128)(2,1)S(1)}, bf16[1024,1024]{1,0:T(8,128)(2,1)}, u32[]{:S(2)}, u32[]{:S(2)}) collective-permute-start(bf16[1024,1024]{1,0:T(8,128)(2,1)S(1)} %add_convert_fusion.5), channel_id=1, source_target_pairs={{0,2},{2,0},{1,3},{3,1},{4,6},{6,4},{5,7},{7,5},{8,10},{10,8},{9,1... | collective-permute-start | bytes 6291464 | tf_op jit(solution)/shard_map/ppermute | solution.py:695
  392.6 104.4 %copy-start.35 = (bf16[4,256,2048]{2,1,0:T(8,128)(2,1)}, bf16[4,256,2048]{2,1,0:T(8,128)(2,1)S(1)}, u32[]{:S(2)}) copy-start(bf16[4,256,2048]{2,1,0:T(8,128)(2,1)S(1)} %add_convert_fusion) | copy-start | bytes 12582916
  399.5 38.5 %copy-start.34 = (bf16[4,256,2048]{2,1,0:T(8,128)(2,1)}, bf16[4,256,2048]{2,1,0:T(8,128)(2,1)S(1)}, u32[]{:S(2)}) copy-start(bf16[4,256,2048]{2,1,0:T(8,128)(2,1)S(1)} %add_convert_fusion.1) | copy-start | bytes 12582916
  399.5 38.5 %copy-start.19 = (bf16[1024,512]{1,0:T(8,128)(2,1)S(1)}, bf16[1024,512]{1,0:T(8,128)(2,1)}, u32[]{:S(2)}) copy-start(bf16[1024,512]{1,0:T(8,128)(2,1)} %convolution_convert_fusion.1.do_ref) | copy-start | bytes 3145732
  399.5 38.5 %copy-start.21 = (bf16[1024,512]{1,0:T(8,128)(2,1)S(1)}, bf16[1024,512]{1,0:T(8,128)(2,1)}, u32[]{:S(2)}) copy-start(bf16[1024,512]{1,0:T(8,128)(2,1)} %copy-done.20) | copy-start | bytes 3145732
  401.0 51.6 %collective-permute-start.6 = (bf16[256,2048]{1,0:T(8,128)(2,1)S(1)}, bf16[256,2048]{1,0:T(8,128)(2,1)}, u32[]{:S(2)}, u32[]{:S(2)}) collective-permute-start(bf16[256,2048]{1,0:T(8,128)(2,1)S(1)} %get-tuple-element.98), channel_id=1, source_target_pairs={{0,8},{4,12},{1,9},{5,13},{2,10},{6,14},{3,11},{7,15}} | collective-permute-start | bytes 3145736 | tf_op jit(solution)/shard_map/ppermute | solution.py:731
  432.4 20.2 %collective-permute-start.7 = (bf16[256,2048]{1,0:T(8,128)(2,1)S(1)}, bf16[256,2048]{1,0:T(8,128)(2,1)}, u32[]{:S(2)}, u32[]{:S(2)}) collective-permute-start(bf16[256,2048]{1,0:T(8,128)(2,1)S(1)} %get-tuple-element.99), channel_id=1, source_target_pairs={{24,16},{28,20},{25,17},{29,21},{26,18},{30,22},{27,19},{31,23}} | collective-permute-start | bytes 3145736 | tf_op jit(solution)/shard_map/ppermute | solution.py:731
  438.0 144.2 %collective-permute-start.2 = (bf16[1024,1024]{1,0:T(8,128)(2,1)}, bf16[1024,1024]{1,0:T(8,128)(2,1)}, u32[]{:S(2)}, u32[]{:S(2)}) collective-permute-start(bf16[1024,1024]{1,0:T(8,128)(2,1)} %add_convert_fusion.4), channel_id=1, source_target_pairs={{0,1},{1,0},{2,3},{3,2},{4,5},{5,4},{6,7},{7,6},{8,9},{9,8},{10,11... | collective-permute-start | bytes 6291464 | tf_op jit(solution)/shard_map/ppermute | solution.py:701
  455.0 21.6 %collective-permute-start.8 = (bf16[256,512]{1,0:T(8,128)(2,1)S(1)}, bf16[256,512]{1,0:T(8,128)(2,1)S(1)}, u32[]{:S(2)}, u32[]{:S(2)}) collective-permute-start(bf16[256,512]{1,0:T(8,128)(2,1)S(1)} %get-tuple-element.105), channel_id=1, source_target_pairs={{0,8},{4,12},{1,9},{5,13},{2,10},{6,14},{3,11},{7,15}} | collective-permute-start | bytes 786440 | tf_op jit(solution)/shard_map/ppermute | solution.py:731
  468.3 8.3 %collective-permute-start.9 = (bf16[256,512]{1,0:T(8,128)(2,1)S(1)}, bf16[256,512]{1,0:T(8,128)(2,1)S(1)}, u32[]{:S(2)}, u32[]{:S(2)}) collective-permute-start(bf16[256,512]{1,0:T(8,128)(2,1)S(1)} %get-tuple-element.106), channel_id=1, source_target_pairs={{24,16},{28,20},{25,17},{29,21},{26,18},{30,22},{27,19},{31,23}} | collective-permute-start | bytes 786440 | tf_op jit(solution)/shard_map/ppermute | solution.py:731
  469.0 28.0 %collective-permute-start.10 = (bf16[256,2048]{1,0:T(8,128)(2,1)S(1)}, bf16[256,2048]{1,0:T(8,128)(2,1)}, u32[]{:S(2)}, u32[]{:S(2)}) collective-permute-start(bf16[256,2048]{1,0:T(8,128)(2,1)S(1)} %get-tuple-element.107), channel_id=1, source_target_pairs={{0,8},{4,12},{8,16},{12,20},{1,9},{5,13},{9,17},{13,21},{2,10},{6,... | collective-permute-start | bytes 3145736 | tf_op jit(solution)/shard_map/ppermute | solution.py:731
  471.3 25.7 %collective-permute-start.11 = (bf16[256,2048]{1,0:T(8,128)(2,1)S(1)}, bf16[256,2048]{1,0:T(8,128)(2,1)}, u32[]{:S(2)}, u32[]{:S(2)}) collective-permute-start(bf16[256,2048]{1,0:T(8,128)(2,1)S(1)} %get-tuple-element.108), channel_id=1, source_target_pairs={{16,8},{20,12},{24,16},{28,20},{17,9},{21,13},{25,17},{29,21},{18,... | collective-permute-start | bytes 3145736 | tf_op jit(solution)/shard_map/ppermute | solution.py:731
  476.6 63.6 %copy-start.22 = (f32[2,4,128,512]{3,2,1,0:T(8,128)}, f32[2,4,128,512]{3,2,1,0:T(8,128)S(1)}, u32[]{:S(2)}) copy-start(f32[2,4,128,512]{3,2,1,0:T(8,128)S(1)} %get-tuple-element.118.refs_1_) | copy-start | bytes 6291460
  500.6 62.6 %collective-permute-start.12 = (bf16[256,512]{1,0:T(8,128)(2,1)S(1)}, bf16[256,512]{1,0:T(8,128)(2,1)S(1)}, u32[]{:S(2)}, u32[]{:S(2)}) collective-permute-start(bf16[256,512]{1,0:T(8,128)(2,1)S(1)} %get-tuple-element.115), channel_id=1, source_target_pairs={{0,8},{4,12},{8,16},{12,20},{1,9},{5,13},{9,17},{13,21},{2,10},{6,... | collective-permute-start | bytes 786440 | tf_op jit(solution)/shard_map/ppermute | solution.py:731
  540.2 23.0 %collective-permute-start.13 = (bf16[256,512]{1,0:T(8,128)(2,1)S(1)}, bf16[256,512]{1,0:T(8,128)(2,1)S(1)}, u32[]{:S(2)}, u32[]{:S(2)}) collective-permute-start(bf16[256,512]{1,0:T(8,128)(2,1)S(1)} %get-tuple-element.116), channel_id=1, source_target_pairs={{16,8},{20,12},{24,16},{28,20},{17,9},{21,13},{25,17},{29,21},{18,... | collective-permute-start | bytes 786440 | tf_op jit(solution)/shard_map/ppermute | solution.py:731
  545.1 18.3 %copy-start.15 = (bf16[2048,256]{1,0:T(8,128)(2,1)}, bf16[2048,256]{1,0:T(8,128)(2,1)S(1)}, u32[]{:S(2)}) copy-start(bf16[2048,256]{1,0:T(8,128)(2,1)S(1)} %get-tuple-element.128) | copy-start | bytes 3145732
  545.1 165.6 %collective-permute-start.22 = (bf16[256,2048]{1,0:T(8,128)(2,1)}, bf16[256,2048]{1,0:T(8,128)(2,1)}, u32[]{:S(2)}, u32[]{:S(2)}) collective-permute-start(bf16[256,2048]{1,0:T(8,128)(2,1)} %get-tuple-element.144), channel_id=1, source_target_pairs={{0,8},{4,12},{8,16},{12,20},{16,24},{20,28},{1,9},{5,13},{9,17},{1... | collective-permute-start | bytes 3145736 | tf_op jit(solution)/shard_map/ppermute | solution.py:731
  561.9 148.8 %collective-permute-start.23 = (bf16[256,2048]{1,0:T(8,128)(2,1)}, bf16[256,2048]{1,0:T(8,128)(2,1)}, u32[]{:S(2)}, u32[]{:S(2)}) collective-permute-start(bf16[256,2048]{1,0:T(8,128)(2,1)} %get-tuple-element.145), channel_id=1, source_target_pairs={{8,0},{12,4},{16,8},{20,12},{24,16},{28,20},{9,1},{13,5},{17,9},{2... | collective-permute-start | bytes 3145736 | tf_op jit(solution)/shard_map/ppermute | solution.py:731
  563.4 35.8 %collective-permute-start.16 = (bf16[256,512]{1,0:T(8,128)(2,1)S(1)}, bf16[256,512]{1,0:T(8,128)(2,1)S(1)}, u32[]{:S(2)}, u32[]{:S(2)}) collective-permute-start(bf16[256,512]{1,0:T(8,128)(2,1)S(1)} %get-tuple-element.138), channel_id=1, source_target_pairs={{0,8},{4,12},{8,16},{12,20},{16,24},{20,28},{1,9},{5,13},{9,17},{1... | collective-permute-start | bytes 786440 | tf_op jit(solution)/shard_map/ppermute | solution.py:731
  580.8 128.6 %copy-start.11 = (bf16[1024,512]{1,0:T(8,128)(2,1)S(1)}, bf16[1024,512]{1,0:T(8,128)(2,1)}, u32[]{:S(2)}) copy-start(bf16[1024,512]{1,0:T(8,128)(2,1)} %copy-done.10) | copy-start | bytes 3145732
  580.8 128.8 %collective-permute-start.17 = (bf16[256,512]{1,0:T(8,128)(2,1)S(1)}, bf16[256,512]{1,0:T(8,128)(2,1)S(1)}, u32[]{:S(2)}, u32[]{:S(2)}) collective-permute-start(bf16[256,512]{1,0:T(8,128)(2,1)S(1)} %get-tuple-element.139), channel_id=1, source_target_pairs={{8,0},{12,4},{16,8},{20,12},{24,16},{28,20},{9,1},{13,5},{17,9},{2... | collective-permute-start | bytes 786440 | tf_op jit(solution)/shard_map/ppermute | solution.py:731
  582.2 135.1 %collective-permute-start.14 = (bf16[256,2048]{1,0:T(8,128)(2,1)}, bf16[256,2048]{1,0:T(8,128)(2,1)}, u32[]{:S(2)}, u32[]{:S(2)}) collective-permute-start(bf16[256,2048]{1,0:T(8,128)(2,1)} %get-tuple-element.131), channel_id=1, source_target_pairs={{0,8},{4,12},{1,9},{5,13},{2,10},{6,14},{3,11},{7,15}} | collective-permute-start | bytes 3145736 | tf_op jit(solution)/shard_map/ppermute | solution.py:731
  599.2 118.1 %collective-permute-start.15 = (bf16[256,2048]{1,0:T(8,128)(2,1)S(1)}, bf16[256,2048]{1,0:T(8,128)(2,1)}, u32[]{:S(2)}, u32[]{:S(2)}) collective-permute-start(bf16[256,2048]{1,0:T(8,128)(2,1)S(1)} %get-tuple-element.132), channel_id=1, source_target_pairs={{24,16},{28,20},{25,17},{29,21},{26,18},{30,22},{27,19},{31,23}} | collective-permute-start | bytes 3145736 | tf_op jit(solution)/shard_map/ppermute | solution.py:731
  709.6 11.6 %copy-start.12 = (bf16[1024,256]{1,0:T(8,128)(2,1)S(1)}, bf16[1024,256]{1,0:T(8,128)(2,1)}, u32[]{:S(2)}) copy-start(bf16[1024,256]{1,0:T(8,128)(2,1)} %get-tuple-element.134.dkv_ref) | copy-start | bytes 1572868
  709.7 18.0 %copy-start.44 = (f32[1024]{0:T(1024)S(1)}, f32[1024]{0:T(1024)}, u32[]{:S(2)}) copy-start(f32[1024]{0:T(1024)} %copy-done.43) | copy-start | bytes 12292
  709.7 18.0 %copy-start.46 = (f32[2048]{0:T(1024)S(1)}, f32[2048]{0:T(1024)}, u32[]{:S(2)}) copy-start(f32[2048]{0:T(1024)} %param.17) | copy-start | bytes 24580
  721.4 52.4 %collective-permute-start.18 = (bf16[256,2048]{1,0:T(8,128)(2,1)}, bf16[256,2048]{1,0:T(8,128)(2,1)S(1)}, u32[]{:S(2)}, u32[]{:S(2)}) collective-permute-start(bf16[256,2048]{1,0:T(8,128)(2,1)} %get-tuple-element.140), channel_id=1, source_target_pairs={{0,8},{4,12},{8,16},{12,20},{1,9},{5,13},{9,17},{13,21},{2,10},{6,... | collective-permute-start | bytes 3145736 | tf_op jit(solution)/shard_map/ppermute | solution.py:731
  726.0 47.8 %collective-permute-start.19 = (bf16[256,2048]{1,0:T(8,128)(2,1)S(1)}, bf16[256,2048]{1,0:T(8,128)(2,1)}, u32[]{:S(2)}, u32[]{:S(2)}) collective-permute-start(bf16[256,2048]{1,0:T(8,128)(2,1)S(1)} %get-tuple-element.141), channel_id=1, source_target_pairs={{16,8},{20,12},{24,16},{28,20},{17,9},{21,13},{25,17},{29,21},{18,... | collective-permute-start | bytes 3145736 | tf_op jit(solution)/shard_map/ppermute | solution.py:731
  733.2 46.9 %slice-start = ((s8[8388608]{0:T(1024)(128)(4,1)}), s8[4194304]{0:T(1024)(128)(4,1)S(1)}, s32[]{:S(2)}) async-start(s8[8388608]{0:T(1024)(128)(4,1)} %bitcast.102), calls=%async_computation | async-start | bytes 8388608
  733.2 46.8 %slice-start.1 = ((s8[8388608]{0:T(1024)(128)(4,1)}), s8[4194304]{0:T(1024)(128)(4,1)S(1)}, s32[]{:S(2)}) async-start(s8[8388608]{0:T(1024)(128)(4,1)} %bitcast.102), calls=%async_computation.1 | async-start | bytes 8388608
  737.2 42.8 %copy-start.30 = (bf16[1024,2048]{1,0:T(8,128)(2,1)S(1)}, bf16[1024,2048]{1,0:T(8,128)(2,1)}, u32[]{:S(2)}) copy-start(bf16[1024,2048]{1,0:T(8,128)(2,1)} %get-tuple-element.82) | copy-start | bytes 12582916
  737.2 42.8 %copy-start.53 = (f32[2048]{0:T(1024)S(1)}, f32[2048]{0:T(1024)}, u32[]{:S(2)}) copy-start(f32[2048]{0:T(1024)} %param.30) | copy-start | bytes 24580
  776.5 22.0 %collective-permute-start.20 = (bf16[256,2048]{1,0:T(8,128)(2,1)S(1)}, bf16[256,2048]{1,0:T(8,128)(2,1)S(1)}, u32[]{:S(2)}, u32[]{:S(2)}) collective-permute-start(bf16[256,2048]{1,0:T(8,128)(2,1)S(1)} %get-tuple-element.142), channel_id=1, source_target_pairs={{0,8},{4,12},{8,16},{12,20},{16,24},{20,28},{1,9},{5,13},{9,17},{1... | collective-permute-start | bytes 3145736 | tf_op jit(solution)/shard_map/ppermute | solution.py:731
  778.7 23.9 %collective-permute-start.21 = (bf16[256,2048]{1,0:T(8,128)(2,1)S(1)}, bf16[256,2048]{1,0:T(8,128)(2,1)S(1)}, u32[]{:S(2)}, u32[]{:S(2)}) collective-permute-start(bf16[256,2048]{1,0:T(8,128)(2,1)S(1)} %get-tuple-element.143), channel_id=1, source_target_pairs={{8,0},{12,4},{16,8},{20,12},{24,16},{28,20},{9,1},{13,5},{17,9},{2... | collective-permute-start | bytes 3145736 | tf_op jit(solution)/shard_map/ppermute | solution.py:731
  780.1 25.6 %copy-start.40 = (f32[256,512]{1,0:T(8,128)S(1)}, f32[256,512]{1,0:T(8,128)}, u32[]{:S(2)}) copy-start(f32[256,512]{1,0:T(8,128)} %get-tuple-element.228) | copy-start | bytes 1572868
  (37 other events, 173.6 us)

commit v3 on v2

v3 whole, which is shorter than its diff:
```python
import functools

import jax
import jax.numpy as jnp
from jax import lax
from jax.experimental import pallas as pl
from jax.experimental.pallas import tpu as pltpu
from jax.sharding import PartitionSpec as P

SPAN = 8
EPSILON = 1e-05
NEG_LARGE = -1e30
MESH = pl.DeviceIdType.MESH
VMEM = pl.BlockSpec(memory_space=pltpu.VMEM)
F32 = jnp.float32
BF16 = jnp.bfloat16


def contract(left, right, left_dim, right_dim):
    return lax.dot_general(
        left, right, (((left_dim,), (right_dim,)), ((), ())), preferred_element_type=F32
    )


def remote(source, target, send_sem, recv_sem, device):
    return pltpu.make_async_remote_copy(
        src_ref=source,
        dst_ref=target,
        send_sem=send_sem,
        recv_sem=recv_sem,
        device_id=device,
        device_id_type=MESH,
    )


def greet(devices):
    barrier = pltpu.get_barrier_semaphore()
    for device in devices:
        pl.semaphore_signal(barrier, inc=1, device_id=device, device_id_type=MESH)
    pl.semaphore_wait(barrier, len(devices))


class TensorSum:
    def __init__(self, chunks, part, result, from_core, summed, from_y, sems):
        block = lax.axis_index("dp")
        lane = lax.axis_index("tensor")
        core = lax.rem(lane, 2)
        self.core_peer = (block, lane + 1 - 2 * core)
        self.y_peer = (block, lax.rem(lane + 2, 4))
        rows, width = part.shape
        half = width // 2
        self.step = rows // chunks
        self.mine = pl.ds(pl.multiple_of(core * half, half), half)
        self.other = pl.ds(pl.multiple_of((1 - core) * half, half), half)
        self.part, self.result = part, result
        self.from_core, self.summed, self.from_y = from_core, summed, from_y
        self.sems = sems

    def span(self, k):
        return pl.ds(pl.multiple_of(k * self.step, self.step), self.step)

    def to_core(self, k):
        at = self.span(k)
        return remote(
            self.part.at[at, self.other], self.from_core.at[at], self.sems[0].at[k],
            self.sems[1].at[k], self.core_peer,
        )

    def to_y(self, k):
        at = self.span(k)
        return remote(
            self.summed.at[at], self.from_y.at[at], self.sems[2].at[k], self.sems[3].at[k],
            self.y_peer,
        )

    def back(self, k):
        at = self.span(k)
        return remote(
            self.result.at[at, self.mine], self.result.at[at, self.mine], self.sems[4].at[k],
            self.sems[5].at[k], self.core_peer,
        )

    def first(self, k):
        self.to_core(k).start()

    def second(self, k):
        at = self.span(k)
        self.to_core(k).wait_recv()
        total = self.part[at, self.mine].astype(F32) + self.from_core[at].astype(F32)
        self.summed[at] = total.astype(BF16)
        self.to_y(k).start()

    def third(self, k):
        at = self.span(k)
        self.to_y(k).wait_recv()
        total = self.summed[at].astype(F32) + self.from_y[at].astype(F32)
        self.result[at, self.mine] = total.astype(BF16)
        self.back(k).start()

    def finish(self, chunks):
        @pl.loop(0, chunks)
        def _(k):
            self.back(k).wait_recv()
            self.back(k).wait_send()
            self.to_core(k).wait_send()
            self.to_y(k).wait_send()


def sum_scratch(chunks, rows, width):
    half = pltpu.VMEM((rows, width // 2), BF16)
    return [pltpu.VMEM((rows, width), BF16), half, half, half] + [
        pltpu.SemaphoreType.DMA((chunks,))
    ] * 6


def grad_rows(left_ref, right, target, which):
    levels, rows = target.shape[0], target.shape[1]

    @pl.loop(0, levels)
    def _(lev):
        if rows % 128 == 0:
            cols = pl.ds(pl.multiple_of((2 * lev + which) * rows, rows), rows)
            target[lev] = contract(left_ref[:, cols], right[...], 0, 0).astype(BF16)
        else:
            cols = pl.ds(pl.multiple_of(2 * lev * rows, 2 * rows), 2 * rows)
            both = contract(left_ref[:, cols], right[...], 0, 0)
            target[lev] = jnp.where(which == 0, both[:rows], both[rows:]).astype(BF16)


def hidden_back_kernel(
    chunks, dpre_ref, wu_ref, n2_ref, activ_ref, cot_ref, far_ref, dn_ref, own_ref, other_ref, down_ref, got_ref,
    activ_x, x_send, x_recv, part, from_core, summed, from_y, *sems,
):
    ts = TensorSum(chunks, part, dn_ref, from_core, summed, from_y, sems)
    side = lax.rem(lax.axis_index("dp"), 2)
    x_peer = (lax.axis_index("dp") + 1 - 2 * side, lax.axis_index("tensor"))
    greet([ts.core_peer, ts.y_peer, x_peer])
    half = activ_x.shape[1]
    mine = pl.ds(pl.multiple_of(side * half, half), half)
    theirs = pl.ds(pl.multiple_of((1 - side) * half, half), half)
    to_x = remote(activ_ref.at[:, theirs], activ_x, x_send.at[0], x_recv.at[0], x_peer)
    to_x.start()

    @pl.loop(0, chunks)
    def _(k):
        at = ts.span(k)
        part[at, :] = contract(dpre_ref[at, :], wu_ref[...], 1, 1).astype(BF16)
        ts.first(k)

        @pl.when(k >= 1)
        def _():
            ts.second(k - 1)

    ts.second(chunks - 1)
    grad_rows(n2_ref, dpre_ref, other_ref, 1 - side)
    rest = remote(
        other_ref.at[pl.ds(0, got_ref.shape[0])], got_ref, x_send.at[1], x_recv.at[1], x_peer
    )
    rest.start()
    grad_rows(n2_ref, dpre_ref, own_ref, side)
    levels, rows = down_ref.shape[0], down_ref.shape[1]

    @pl.loop(0, levels)
    def _(lev):
        cols = pl.ds(pl.multiple_of(lev * rows, rows), rows)
        down_ref[lev] = contract(cot_ref[:, cols], activ_ref[:, mine], 0, 0).astype(BF16)

    ready = chunks // 2

    @pl.loop(0, ready)
    def _(k):
        ts.third(k)

    to_x.wait_recv()

    @pl.loop(0, levels)
    def _(lev):
        cols = pl.ds(pl.multiple_of(lev * rows, rows), rows)
        far = contract(far_ref[:, cols], activ_x[...], 0, 0)
        down_ref[lev] = (down_ref[lev].astype(F32) + far).astype(BF16)

    @pl.loop(ready, chunks)
    def _(k):
        ts.third(k)

    ts.finish(chunks)
    to_x.wait_send()
    rest.wait()


def hidden_back(d_pre, up_weight, normed2, activ, cotangent, far_cotangent, count, chunks=4):
    rows, width = d_pre.shape[0], up_weight.shape[0]
    hidden = up_weight.shape[1]
    levels = count // 2
    half = jax.ShapeDtypeStruct((levels, width // count, hidden), BF16)
    got = jax.ShapeDtypeStruct((levels // 4, width // count, hidden), BF16)
    hbm = pl.BlockSpec(memory_space=pl.ANY)
    dma = pltpu.SemaphoreType.DMA
    return pl.pallas_call(
        functools.partial(hidden_back_kernel, chunks),
        out_shape=(
            jax.ShapeDtypeStruct((rows, width), BF16),
            half,
            half,
            jax.ShapeDtypeStruct((levels, width // levels, hidden // 2), BF16),
            got,
        ),
        in_specs=[VMEM] * 6,
        out_specs=(VMEM,) * 4 + (hbm,),
        scratch_shapes=[pltpu.VMEM((rows, hidden // 2), BF16), dma((2,)), dma((2,))]
        + sum_scratch(chunks, rows, width),
        compiler_params=pltpu.CompilerParams(
            collective_id=4, has_side_effects=True, vmem_limit_bytes=62 << 20
        ),
        name="hidden_back",
    )(d_pre, up_weight, normed2, activ, cotangent, far_cotangent)


class Chain:
    def __init__(self, length, level, upper, lower, pair, bufs, sems):
        self.length, self.level = length, level
        self.peers = (upper, lower)
        self.pair = pair
        self.bufs = bufs
        self.sems = sems

    def copy(self, way, s):
        inward, outward = self.bufs[2 * way], self.bufs[2 * way + 1]
        send, recv = self.sems[2 * way], self.sems[2 * way + 1]
        return remote(
            outward.at[s - 1], inward.at[s - 1], send.at[s - 1], recv.at[s - 1], self.peers[way]
        )

    def rank(self, way):
        return self.level if way == 0 else self.length - 1 - self.level

    def start(self, s):
        for way in range(2):
            rank = self.rank(way)
            slot = rank + self.length - s
            slot = jnp.clip(slot if way == 0 else self.length - 1 - slot, 0, self.length - 1)
            inward, outward = self.bufs[2 * way], self.bufs[2 * way + 1]

            @pl.when(rank <= s - 1)
            def _(way=way, rank=rank, slot=slot, inward=inward, outward=outward):
                outward[s - 1] = self.pair[slot]
                if s > 1:
                    @pl.when(rank >= 1)
                    def _():
                        outward[s - 1] = (
                            self.pair[slot].astype(F32) + inward[s - 2].astype(F32)
                        ).astype(BF16)

                self.copy(way, s).start()

    def arrive(self, s):
        for way in range(2):
            rank = self.rank(way)

            @pl.when((rank >= 1) & (rank <= s))
            def _(way=way):
                self.copy(way, s).wait_recv()

    def result(self, target):
        last = self.length - 2
        target[...] = self.pair[self.level].astype(F32)
        for way in range(2):
            @pl.when(self.rank(way) >= 1)
            def _(way=way):
                target[...] += self.bufs[2 * way][last].astype(F32)

    def drain(self, last=None):
        for s in range(1, (last or self.length - 1) + 1):
            for way in range(2):
                rank = self.rank(way)

                @pl.when(rank <= s - 1)
                def _(way=way, s=s):
                    self.copy(way, s).wait_send()


def chain_scratch(length, shape):
    return [pltpu.VMEM((length - 1,) + shape, BF16)] * 4 + [
        pltpu.SemaphoreType.DMA((length - 1,))
    ] * 4


def chain_peers():
    count = lax.axis_size("dp")
    block = lax.axis_index("dp")
    lane = lax.axis_index("tensor")
    level = block // 2
    upper = (jnp.where(level < count // 2 - 1, block + 2, block + 2 - count), lane)
    lower = (jnp.where(level > 0, block - 2, block - 2 + count), lane)
    return count // 2, level, upper, lower


def query_back_kernel(
    chunks, steps, dq_ref, wq_ref, n1_ref, dkv_ref, wide_ref, down_ref, dn_ref, grad_ref, tot_ref,
    far_up, far_down, down_out, d_send, d_recv, down_low, down_got,
    part, from_core, summed, from_y, kv_core, kv_sum, kv_x, kv_pair, kv_z, kv_up, kv_y, kv_sems, own_ref,
    other_ref, got_ref, q_send, q_recv, *rest,
):
    chain_bufs, chain_sems, sems = rest[:4], rest[4:8], rest[8:14]
    wide_bufs, wide_sems = rest[14:18], rest[18:]
    ts = TensorSum(chunks, part, dn_ref, from_core, summed, from_y, sems)
    block = lax.axis_index("dp")
    lane = lax.axis_index("tensor")
    place = lax.rem(block, SPAN)
    side = lax.rem(place, 2)
    level = place // 2
    levels = SPAN // 2
    x_peer = (block + 1 - 2 * side, lane)
    upper = (jnp.where(level < levels - 1, block + 2, block + 2 - SPAN), lane)
    lower = (jnp.where(level > 0, block - 2, block - 2 + SPAN), lane)
    length, chain_level, chain_upper, chain_lower = chain_peers()
    if length == levels:
        greet([ts.core_peer, ts.y_peer, x_peer, upper, lower])
    else:
        greet([ts.core_peer, ts.y_peer, x_peer, upper, lower, chain_upper, chain_lower])
    chain = Chain(length, chain_level, chain_upper, chain_lower, own_ref, chain_bufs, chain_sems)
    wide = Chain(length, chain_level, chain_upper, chain_lower, wide_ref, wide_bufs, wide_sems)
    core = lax.rem(lane, 2)
    seq_rows = tot_ref.shape[0]
    half = seq_rows // 2
    mine = pl.ds(pl.multiple_of(core * half, half), half)
    other = pl.ds(pl.multiple_of((1 - core) * half, half), half)

    def kv_copy(source, target, index, device):
        return remote(source, target, kv_sems.at[0, index], kv_sems.at[1, index], device)

    to_core = [
        kv_copy(
            dkv_ref.at[pl.ds(2 * lev, 2), other], kv_core.at[lev], 3 + levels + lev, ts.core_peer
        )
        for lev in range(levels)
    ]
    for copy in to_core:
        copy.start()
    grad_levels, rows = own_ref.shape[0], own_ref.shape[1]

    @pl.loop(0, chunks)
    def _(k):
        at = ts.span(k)
        part[at, :] = contract(dq_ref[at, :], wq_ref[...], 1, 1).astype(BF16)
        ts.first(k)

        @pl.when(k >= 1)
        def _():
            ts.second(k - 1)

    ts.second(chunks - 1)
    for lev in range(levels):
        to_core[lev].wait_recv()
        total = dkv_ref[pl.ds(2 * lev, 2), mine].astype(F32) + kv_core[lev].astype(F32)
        kv_sum[lev] = total.astype(BF16)

    to_x = kv_copy(kv_sum.at[:, 1 - side], kv_x, 1, x_peer)
    to_x.start()
    wide.start(1)

    def grad(target, which):
        grad_rows(n1_ref, dq_ref, target, which)

    grad(other_ref, 1 - side)
    q_to_x = remote(other_ref, got_ref, q_send, q_recv, x_peer)
    grad(own_ref, side)
    half_rows, half_cols = down_low.shape
    down_mine = pl.ds(pl.multiple_of(side * half_rows, half_rows), half_rows)
    down_theirs = pl.ds(pl.multiple_of((1 - side) * half_rows, half_rows), half_rows)
    down_low[...] = down_ref[down_theirs].astype(BF16)
    to_x.wait_recv()
    q_to_x.start()
    d_to_x = remote(down_low, down_got, d_send, d_recv, x_peer)
    d_to_x.start()

    @pl.loop(0, levels)
    def _(lev):
        kv_pair[lev] = (kv_sum[lev, side].astype(F32) + kv_x[lev].astype(F32)).astype(BF16)

    def down(s):
        slot = jnp.maximum(level - levels + s, 0)
        return kv_copy(kv_up.at[s - 1], kv_z.at[s - 1], 1 + s, lower), slot

    for s in range(1, levels):
        copy, slot = down(s)

        @pl.when(level >= levels - s)
        def _(copy=copy, slot=slot, s=s):
            kv_up[s - 1] = kv_pair[slot]
            if s > 1:
                @pl.when(level < levels - 1)
                def _():
                    kv_up[s - 1] = (
                        kv_pair[slot].astype(F32) + kv_z[s - 2].astype(F32)
                    ).astype(BF16)

            copy.start()

        @pl.when((level >= levels - 1 - s) & (level < levels - 1))
        def _(copy=copy):
            copy.wait_recv()

    kv_up[levels - 1] = kv_pair[level]

    @pl.when(level < levels - 1)
    def _():
        kv_up[levels - 1] = (
            kv_pair[level].astype(F32) + kv_z[levels - 2].astype(F32)
        ).astype(BF16)

    to_y = kv_copy(kv_up.at[levels - 1], kv_y, 1 + levels, ts.y_peer)
    to_y.start()
    for s in range(1, steps):
        wide.arrive(s)
        wide.start(s + 1)
    q_to_x.wait_recv()

    @pl.loop(0, grad_levels)
    def _(lev):
        own_ref[lev] = (own_ref[lev].astype(F32) + got_ref[lev].astype(F32)).astype(BF16)

    chain.start(1)
    to_y.wait_recv()
    tot_ref[mine] = (kv_up[levels - 1].astype(F32) + kv_y[...].astype(F32)).astype(BF16)
    back = kv_copy(tot_ref.at[mine], tot_ref.at[mine], 2 + levels, ts.core_peer)
    back.start()
    half_way = chunks // 2
    for s in range(1, length):
        if s == 2:
            @pl.loop(0, half_way)
            def _(k):
                ts.third(k)

        chain.arrive(s)
        if s + 1 < length:
            chain.start(s + 1)

    @pl.loop(half_way, chunks)
    def _(k):
        ts.third(k)

    chain.result(grad_ref)
    d_to_x.wait()
    first = pl.ds(pl.multiple_of(side * half_cols, half_cols), half_cols)
    second = pl.ds(pl.multiple_of((1 - side) * half_cols, half_cols), half_cols)
    down_out[:, first] = down_ref[down_mine]
    down_out[:, second] = down_got[...].astype(F32)
    wide.arrive(steps)
    far_up[...] = wide.bufs[0][steps - 1]
    far_down[...] = wide.bufs[2][steps - 1]
    chain.drain()
    wide.drain(steps)
    q_to_x.wait_send()
    back.wait()
    for copy in to_core:
        copy.wait_send()
    to_x.wait_send()
    to_y.wait_send()
    for s in range(1, levels):
        copy, _slot = down(s)

        @pl.when(level >= levels - s)
        def _(copy=copy):
            copy.wait_send()

    ts.finish(chunks)


def query_back(d_queries, query_weight, normed1, parts, wide, down, count, chunks=4):
    rows, width = d_queries.shape[0], query_weight.shape[0]
    kv_width = parts.shape[2]
    steps = count // 2 - 2
    levels = SPAN // 2
    shape = (width // count, query_weight.shape[1])
    half = pltpu.VMEM((count // 2,) + shape, BF16)
    piece = (rows // 2, kv_width)
    return pl.pallas_call(
        functools.partial(query_back_kernel, chunks, steps),
        out_shape=(
            jax.ShapeDtypeStruct((rows, width), BF16),
            jax.ShapeDtypeStruct(shape, F32),
            jax.ShapeDtypeStruct((rows, kv_width), BF16),
            jax.ShapeDtypeStruct(wide.shape[1:], BF16),
            jax.ShapeDtypeStruct(wide.shape[1:], BF16),
            jax.ShapeDtypeStruct((down.shape[0] // 2, 2 * down.shape[1]), F32),
        ),
        in_specs=[VMEM] * 6,
        out_specs=(VMEM,) * 6,
        scratch_shapes=[
            pltpu.SemaphoreType.DMA,
            pltpu.SemaphoreType.DMA,
            pltpu.VMEM((down.shape[0] // 2, down.shape[1]), BF16),
            pltpu.VMEM((down.shape[0] // 2, down.shape[1]), BF16),
        ]
        + sum_scratch(chunks, rows, width)[:4]
        + [
            pltpu.VMEM((levels, 2) + piece, BF16),
            pltpu.VMEM((levels, 2) + piece, BF16),
            pltpu.VMEM((levels,) + piece, BF16),
            pltpu.VMEM((levels,) + piece, BF16),
            pltpu.VMEM((levels - 1,) + piece, BF16),
            pltpu.VMEM((levels,) + piece, BF16),
            pltpu.VMEM(piece, BF16),
            pltpu.SemaphoreType.DMA((2, 3 + 2 * levels)),
            half,
            half,
            half,
            pltpu.SemaphoreType.DMA,
            pltpu.SemaphoreType.DMA,
        ]
        + chain_scratch(count // 2, shape)
        + [pltpu.SemaphoreType.DMA((chunks,))] * 6
        + chain_scratch(steps + 1, wide.shape[1:]),
        compiler_params=pltpu.CompilerParams(
            collective_id=5, has_side_effects=True, vmem_limit_bytes=63 << 20
        ),
        name="query_back",
    )(d_queries, query_weight, normed1, parts, wide, down)


def finish_kernel(
    chunk, n1_ref, dkv_ref, wkv_ref, dn_ref, x_ref, dm_ref, gain_ref, vec_in, ends_ref, far_up, far_down,
    grad_x, grad_ref, vec_ref, up_ref, up_out, up_in, up_send, up_recv, own_ref, other_ref, got_ref,
    x_send, x_recv, own_vec, low_vec, slots, send, recv, acc, *chain_refs,
):
    block = lax.axis_index("dp")
    lane = lax.axis_index("tensor")
    count = lax.axis_size("dp")
    side = lax.rem(block, 2)
    pairs = count // 2
    others = [(lax.rem(block + 2 * k, count), lane) for k in range(1, pairs)]
    x_peer = (block + 1 - 2 * side, lane)
    greet([x_peer] + others)
    length, level, upper, lower = chain_peers()

    def last(way):
        return remote(
            up_out.at[way], up_in.at[way], up_send.at[way], up_recv.at[way], (upper, lower)[way]
        )

    ranks = (level, length - 1 - level)
    grad_rows(n1_ref, dkv_ref, other_ref, 1 - side)
    to_x = remote(other_ref, got_ref, x_send, x_recv, x_peer)
    to_x.start()
    for way, far in enumerate((far_up, far_down)):
        @pl.when(ranks[way] < length - 1)
        def _(way=way, far=far):
            up_out[way] = ends_ref[1 + way]

            @pl.when(ranks[way] >= 1)
            def _():
                up_out[way] = (ends_ref[1 + way].astype(F32) + far[...].astype(F32)).astype(BF16)

            last(way).start()

    grad_rows(n1_ref, dkv_ref, own_ref, side)
    rows, width = x_ref.shape
    acc[...] = jnp.zeros_like(acc)

    def norm_back(k):
        at = pl.ds(pl.multiple_of(k * chunk, chunk), chunk)
        values = x_ref[at, :].astype(F32)
        centred = values - jnp.mean(values, axis=-1, keepdims=True)
        scale = lax.rsqrt(jnp.mean(centred * centred, axis=-1, keepdims=True) + EPSILON)
        hat = centred * scale
        grad = dn_ref[at, :].astype(F32) + contract(dkv_ref[at, :], wkv_ref[...], 1, 1)
        acc[0] += jnp.sum((grad * hat).reshape(chunk // 8, 8, width), axis=0)
        acc[1] += jnp.sum(grad.reshape(chunk // 8, 8, width), axis=0)
        scaled = grad * gain_ref[...]
        first = jnp.mean(scaled, axis=-1, keepdims=True)
        second = jnp.mean(scaled * hat, axis=-1, keepdims=True)
        grad_x[at, :] = dm_ref[at, :].astype(F32) + scale * (scaled - first - hat * second)

    chain = Chain(length, level, upper, lower, own_ref, chain_refs[:4], chain_refs[4:8])
    chunks = rows // chunk
    half = chunks // 2

    @pl.loop(0, half)
    def _(k):
        norm_back(k)

    to_x.wait_recv()
    own_ref[...] = (own_ref[...].astype(F32) + got_ref[...].astype(F32)).astype(BF16)
    chain.start(1)

    @pl.loop(half, chunks)
    def _(k):
        norm_back(k)

    own_vec[...] = vec_in[...]
    own_vec[0:1, :] = jnp.sum(acc[0], axis=0, keepdims=True)
    own_vec[1:2, :] = jnp.sum(acc[1], axis=0, keepdims=True)
    head = dkv_ref.shape[1] // 2
    own_vec[2:3, 0:head] = jnp.sum(dkv_ref[:, head:].astype(F32), axis=0, keepdims=True)
    low_vec[0] = own_vec[...].astype(BF16)
    to_pair = remote(low_vec.at[0], slots.at[0], send.at[0], recv.at[0], x_peer)
    to_pair.start()
    chain.arrive(1)
    if length > 2:
        chain.start(2)
    to_pair.wait()
    own_vec[...] += slots[0].astype(F32)
    low_vec[1] = own_vec[...].astype(BF16)
    copies = []
    for k in range(1, pairs):
        copy = remote(low_vec.at[1], slots.at[k], send.at[k], recv.at[k], others[k - 1])
        copy.start()
        copies.append(copy)
    for s in range(2, length):
        chain.arrive(s)
        if s + 1 < length:
            chain.start(s + 1)
    chain.result(grad_ref)
    total = own_vec[...]
    for k in range(1, pairs):
        copies[k - 1].wait()
        total = total + slots[k].astype(F32)
    vec_ref[...] = total
    up_ref[...] = ends_ref[0].astype(F32)
    for way in range(2):
        @pl.when(ranks[way] >= 1)
        def _(way=way):
            last(way).wait_recv()
            up_ref[...] += up_in[way].astype(F32)

        @pl.when(ranks[way] < length - 1)
        def _(way=way):
            last(way).wait_send()

    chain.drain()
    to_x.wait_send()


def finish(
    normed1, d_keyval, keyval_weight, d_normed1, inputs, d_middle, gain, values, ends, far_up, far_down, count,
    chunk=128,
):
    rows, width = inputs.shape
    flat = jnp.concatenate(values)
    lines = -(-flat.shape[0] // width)
    height = -(-(3 + lines) // 8) * 8
    packed = jnp.pad(flat, (3 * width, (height - 3) * width - flat.shape[0])).reshape(height, width)
    shape = (width // count, d_keyval.shape[1])
    half = pltpu.VMEM((count // 2,) + shape, BF16)
    dma = pltpu.SemaphoreType.DMA
    two = pltpu.VMEM((2,) + far_up.shape, BF16)
    grad_x, grad, total, wide = pl.pallas_call(
        functools.partial(finish_kernel, chunk),
        out_shape=(
            jax.ShapeDtypeStruct((rows, width), F32),
            jax.ShapeDtypeStruct(shape, F32),
            jax.ShapeDtypeStruct((height, width), F32),
            jax.ShapeDtypeStruct(far_up.shape, F32),
        ),
        in_specs=[VMEM] * 11,
        out_specs=(VMEM,) * 4,
        scratch_shapes=[two, two, dma((2,)), dma((2,)), half, half, half, dma, dma]
        + [
            pltpu.VMEM((height, width), F32),
            pltpu.VMEM((2, height, width), BF16),
            pltpu.VMEM((count // 2, height, width), BF16),
            dma((count // 2,)),
            dma((count // 2,)),
            pltpu.VMEM((2, 8, width), F32),
        ]
        + chain_scratch(count // 2, shape),
        compiler_params=pltpu.CompilerParams(
            collective_id=2, has_side_effects=True, vmem_limit_bytes=56 << 20
        ),
        name="finish",
    )(
        normed1, d_keyval, keyval_weight, d_normed1, inputs, d_middle, gain.reshape(1, width), packed, ends,
        far_up, far_down,
    )
    flat = total[3:].reshape(-1)
    pieces = []
    start = 0
    for value in values:
        pieces.append(flat[start : start + value.shape[0]])
        start += value.shape[0]
    head = d_keyval.shape[1] // 2
    return grad_x, grad, total[0], total[1], total[2, :head], pieces, wide


def together(*values):
    return lax.optimization_barrier(values)


class ScatterSum:
    def __init__(self, own, other, arrived=None):
        self.count = lax.axis_size("dp")
        self.length = self.count // 2
        self.level = lax.axis_index("dp") // 2
        self.own = own
        if arrived is not None:
            other = other[arrived.shape[0] :]
        got = lax.ppermute(other, "dp", [(p, p ^ 1) for p in range(self.count)])
        if arrived is not None:
            got = jnp.concatenate([arrived, got], axis=0)
        self.flying = (got,)
        self.s = 0

    def shifted(self, value, sources, step):
        pairs = [
            (2 * source + side, 2 * (source + step) + side)
            for source in sources
            for side in range(2)
        ]
        return lax.ppermute(value, "dp", pairs)

    def slot(self, index):
        index = jnp.clip(index, 0, self.length - 1)
        return lax.dynamic_index_in_dim(self.total, index, 0, keepdims=False)

    def step(self, *values):
        length, level = self.length, self.level
        self.s += 1
        s = self.s
        if s == 1:
            self.total = (self.own.astype(F32) + self.flying[0].astype(F32)).astype(BF16)
            up, down = self.slot(level + length - 1), self.slot(level - length + 1)
        else:
            up, down = self.flying
            up = self.slot(level + length - s).astype(F32) + up.astype(F32)
            if s == length:
                self.result = up + down.astype(F32)
                return values
            down = self.slot(level - length + s).astype(F32) + down.astype(F32)
            up, down = up.astype(BF16), down.astype(BF16)
        up, down, *values = together(up, down, *values)
        self.flying = (
            self.shifted(up, range(0, s), 1),
            self.shifted(down, range(length - s, length), -1),
        )
        return values

    def finish(self):
        while self.s < self.length:
            self.step()
        return self.result


def weight_grad_kernel(left_ref, right_ref, own_ref, other_ref):
    side = lax.rem(lax.axis_index("dp"), 2)
    grad_rows(left_ref, right_ref, other_ref, 1 - side)
    grad_rows(left_ref, right_ref, own_ref, side)


def weight_grad(left, right, count):
    half = jax.ShapeDtypeStruct((count // 2, left.shape[1] // count, right.shape[1]), BF16)
    return pl.pallas_call(
        weight_grad_kernel,
        out_shape=(half, half),
        in_specs=[VMEM] * 2,
        out_specs=(VMEM,) * 2,
        compiler_params=pltpu.CompilerParams(vmem_limit_bytes=40 << 20),
        cost_estimate=pl.CostEstimate(
            flops=2 * left.shape[0] * left.shape[1] * right.shape[1],
            bytes_accessed=16 << 20,
            transcendentals=0,
        ),
        name="weight_grad",
    )(left, right)


def front_kernel(
    block, chunks, q_ref, own_kv, cot_hbm, wo_ref, wd_hbm, kv_ref, ctx_ref, lse_ref, sum_ref, g_ref, far_ref,
    cot_ref, wd_ref, local_sem, x_send, x_recv, z_send, z_recv, s_send, s_recv, f_send, f_recv, acc, peak, total,
    part, from_core, summed, from_y, *sems,
):
    ts = TensorSum(chunks, part, sum_ref, from_core, summed, from_y, sems)
    dp = lax.axis_index("dp")
    lane = lax.axis_index("tensor")
    place = lax.rem(dp, SPAN)
    side = lax.rem(place, 2)
    level = place // 2
    levels = SPAN // 2
    core = lax.rem(lane, 2)
    y_lane = lax.rem(lane + 2, 4)
    core_peer, y_peer = ts.core_peer, ts.y_peer
    x_peer = (dp + 1 - 2 * side, lane)
    upper = (jnp.where(level < levels - 1, dp + 2, dp + 2 - SPAN), lane)
    lower = (jnp.where(level > 0, dp - 2, dp - 2 + SPAN), lane)
    seq_rows = own_kv.shape[0]
    piece = seq_rows // 4
    head = kv_ref.shape[2] // 2
    heads = q_ref.shape[1] // head
    parts = seq_rows // block

    def rows_of(which):
        return pl.ds(pl.multiple_of(which * piece, piece), piece)

    local = [
        pltpu.make_async_copy(own_kv, kv_ref.at[place], local_sem.at[0]),
        pltpu.make_async_copy(cot_hbm, cot_ref, local_sem.at[1]),
        pltpu.make_async_copy(wd_hbm, wd_ref, local_sem.at[2]),
    ]
    local[0].start()
    greet([core_peer, y_peer, x_peer, upper, lower])
    to_x = remote(own_kv.at[rows_of(lane)], kv_ref.at[place, rows_of(lane)], x_send, x_recv, x_peer)
    to_x.start()
    far_pieces = f_send.shape[1]
    far_step = cot_hbm.shape[0] // (2 * far_pieces)

    def far(kind, k):
        start = pl.multiple_of((core * far_pieces + k) * far_step, far_step)
        source = cot_hbm if kind == 0 else far_ref
        return remote(
            source.at[pl.ds(start, far_step)], far_ref.at[pl.ds(start, far_step)], f_send.at[kind, k],
            f_recv.at[kind, k], x_peer if kind == 0 else core_peer,
        )

    def share(s, kind):
        at = rows_of(y_lane if kind == 2 else lane)
        ref = kv_ref.at[pl.ds(2 * (level - s), 2), at]
        return remote(
            ref, ref, s_send.at[s, kind], s_recv.at[s, kind], y_peer if kind == 0 else core_peer
        )

    def share_pair(kind):
        ref = kv_ref.at[place + 1 - 2 * side, rows_of(y_lane if kind == 2 else lane)]
        return remote(
            ref, ref, s_send.at[0, kind], s_recv.at[0, kind], y_peer if kind == 0 else core_peer
        )

    def up(s):
        ref = kv_ref.at[pl.ds(2 * (level - s), 2), rows_of(lane)]
        return remote(ref, ref, z_send.at[s], z_recv.at[s], upper)

    def from_below(s):
        ref = kv_ref.at[pl.ds(2 * (level - 1 - s), 2), rows_of(lane)]
        return remote(ref, ref, z_send.at[s], z_recv.at[s], upper)

    def forward(s):
        from_below(s - 1).wait_recv()

        @pl.when((s < levels - 1) & (level < levels - 1))
        def _():
            up(s).start()

        share(s, 0).start()
        share(s, 1).start()

    def score(i, h, at_block, at_row, diagonal):
        keys = kv_ref[at_block, pl.ds(at_row, block), 0:head]
        query = q_ref[i * block : (i + 1) * block, h * head : (h + 1) * head]
        scores = contract(keys, query, 1, 1)
        if diagonal:
            key_at = lax.broadcasted_iota(jnp.int32, scores.shape, 0)
            query_at = lax.broadcasted_iota(jnp.int32, scores.shape, 1)
            scores = jnp.where(key_at <= query_at, scores, NEG_LARGE)
        return scores

    def soften(i, h, scores):
        old = peak[i, h]
        new = jnp.maximum(old, jnp.max(scores, axis=0, keepdims=True))
        probs = jnp.exp(scores - new)
        fade = jnp.exp(old - new)
        total[i, h] = total[i, h] * fade + jnp.sum(probs, axis=0, keepdims=True)
        peak[i, h] = new
        return probs.astype(BF16), fade

    def weigh(i, h, at_block, at_row, probs, fade):
        values = kv_ref[at_block, pl.ds(at_row, block), head : 2 * head]
        acc[i, h] = acc[i, h] * fade + contract(values, probs, 0, 0)

    def attend(i, pieces):
        items = [(h, piece) for piece in pieces for h in range(heads)]
        scores = score(i, items[0][0], *items[0][1])
        waiting = None
        for n, (h, (at_block, at_row, _diagonal)) in enumerate(items):
            following = None
            if n + 1 < len(items):
                following = score(i, items[n + 1][0], *items[n + 1][1])
            probs, fade = soften(i, h, scores)
            if waiting is not None:
                weigh(i, *waiting)
            waiting = (h, at_block, at_row, probs, fade)
            scores = following
        weigh(i, *waiting)

    def attend_level(i, s):
        @pl.loop(0, 2)
        def _(b):
            attend(i, [(2 * (level - s) + b, n * block, False) for n in range(parts)])

    peak[...] = jnp.full_like(peak, NEG_LARGE)
    total[...] = jnp.zeros_like(total)
    acc[...] = jnp.zeros_like(acc)
    local[0].wait()
    for copy in local[1:]:
        copy.start()
    for k in range(far_pieces):
        far(0, k).start()
    to_x.wait_recv()

    @pl.when(level < levels - 1)
    def _():
        up(0).start()

    share_pair(0).start()
    share_pair(1).start()
    for i in range(parts):
        attend(i, [(place, n * block, n == i) for n in range(i + 1)])

    @pl.when(level >= 1)
    def _():
        forward(1)

    share_pair(0).wait_recv()
    share_pair(2).start()
    share_pair(1).wait_recv()
    share_pair(2).wait_recv()

    @pl.when(side == 1)
    def _():
        for i in range(parts):
            attend(i, [(place - 1, n * block, False) for n in range(parts)])

    def complete(i):
        span = slice(i * block, (i + 1) * block)
        for h in range(heads):
            context = acc[i, h] / total[i, h]
            ctx_ref[span, h * head : (h + 1) * head] = context.T.astype(BF16)
            lse_ref[h : h + 1, span] = peak[i, h] + jnp.log(total[i, h])
        each = chunks // parts
        first = i * each

        @pl.loop(first, first + each)
        def _(k):
            at = ts.span(k)
            part[at, :] = jnp.dot(
                ctx_ref[at, :], wo_ref[...], preferred_element_type=F32
            ).astype(BF16)
            ts.first(k)

        @pl.loop(first, first + each)
        def _(k):
            ts.second(k)

    @pl.loop(1, level + 1)
    def _(s):
        @pl.when(s < level)
        def _():
            forward(s + 1)

        share(s, 0).wait_recv()
        share(s, 2).start()
        share(s, 1).wait_recv()
        share(s, 2).wait_recv()
        attend_level(0, s)

    complete(0)
    for i in range(1, parts):
        @pl.loop(1, level + 1)
        def _(s, i=i):
            attend_level(i, s)

        complete(i)

    for k in range(far_pieces):
        far(0, k).wait_recv()
        far(1, k).start()
    ready = chunks - chunks // parts

    @pl.loop(0, ready)
    def _(k):
        ts.third(k)

    for copy in local[1:]:
        copy.wait()
    tile = g_ref.shape[1] // 8

    @pl.loop(0, 8)
    def _(j):
        cols = pl.ds(pl.multiple_of(j * tile, tile), tile)
        g_ref[:, cols] = contract(cot_ref[...], wd_ref[cols, :], 1, 1).astype(BF16)

    @pl.loop(ready, chunks)
    def _(k):
        ts.third(k)

    to_x.wait_send()

    @pl.when(level < levels - 1)
    def _():
        up(0).wait_send()

    for kind in range(3):
        share_pair(kind).wait_send()

    @pl.loop(1, level + 1)
    def _(s):
        for kind in range(3):
            share(s, kind).wait_send()

        @pl.when((s < levels - 1) & (level < levels - 1))
        def _():
            up(s).wait_send()

    for k in range(far_pieces):
        far(0, k).wait_send()
        far(1, k).wait()
    ts.finish(chunks)


def front(queries, keyval, cotangent, output_weight, down_weight, block=512, chunks=8):
    rows, width = queries.shape
    wide = output_weight.shape[1]
    hidden = down_weight.shape[0]
    head = keyval.shape[1] // 2
    heads = width // head
    levels = SPAN // 2
    dma = pltpu.SemaphoreType.DMA
    hbm = pl.BlockSpec(memory_space=pl.ANY)
    stat = pltpu.VMEM((rows // block, heads, 1, block), F32)
    return pl.pallas_call(
        functools.partial(front_kernel, block, chunks),
        out_shape=(
            jax.ShapeDtypeStruct((SPAN,) + keyval.shape, BF16),
            jax.ShapeDtypeStruct((rows, width), BF16),
            jax.ShapeDtypeStruct((heads, rows), F32),
            jax.ShapeDtypeStruct((rows, wide), BF16),
            jax.ShapeDtypeStruct((rows, hidden), BF16),
            jax.ShapeDtypeStruct(cotangent.shape, BF16),
        ),
        in_specs=[VMEM, VMEM, hbm, VMEM, hbm],
        out_specs=(VMEM,) * 5 + (hbm,),
        scratch_shapes=[
            pltpu.VMEM(cotangent.shape, BF16),
            pltpu.VMEM(down_weight.shape, BF16),
            dma((3,)),
            dma,
            dma,
            dma((levels - 1,)),
            dma((levels - 1,)),
            dma((levels, 3)),
            dma((levels, 3)),
            dma((2, 4)),
            dma((2, 4)),
            pltpu.VMEM((rows // block, heads, head, block), F32),
            stat,
            stat,
        ]
        + sum_scratch(chunks, rows, wide),
        compiler_params=pltpu.CompilerParams(
            collective_id=1, has_side_effects=True, vmem_limit_bytes=60 << 20
        ),
        name="front",
    )(queries, keyval, cotangent, output_weight, down_weight)


def attend_back_kernel(
    block, chunks, q_ref, kv_ref, do_ref, ctx_ref, lse_ref, pair_ref, mlp_ref, sent_ref, dq_ref, dkv_ref,
    grad_ref, out_ref, got_ref, dq_acc, dkv_acc, delta, x_send, x_recv, from_core, summed, from_y, *rest,
):
    sems, chain_refs = rest[:6], rest[6:]
    rows = q_ref.shape[0]
    head = kv_ref.shape[1] // 2
    heads = q_ref.shape[1] // head
    place = lax.rem(lax.axis_index("dp"), SPAN)
    side = lax.rem(lax.axis_index("dp"), 2)
    x_peer = (lax.axis_index("dp") + 1 - 2 * side, lax.axis_index("tensor"))
    ts = TensorSum(chunks, mlp_ref, out_ref, from_core, summed, from_y, sems)
    length, level, upper, lower = chain_peers()
    chain = Chain(length, level, upper, lower, pair_ref, chain_refs[:4], chain_refs[4:])
    greet([ts.core_peer, ts.y_peer, x_peer, upper, lower])
    left = got_ref.shape[0]
    to_x = remote(
        sent_ref.at[pl.ds(sent_ref.shape[0] - left, left)], got_ref, x_send, x_recv, x_peer
    )
    to_x.start()

    @pl.loop(0, chunks)
    def _(k):
        ts.first(k)

    chain.start(1)
    levels = SPAN // 2
    parts = 2 * rows // block
    per_slot = -(-(length - 1) // (levels - 1))
    done = 0
    for target in range(levels):
        dkv_acc[...] = jnp.zeros_like(dkv_acc)
        for i in range(rows // block):
            span = slice(i * block, (i + 1) * block)
            if target == 0:
                for h in range(heads):
                    cols = slice(h * head, (h + 1) * head)
                    product = do_ref[span, cols].astype(F32) * ctx_ref[span, cols].astype(F32)
                    delta[h : h + 1, span] = jnp.sum(product.T, axis=0, keepdims=True)
                dq_acc[i] = jnp.zeros_like(dq_acc[i])

            def step(j, diagonal, span=span, i=i):
                at = pl.ds(pl.multiple_of(j * block, block), block)
                kv_at = pl.ds(pl.multiple_of((target * parts + j) * block, block), block)
                keys = kv_ref[kv_at, 0:head]
                values = kv_ref[kv_at, head : 2 * head]
                d_keys = jnp.zeros((block, head), F32)
                d_values = jnp.zeros((block, head), F32)

                def begin(h):
                    cols = slice(h * head, (h + 1) * head)
                    scores = contract(keys, q_ref[span, cols], 1, 1)
                    if diagonal:
                        key_at = lax.broadcasted_iota(jnp.int32, scores.shape, 0)
                        query_at = lax.broadcasted_iota(jnp.int32, scores.shape, 1)
                        scores = jnp.where(key_at <= query_at, scores, NEG_LARGE)
                    return scores, contract(values, do_ref[span, cols], 1, 1)

                begun = begin(0)
                for h in range(heads):
                    cols = slice(h * head, (h + 1) * head)
                    scores, d_probs = begun
                    if h + 1 < heads:
                        begun = begin(h + 1)
                    probs = jnp.exp(scores - lse_ref[h : h + 1, span])
                    d_scores = (probs * (d_probs - delta[h : h + 1, span])).astype(BF16)
                    d_values += contract(probs.astype(BF16), do_ref[span, cols], 1, 0)
                    d_keys += contract(d_scores, q_ref[span, cols], 1, 0)
                    dq_acc[i, h] += contract(keys, d_scores, 0, 0)
                dkv_acc[at, 0:head] += d_keys
                dkv_acc[at, head : 2 * head] += d_values

            full = (place * rows + i * block) // block - target * parts

            @pl.loop(0, jnp.clip(full, 0, parts))
            def _(j):
                step(j, False)

            @pl.when((full >= 0) & (full < parts))
            def _():
                step(full, True)

            if target == 0 and i == 0:
                @pl.loop(0, chunks)
                def _(k):
                    ts.second(k)

        for b in range(2):
            dkv_ref[2 * target + b] = dkv_acc[b * rows : (b + 1) * rows].astype(BF16)
        if target < levels - 1:
            for _ in range(per_slot):
                if done < length - 1:
                    done += 1
                    chain.arrive(done)
                    if done < length - 1:
                        chain.start(done + 1)
            if done == length - 1:
                chain.result(grad_ref)
        if target == levels - 2:
            @pl.loop(0, chunks)
            def _(k):
                ts.third(k)

    for i in range(rows // block):
        span = slice(i * block, (i + 1) * block)
        for h in range(heads):
            dq_ref[span, h * head : (h + 1) * head] = (
                (dq_acc[i, h] * head**-0.5).T.astype(BF16)
            )
    chain.drain()
    ts.finish(chunks)
    to_x.wait()


def attend_back(queries, keyval, d_context, context, lse, pair, mlp_part, sent, block=512, chunks=4):
    rows, width = queries.shape
    head = keyval.shape[1] // 2
    heads = width // head
    hbm = pl.BlockSpec(memory_space=pl.ANY)
    dma = pltpu.SemaphoreType.DMA
    return pl.pallas_call(
        functools.partial(attend_back_kernel, block, chunks),
        out_shape=(
            jax.ShapeDtypeStruct((rows, width), BF16),
            jax.ShapeDtypeStruct((SPAN, rows, 2 * head), BF16),
            jax.ShapeDtypeStruct(pair.shape[1:], F32),
            jax.ShapeDtypeStruct(mlp_part.shape, BF16),
            jax.ShapeDtypeStruct((sent.shape[0] * 3 // 4,) + sent.shape[1:], BF16),
        ),
        in_specs=[VMEM] * 7 + [hbm],
        out_specs=(VMEM,) * 4 + (hbm,),
        scratch_shapes=[
            pltpu.VMEM((rows // block, heads, head, block), F32),
            pltpu.VMEM((2 * rows, 2 * head), F32),
            pltpu.VMEM((heads, rows), F32),
            dma,
            dma,
        ]
        + sum_scratch(chunks, *mlp_part.shape)[1:]
        + chain_scratch(*pair.shape[:1], pair.shape[1:]),
        compiler_params=pltpu.CompilerParams(
            collective_id=6, has_side_effects=True, vmem_limit_bytes=63 << 20
        ),
        name="attend_back",
    )(queries, keyval, d_context, context, lse, pair, mlp_part, sent)


def layer_norm(values, norm_gain, norm_bias):
    average = jnp.mean(values, axis=-1, keepdims=True)
    centred = values - average
    variance = jnp.mean(centred * centred, axis=-1, keepdims=True)
    return centred * lax.rsqrt(variance + EPSILON) * norm_gain + norm_bias


def gelu_tanh(values):
    return jax.nn.gelu(values, approximate=True)


def per_device(
    inputs,
    first_gain,
    first_bias,
    query_weight,
    query_bias,
    keyval_weight,
    value_bias,
    output_weight,
    output_bias,
    second_gain,
    second_bias,
    up_weight,
    up_bias,
    down_weight,
    down_bias,
    cotangent,
):
    count = lax.axis_size("dp")
    head_size = value_bias.shape[0]
    score_scale = head_size ** (-0.5)
    x_full = inputs.astype(F32)
    normed1 = layer_norm(x_full, first_gain, first_bias).astype(BF16)
    query_pre = jnp.dot(normed1, query_weight, preferred_element_type=F32) + query_bias
    queries = (query_pre * score_scale).astype(BF16)
    kv_bias = jnp.concatenate([jnp.zeros_like(value_bias), value_bias])
    keyval = (jnp.dot(normed1, keyval_weight, preferred_element_type=F32) + kv_bias).astype(BF16)
    keyval_all, context_low, lse, attn_sum, d_activ, far_cotangent = front(
        queries, keyval, cotangent, output_weight, down_weight
    )
    keyval_all = keyval_all.reshape(-1, keyval.shape[1])
    middle = x_full + attn_sum.astype(F32) + output_bias
    normed2_full, second_pull = jax.vjp(layer_norm, middle, second_gain, second_bias)
    normed2 = normed2_full.astype(BF16)
    pre_act = jnp.dot(normed2, up_weight, preferred_element_type=F32) + up_bias
    act_full, gelu_pull = jax.vjp(gelu_tanh, pre_act)
    activ = act_full.astype(BF16)
    grad_full = cotangent.astype(F32)
    d_pre = gelu_pull(d_activ.astype(F32))[0].astype(BF16)
    d_normed2, up_own, up_other, pair_down, arrived = hidden_back(
        d_pre, up_weight, normed2, activ, cotangent, far_cotangent, count
    )
    d_up_bias = jnp.sum(d_pre.astype(F32), axis=0)
    d_down_bias = jnp.sum(grad_full, axis=0)
    d_middle_norm, d_second_gain, d_second_bias = second_pull(d_normed2.astype(F32))
    d_middle = grad_full + d_middle_norm
    d_output_bias = jnp.sum(d_middle, axis=0)
    d_middle_low = d_middle.astype(BF16)
    d_context = contract(d_middle_low, output_weight, 1, 1).astype(BF16)
    mlp_part = jnp.dot(activ, down_weight, preferred_element_type=F32).astype(BF16)
    grad_out_own, grad_out_other = weight_grad(d_middle_low, context_low, count)
    scatter_out = ScatterSum(grad_out_own, grad_out_other)
    d_queries, d_kv_parts, half_down, mlp_sum, rest = attend_back(
        queries, keyval_all, d_context, context_low, lse, pair_down, mlp_part, up_other
    )
    arrived = jnp.concatenate([arrived, rest], axis=0)
    pair_up = (up_own.astype(F32) + arrived.astype(F32)).astype(BF16)
    scatter_out.finish()
    d_query_bias = jnp.sum(d_queries.astype(F32), axis=0)
    d_normed1_sum, sent_query, d_keyval, far_up, far_down, sent_down = query_back(
        d_queries, query_weight, normed1, d_kv_parts, pair_up, half_down, count
    )
    layer_out = (middle + mlp_sum.astype(F32) + down_bias).astype(BF16)
    level = lax.axis_index("dp") // 2
    ends = jnp.stack(
        [
            lax.dynamic_index_in_dim(pair_up, jnp.clip(level + k, 0, count // 2 - 1), 0, False)
            for k in (0, 1, -1)
        ]
    )
    grad_inputs, sent_kv, sum_gain, sum_bias, sum_value, sums, sent_up = finish(
        normed1,
        d_keyval,
        keyval_weight,
        d_normed1_sum,
        inputs,
        d_middle_low,
        first_gain,
        [d_up_bias, d_output_bias, d_second_gain, d_second_bias, d_down_bias, d_query_bias],
        ends,
        far_up,
        far_down,
        count,
    )
    return (
        layer_out,
        grad_inputs,
        sum_gain,
        sum_bias,
        sent_query,
        sums[5],
        sent_kv,
        sum_value,
        scatter_out.result.T,
        sums[1],
        sums[2],
        sums[3],
        sent_up,
        sums[0],
        sent_down.T,
        sums[4],
    )


def solution(mesh):
    in_specs = (
        P("dp", None),
        P(),
        P(),
        P(None, "tensor"),
        P("tensor"),
        P(),
        P(),
        P("tensor", None),
        P(),
        P(),
        P(),
        P(None, "tensor"),
        P("tensor"),
        P("tensor", None),
        P(),
        P("dp", None),
    )
    out_specs = (
        P("dp", None),
        P("dp", None),
        P(),
        P(),
        P("dp", "tensor"),
        P("tensor"),
        P("dp", None),
        P(),
        P("tensor", "dp"),
        P(),
        P(),
        P(),
        P("dp", "tensor"),
        P("tensor"),
        P("tensor", "dp"),
        P(),
    )
    return jax.shard_map(
        per_device, mesh=mesh, in_specs=in_specs, out_specs=out_specs, check_vma=False
    )
```

time: 816 us -> 612 us (0.75)
  starting transfers between devices: 156 us -> 16.3 us
  Pallas kernels: 364 us -> 464 us
  waiting for transfers between devices: 103 us -> 5.65 us
  other arithmetic: 98.2 us -> 55.1 us
  local copies, waits for them, and re-layouts: 35.8 us -> 22.2 us
  matrix products: 48.2 us -> 36.5 us
    ppermute x18 -> x6, starting transfers between devices: 152 us -> 15 us  [shifted(): return lax.ppermute(value, 'dp', pairs)]
    pallas_call x9 -> x4, Pallas kernels: 257 us -> 368 us  [the longest x1 124 us: query_back(): pl.pallas_call(functools.partial(query_back_kernel, chunks, steps), out_s...]
    ppermute x3 -> x1, waiting for transfers between devices: 72.3 us -> 0.01 us  [__init__(): got = lax.ppermute(other, 'dp', [(p, p ^ 1) for p in range(self.count)])]
    ppermute x18 -> x6, waiting for transfers between devices: 30.7 us -> 5.65 us  [shifted(): return lax.ppermute(value, 'dp', pairs)]
    add x2 -> x0, other arithmetic: 16.2 us -> none  [the longest x1 13.2 us: per_device(): grad_inputs = d_middle + d_x_norm]
    pallas_call x2 -> x1, Pallas kernels: 17 us -> 4.49 us  [weight_grad(): pl.pallas_call(weight_grad_kernel, out_shape=(half, half), in_specs=[VMEM...]
    unnamed x134 -> x83, local copies, waits for them, and re-layouts: 27.2 us -> 15.2 us
    convert_element_type x6 -> x2, other arithmetic: 12.8 us -> 1.07 us  [step(): up, down = (up.astype(BF16), down.astype(BF16))]
  transfers between devices with their start and end apart: 24 -> 7, of which waited for: 6 -> 1; matrix products, arithmetic and copies ran while one was open for 13% -> 7% of each run, Pallas kernels for 20% -> 49%
where the time goes in v3:
time: 612 us; the launch traced here: 601 us
  Pallas kernels  464 us (76%)
  other arithmetic  55.1 us (9%)
  matrix products  36.5 us (6%)
  local copies, waits for them, and re-layouts  22.2 us (4%)
  starting transfers between devices  16.3 us (3%)
    pallas_call x1, Pallas kernels, query_back(): pl.pallas_call(functools.partial(query_back_kernel, chunks, steps), out_s...  124 us
    pallas_call x1, Pallas kernels, attend_back(): pl.pallas_call(functools.partial(attend_back_kernel, block, chunks), out_...  113 us
    pallas_call x1, Pallas kernels, hidden_back(): pl.pallas_call(functools.partial(hidden_back_kernel, chunks), out_shape=(...  91.1 us
    pallas_call x1, Pallas kernels, front(): pl.pallas_call(functools.partial(front_kernel, block, chunks), out_shape=...  75.6 us
    pallas_call x1, Pallas kernels, finish(): pl.pallas_call(functools.partial(finish_kernel, chunk), out_shape=(jax.Sh...  55.7 us
    dot_general x1, matrix products, per_device(): pre_act = jnp.dot(normed2, up_weight, preferred_element_type=F32) + up_bias  17.2 us
    unnamed x83, local copies, waits for them, and re-layouts  15.2 us
    ppermute x6, starting transfers between devices, shifted(): return lax.ppermute(value, 'dp', pairs)  15 us
  transfers between devices with their start and end apart: 7, of which 1 were waited for; matrix products, arithmetic and copies ran while one was open for 7% of the time, Pallas kernels for 49%

profile of v3, /device:TPU:0, one launch (start us, length us, event | category | flops | bytes accessed | tf_op | source)
XLA Modules:
  0.0 601.2 jit_solution(12376189082063209825)
XLA Ops:
  0.7 3.0 convert_reduce_fusion.1
  3.7 3.6 fusion.5
  7.3 1.9 fusion.8.n1_ref
  9.2 3.3 multiply_convert_fusion.1.q_ref
  12.5 2.1 fusion.25.own_kv
  14.6 75.6 %front.1 = (bf16[8,1024,256]{2,1,0:T(8,128)(2,1)}, bf16[1024,512]{1,0:T(8,128)(2,1)}, f32[4,1024]{1,0:T(4,128)}, bf16[1024,2048]{1,0:T(8,128)(2,1)}, bf16[1024,2...) custom-call(bf16[1024,512]{1,0:T(8,128)(2,1)} %multiply_convert_fusion.1.q_ref, bf16[1024,256]{1,0:T(8,128)(2,1)} %fusion.25.own_kv, ...), custom_call_target="tpu_custom_call" | custom-call | tf_op jit(solution)/shard_map/front/pallas_call | solution.py:1018
  90.3 5.0 fusion.22
  95.3 0.8 copy-done.7
  96.2 2.4 multiply_reduce_fusion
  98.7 2.8 add_convert_fusion.2.n2_ref
  102.1 17.2 %convert_reduce_fusion.3 = (f32[2048]{0:T(1024)S(1)}, bf16[1024,2048]{1,0:T(8,128)(2,1)}, bf16[1024,2048]{1,0:T(8,128)(2,1)}) fusion(f32[2048]{0:T(1024)S(1)} %copy-done.30, bf16[1024,2048]{1,0:T(8,128)(2,1)S(1)} %copy-done.29, bf16[1024,2048]{1,0:T(8,128)(2,1)S(1)} %add_convert_fusion.2.n2_ref, bf16[2048,2048]{1,0:T(8,128)(2,1)S(1)} %bitcast.44), kind=kOutput, calls=%fused_computation.34 | convolution fusion | flops 8644458496 | bytes 25182208 | tf_op jit(solution)/shard_map/dot_general | solution.py:1246
  119.3 91.1 %hidden_back.1 = (bf16[1024,2048]{1,0:T(8,128)(2,1)}, bf16[4,256,2048]{2,1,0:T(8,128)(2,1)}, bf16[4,256,2048]{2,1,0:T(8,128)(2,1)}, bf16[4,512,1024]{2,1,0:T(8,128)(2,1)}, bf16[1,256,2048]{2,1,0:T(8,128)(2,1)}) custom-call(bf16[1024,2048]{1,0:T(8,128)(2,1)} %get-tuple-element.106.dpre_ref, bf16[2048,2048]{1,0:T(8,128)(2,1)} %wu_ref.1, ...), custom_call_target="tpu_custom_call" | custom-call | tf_op jit(solution)/shard_map/hidden_back/pallas_call | solution.py:199
  210.5 8.9 %fusion.20 = (f32[2048]{0:T(1024)S(1)}, f32[1024]{0:T(1024)S(1)}, f32[2048]{0:T(1024)S(1)}) fusion(bf16[1024,2048]{1,0:T(8,128)(2,1)} %get-tuple-element.54, f32[1024]{0:T(1024)S(1)} %fusion.32, f32[1024]{0:T(1024)S(1)} %broadcast_multiply_fusion, f32[2048]{0:T(1024)S(1)} %copy-done.21, bf16[1024,2048]{1,0:T(8,128)(2,1)} %get-tuple-element.50, ...), kind=kLoop, calls=%fused_computation.33 | loop fusion | flops 27257856 | bytes 12627968 | tf_op jit(solution)/shard_map/transpose(jvp())/reduce_sum | solution.py:1205
  219.4 4.2 fusion.34
  223.7 2.9 convert_reduce_fusion.2
  226.7 4.5 weight_grad.1
  231.2 1.3 collective-permute-start
  232.5 3.3 convolution_convert_fusion.1.do_ref
  235.8 10.6 %convolution_convert_fusion.mlp_ref = bf16[1024,2048]{1,0:T(8,128)(2,1)} fusion(bf16[1024,2048]{1,0:T(8,128)(2,1)S(1)} %copy-done.14, bf16[2048,2048]{1,0:T(8,128)(2,1)S(1)} %bitcast.46), kind=kOutput, calls=%fused_computation.44 | convolution fusion | flops 8592031744 | bytes 16777216 | tf_op jit(solution)/shard_map/dot_general | solution.py:1261
  246.4 113.2 %attend_back.1 = (bf16[1024,512]{1,0:T(8,128)(2,1)}, bf16[8,1024,256]{2,1,0:T(8,128)(2,1)}, f32[512,1024]{1,0:T(8,128)}, bf16[1024,2048]{1,0:T(8,128)(2,1)}, bf16[3,256,2048]{2,1,0:T(8,128)(2,1)}) custom-call(bf16[1024,512]{1,0:T(8,128)(2,1)} %multiply_convert_fusion.1.q_ref, bf16[8192,256]{1,0:T(8,128)(2,1)} %bitcast.47, ...), custom_call_target="tpu_custom_call" | custom-call | tf_op jit(solution)/shard_map/attend_back/pallas_call | solution.py:1174
  359.6 1.4 convert_reduce_fusion.4
  361.1 5.6 add_convert_fusion.wide_ref
  366.7 0.7 reshape.109.vec_in
  367.4 123.8 %query_back.1 = (bf16[1024,2048]{1,0:T(8,128)(2,1)}, f32[256,512]{1,0:T(8,128)}, bf16[1024,256]{1,0:T(8,128)(2,1)}, bf16[256,2048]{1,0:T(8,128)(2,1)}, bf16[256,2048]{1,0:T(8,128)(2,1)}, /*index=5*/f32[256,2048]{1,0:T(8,128)}) custom-call(bf16[1024,512]{1,0:T(8,128)(2,1)} %get-tuple-element.60.dq_ref, bf16[2048,512]{1,0:T(8,128)(2,1)} %wq_ref.1, ...), custom_call_target="tpu_custom_call" | custom-call | tf_op jit(solution)/shard_map/query_back/pallas_call | solution.py:478
  491.3 7.7 %add_convert_fusion.1 = bf16[1024,2048]{1,0:T(8,128)(2,1)} fusion(bf16[1024,2048]{1,0:T(8,128)(2,1)} %get-tuple-element.59, bf16[1024,2048]{1,0:T(8,128)(2,1)} %get-tuple-element.50, bf16[1024,2048]{1,0:T(8,128)(2,1)} %x_ref.1, f32[2048]{0:T(1024)S(1)} %copy-done.25, f32[2048]{0:T(1024)S(1)} %copy-done.21), kind=kLoop, calls=%fused_computation.36 | loop fusion | flops 16777216 | bytes 16793600 | tf_op jit(solution)/shard_map/convert_element_type | solution.py:1274
  499.0 1.5 add_convert_fusion.3
  500.6 0.7 collective-permute-start.2
  501.3 2.1 collective-permute-start.1
  503.8 5.6 collective-permute-done.1
  509.6 0.7 collective-permute-start.4
  510.2 5.0 collective-permute-start.3
  515.3 2.0 pad_maximum_fusion.ends_ref
  517.3 55.7 %finish.1 = (f32[1024,2048]{1,0:T(8,128)}, f32[256,256]{1,0:T(8,128)}, f32[16,2048]{1,0:T(8,128)}, f32[256,2048]{1,0:T(8,128)}) custom-call(bf16[1024,2048]{1,0:T(8,128)(2,1)} %copy-done.9, bf16[1024,256]{1,0:T(8,128)(2,1)} %get-tuple-element.66.dkv_ref, bf16[2048,256]{1,0:T(8,128)(2,1)} %wkv_ref.1, bf16[1024,2048]{1,0:T(8,128)(2,1)} %get-tuple-element.67.dn_ref, ...), custom_call_target="tpu_custom_call" | custom-call | tf_op jit(solution)/shard_map/finish/pallas_call | solution.py:648
  573.0 0.9 fusion.26
  573.9 1.3 collective-permute-start.6
  575.2 5.3 collective-permute-start.5
  580.5 1.8 fusion.35
  582.3 0.9 slice.52
  583.2 0.7 reshape.110
  583.9 1.3 slice.65
  585.1 1.8 copy.33
  586.9 1.2 slice_bitcast_fusion
  588.1 1.0 fusion.31
  589.2 1.0 copy.32
  590.2 8.0 %copy.43 = f32[1024,2048]{1,0:T(8,128)} copy(f32[1024,2048]{1,0:T(8,128)} %get-tuple-element.144) | data formatting | bytes 16777216
  598.2 0.8 copy.44
  599.0 0.7 copy.45
  599.7 1.3 copy.46
  (96 shorter events, 1.4 us)
Async XLA Ops:
  0.6 6.6 %copy-start.4 = (bf16[1024,2048]{1,0:T(8,128)(2,1)S(1)}, bf16[1024,2048]{1,0:T(8,128)(2,1)}, u32[]{:S(2)}) copy-start(bf16[1024,2048]{1,0:T(8,128)(2,1)} %x_ref.1) | copy-start | bytes 12582916
  0.7 6.6 %copy-start.28 = (f32[128]{0:T(128)S(1)}, f32[128]{0:T(128)}, u32[]{:S(2)}) copy-start(f32[128]{0:T(128)} %param.22) | copy-start | bytes 1540
  0.7 6.6 %copy-start.26 = (f32[2048]{0:T(1024)S(1)}, f32[2048]{0:T(1024)}, u32[]{:S(2)}) copy-start(f32[2048]{0:T(1024)} %param.18) | copy-start | bytes 24580
  0.7 6.6 %copy-start.24 = (f32[2048]{0:T(1024)S(1)}, f32[2048]{0:T(1024)}, u32[]{:S(2)}) copy-start(f32[2048]{0:T(1024)} %param.17) | copy-start | bytes 24580
  0.7 8.5 %copy-start.15 = (bf16[2048,512]{1,0:T(8,128)(2,1)S(1)}, bf16[2048,512]{1,0:T(8,128)(2,1)}, u32[]{:S(2)}) copy-start(bf16[2048,512]{1,0:T(8,128)(2,1)} %wq_ref.1) | copy-start | bytes 6291460
  0.7 8.5 %copy-start.31 = (f32[512]{0:T(512)S(1)}, f32[512]{0:T(512)}, u32[]{:S(2)}) copy-start(f32[512]{0:T(512)} %param.20) | copy-start | bytes 6148
  9.2 3.3 copy-start.9
  9.2 3.3 copy-start.19
  14.6 75.6 %copy-start.21 = (f32[2048]{0:T(1024)S(1)}, f32[2048]{0:T(1024)}, u32[]{:S(2)}) copy-start(f32[2048]{0:T(1024)} %param.24) | copy-start | bytes 24580
  90.2 5.1 copy-start.5
  90.2 5.9 copy-start.7
  90.3 8.4 %copy-start.23 = (f32[2048]{0:T(1024)S(1)}, f32[2048]{0:T(1024)}, u32[]{:S(2)}) copy-start(f32[2048]{0:T(1024)} %param.25) | copy-start | bytes 24580
  90.3 8.4 %copy-start.27 = (f32[2048]{0:T(1024)S(1)}, f32[2048]{0:T(1024)}, u32[]{:S(2)}) copy-start(f32[2048]{0:T(1024)} %param.26) | copy-start | bytes 24580
  96.2 5.4 slice-start
  98.6 2.9 copy-start.29
  98.6 2.9 copy-start.30
  98.7 3.4 slice-start.1
  101.5 17.8 %copy-start.13 = (bf16[1024,2048]{1,0:T(8,128)(2,1)}, bf16[1024,2048]{1,0:T(8,128)(2,1)S(1)}, u32[]{:S(2)}) copy-start(bf16[1024,2048]{1,0:T(8,128)(2,1)S(1)} %add_convert_fusion.2.n2_ref) | copy-start | bytes 12582916
  210.4 8.9 %copy-start.6 = (bf16[1024,2048]{1,0:T(8,128)(2,1)S(1)}, bf16[1024,2048]{1,0:T(8,128)(2,1)}, u32[]{:S(2)}) copy-start(bf16[1024,2048]{1,0:T(8,128)(2,1)} %x_ref.1) | copy-start | bytes 12582916
  210.5 8.9 %copy-start.8 = (bf16[1024,2048]{1,0:T(8,128)(2,1)S(1)}, bf16[1024,2048]{1,0:T(8,128)(2,1)}, u32[]{:S(2)}) copy-start(bf16[1024,2048]{1,0:T(8,128)(2,1)} %get-tuple-element.50) | copy-start | bytes 12582916
  210.5 8.9 %copy-start.12 = (bf16[1024,2048]{1,0:T(8,128)(2,1)S(1)}, bf16[1024,2048]{1,0:T(8,128)(2,1)}, u32[]{:S(2)}) copy-start(bf16[1024,2048]{1,0:T(8,128)(2,1)} %get-tuple-element.54) | copy-start | bytes 12582916
  219.4 4.3 copy-start.10
  223.7 3.0 copy-start.3
  223.7 8.8 %copy-start.18 = (bf16[512,2048]{1,0:T(8,128)(2,1)S(1)}, bf16[512,2048]{1,0:T(8,128)(2,1)}, u32[]{:S(2)}) copy-start(bf16[512,2048]{1,0:T(8,128)(2,1)} %wo_ref.1) | copy-start | bytes 6291460
  226.6 9.2 %copy-start = (bf16[1024,2048]{1,0:T(8,128)(2,1)}, bf16[1024,2048]{1,0:T(8,128)(2,1)S(1)}, u32[]{:S(2)}) copy-start(bf16[1024,2048]{1,0:T(8,128)(2,1)S(1)} %get-tuple-element.109.dm_ref.left_ref) | copy-start | bytes 12582916
  226.6 9.2 %slice-start.2 = ((s8[8388608]{0:T(1024)(128)(4,1)}), s8[4194304]{0:T(1024)(128)(4,1)S(1)}, s32[]{:S(2)}) async-start(s8[8388608]{0:T(1024)(128)(4,1)} %bitcast.45), calls=%async_computation.2 | async-start | bytes 8388608
  231.1 15.2 %copy-start.1 = (bf16[4,256,512]{2,1,0:T(8,128)(2,1)}, bf16[4,256,512]{2,1,0:T(8,128)(2,1)S(1)}, u32[]{:S(2)}) copy-start(bf16[4,256,512]{2,1,0:T(8,128)(2,1)S(1)} %get-tuple-element.74) | copy-start | bytes 3145732
  231.2 4.6 copy-start.14
  231.2 4.6 slice-start.3
  231.2 267.8 %collective-permute-start = (bf16[4,256,512]{2,1,0:T(8,128)(2,1)}, bf16[4,256,512]{2,1,0:T(8,128)(2,1)}, u32[]{:S(2)}, u32[]{:S(2)}) collective-permute-start(bf16[4,256,512]{2,1,0:T(8,128)(2,1)} %get-tuple-element.75), channel_id=1, source_target_pairs={{0,4},{4,0},{8,12},{12,8},{16,20},{20,16},{24,28},{28,24},{1,5},{5... | collective-permute-start | bytes 3145736 | tf_op jit(solution)/shard_map/ppermute | solution.py:698
  367.4 123.9 %copy-start.25 = (f32[2048]{0:T(1024)S(1)}, f32[2048]{0:T(1024)}, u32[]{:S(2)}) copy-start(f32[2048]{0:T(1024)} %param.30) | copy-start | bytes 24580
  491.2 7.7 %copy-start.2 = (bf16[4,256,512]{2,1,0:T(8,128)(2,1)S(1)}, bf16[4,256,512]{2,1,0:T(8,128)(2,1)}, u32[]{:S(2)}) copy-start(bf16[4,256,512]{2,1,0:T(8,128)(2,1)} %copy-done.1) | copy-start | bytes 3145732
  491.3 12.1 %copy-start.11 = (bf16[4,256,2048]{2,1,0:T(8,128)(2,1)S(1)}, bf16[4,256,2048]{2,1,0:T(8,128)(2,1)}, u32[]{:S(2)}) copy-start(bf16[4,256,2048]{2,1,0:T(8,128)(2,1)} %add_convert_fusion.wide_ref) | copy-start | bytes 12582916
  500.6 3.2 collective-permute-start.2
  501.3 8.2 %collective-permute-start.1 = (bf16[256,512]{1,0:T(8,128)(2,1)S(1)}, bf16[256,512]{1,0:T(8,128)(2,1)S(1)}, u32[]{:S(2)}, u32[]{:S(2)}) collective-permute-start(bf16[256,512]{1,0:T(8,128)(2,1)S(1)} %get-tuple-element.76), channel_id=1, source_target_pairs={{0,8},{4,12},{1,9},{5,13},{2,10},{6,14},{3,11},{7,15}} | collective-permute-start | bytes 786440 | tf_op jit(solution)/shard_map/ppermute | solution.py:710
  509.6 63.4 %collective-permute-start.4 = (bf16[256,512]{1,0:T(8,128)(2,1)S(1)}, bf16[256,512]{1,0:T(8,128)(2,1)S(1)}, u32[]{:S(2)}, u32[]{:S(2)}) collective-permute-start(bf16[256,512]{1,0:T(8,128)(2,1)S(1)} %get-tuple-element.79), channel_id=1, source_target_pairs={{16,8},{20,12},{24,16},{28,20},{17,9},{21,13},{25,17},{29,21},{18,... | collective-permute-start | bytes 786440 | tf_op jit(solution)/shard_map/ppermute | solution.py:710
  510.2 62.7 %collective-permute-start.3 = (bf16[256,512]{1,0:T(8,128)(2,1)S(1)}, bf16[256,512]{1,0:T(8,128)(2,1)S(1)}, u32[]{:S(2)}, u32[]{:S(2)}) collective-permute-start(bf16[256,512]{1,0:T(8,128)(2,1)S(1)} %get-tuple-element.78), channel_id=1, source_target_pairs={{0,8},{4,12},{8,16},{12,20},{1,9},{5,13},{9,17},{13,21},{2,10},{6,... | collective-permute-start | bytes 786440 | tf_op jit(solution)/shard_map/ppermute | solution.py:710
  517.3 67.8 %copy-start.16 = (f32[256,2048]{1,0:T(8,128)S(1)}, f32[256,2048]{1,0:T(8,128)}, u32[]{:S(2)}) copy-start(f32[256,2048]{1,0:T(8,128)} %get-tuple-element.83) | copy-start | bytes 6291460
  573.9 14.2 %collective-permute-start.6 = (bf16[256,512]{1,0:T(8,128)(2,1)}, bf16[256,512]{1,0:T(8,128)(2,1)S(1)}, u32[]{:S(2)}, u32[]{:S(2)}) collective-permute-start(bf16[256,512]{1,0:T(8,128)(2,1)} %get-tuple-element.81), channel_id=1, source_target_pairs={{8,0},{12,4},{16,8},{20,12},{24,16},{28,20},{9,1},{13,5},{17,9},{2... | collective-permute-start | bytes 786440 | tf_op jit(solution)/shard_map/ppermute | solution.py:710
  575.2 12.9 %collective-permute-start.5 = (bf16[256,512]{1,0:T(8,128)(2,1)}, bf16[256,512]{1,0:T(8,128)(2,1)}, u32[]{:S(2)}, u32[]{:S(2)}) collective-permute-start(bf16[256,512]{1,0:T(8,128)(2,1)} %get-tuple-element.80), channel_id=1, source_target_pairs={{0,8},{4,12},{8,16},{12,20},{16,24},{20,28},{1,9},{5,13},{9,17},{1... | collective-permute-start | bytes 786440 | tf_op jit(solution)/shard_map/ppermute | solution.py:710
  590.2 8.0 %copy-start.20 = (f32[256,512]{1,0:T(8,128)S(1)}, f32[256,512]{1,0:T(8,128)}, u32[]{:S(2)}) copy-start(f32[256,512]{1,0:T(8,128)} %get-tuple-element.147) | copy-start | bytes 1572868
  590.2 8.8 %copy-start.22 = (f32[256,256]{1,0:T(8,128)S(1)}, f32[256,256]{1,0:T(8,128)}, u32[]{:S(2)}) copy-start(f32[256,256]{1,0:T(8,128)} %get-tuple-element.149) | copy-start | bytes 786436
  590.2 9.5 %copy-start.17 = (f32[256,2048]{1,0:T(8,128)S(1)}, f32[256,2048]{1,0:T(8,128)}, u32[]{:S(2)}) copy-start(f32[256,2048]{1,0:T(8,128)} %get-tuple-element.155) | copy-start | bytes 6291460

commit v4 on v3

--- a/solution.py
+++ b/solution.py
@@ -127,24 +127,110 @@
             target[lev] = jnp.where(which == 0, both[:rows], both[rows:]).astype(BF16)
 
 
+def hidden_kernel(tiles, x_ref, attn_ref, g_ref, wu_ref, bias_ref, vec_ref, n2_ref, act_ref, dpre_ref, sums_ref, acc):
+    step = pl.program_id(0)
+
+    @pl.when(step == 0)
+    def _():
+        acc[...] = jnp.zeros_like(acc)
+
+    rows = x_ref.shape[0]
+    values = x_ref[...].astype(F32) + attn_ref[...].astype(F32) + vec_ref[0:1, :]
+    centred = values - jnp.mean(values, axis=-1, keepdims=True)
+    scale = lax.rsqrt(jnp.mean(centred * centred, axis=-1, keepdims=True) + EPSILON)
+    n2_ref[...] = (centred * scale * vec_ref[1:2, :] + vec_ref[2:3, :]).astype(BF16)
+    tile = wu_ref.shape[1] // tiles
+    root = 0.7978845608028654
+    for j in range(tiles):
+        cols = slice(j * tile, (j + 1) * tile)
+        pre = jnp.dot(n2_ref[...], wu_ref[:, cols], preferred_element_type=F32) + bias_ref[0:1, cols]
+        square = pre * pre
+        bend = jnp.tanh(root * pre * (1.0 + 0.044715 * square))
+        half = 0.5 * (1.0 + bend)
+        act_ref[:, cols] = (pre * half).astype(BF16)
+        slope = half + (0.5 * root) * pre * (1.0 - bend * bend) * (1.0 + (3 * 0.044715) * square)
+        d_pre = (g_ref[:, cols].astype(F32) * slope).astype(BF16)
+        dpre_ref[:, cols] = d_pre
+        acc[:, cols] += jnp.sum(d_pre.astype(F32).reshape(rows // 8, 8, tile), axis=0)
+
+    @pl.when(step == pl.num_programs(0) - 1)
+    def _():
+        sums_ref[...] = jnp.sum(acc[...], axis=0, keepdims=True)
+
+
+def hidden_stage(inputs, attn_sum, d_activ, up_weight, up_bias, output_bias, gain, bias, block=256, tiles=4):
+    rows, width = inputs.shape
+    wide = up_weight.shape[1]
+    vec = jnp.pad(jnp.stack([output_bias, gain, bias]), ((0, 5), (0, 0)))
+    row = lambda cols: pl.BlockSpec((block, cols), lambda k: (k, 0))
+    fixed = lambda shape: pl.BlockSpec(shape, lambda k: (0, 0))
+    return pl.pallas_call(
+        functools.partial(hidden_kernel, tiles),
+        grid=(rows // block,),
+        out_shape=(
+            jax.ShapeDtypeStruct((rows, width), BF16),
+            jax.ShapeDtypeStruct((rows, wide), BF16),
+            jax.ShapeDtypeStruct((rows, wide), BF16),
+            jax.ShapeDtypeStruct((1, wide), F32),
+        ),
+        in_specs=[
+            row(width),
+            row(width),
+            row(wide),
+            pl.BlockSpec(up_weight.shape, lambda k: (0, 0), pipeline_mode=pl.Buffered(1)),
+            fixed((1, wide)),
+            fixed((8, width)),
+        ],
+        out_specs=(row(width), row(wide), row(wide), fixed((1, wide))),
+        scratch_shapes=[pltpu.VMEM((8, wide), F32)],
+        compiler_params=pltpu.CompilerParams(vmem_limit_bytes=60 << 20),
+        name="hidden",
+    )(inputs, attn_sum, d_activ, up_weight, up_bias.reshape(1, wide), vec)
+
+
 def hidden_back_kernel(
-    chunks, dpre_ref, wu_ref, n2_ref, activ_ref, cot_ref, far_ref, dn_ref, own_ref, other_ref, down_ref, got_ref,
-    activ_x, x_send, x_recv, part, from_core, summed, from_y, *sems,
+    chunks, dpre_ref, wu_hbm, n2_hbm, activ_hbm, cot_hbm, far_hbm, wd_hbm, dn_ref, own_out, other_out, down_out,
+    mlp_out, weight_ref, n2_ref, activ_ref, cot_ref, far_ref, own_ref, other_ref, down_ref, mlp_ref, in_sem, out_sem,
+    mlp_sem, activ_x, x_send, x_recv, part,
+    from_core, summed, from_y, *sems,
 ):
     ts = TensorSum(chunks, part, dn_ref, from_core, summed, from_y, sems)
     side = lax.rem(lax.axis_index("dp"), 2)
     x_peer = (lax.axis_index("dp") + 1 - 2 * side, lax.axis_index("tensor"))
-    greet([ts.core_peer, ts.y_peer, x_peer])
     half = activ_x.shape[1]
     mine = pl.ds(pl.multiple_of(side * half, half), half)
     theirs = pl.ds(pl.multiple_of((1 - side) * half, half), half)
-    to_x = remote(activ_ref.at[:, theirs], activ_x, x_send.at[0], x_recv.at[0], x_peer)
+    local = [
+        pltpu.make_async_copy(source, target, in_sem.at[n])
+        for n, (source, target) in enumerate(
+            [
+                (wu_hbm, weight_ref),
+                (n2_hbm, n2_ref),
+                (activ_hbm, activ_ref),
+                (cot_hbm, cot_ref),
+                (far_hbm, far_ref),
+                (wd_hbm, weight_ref),
+            ]
+        )
+    ]
+    results = [
+        pltpu.make_async_copy(source, target, out_sem.at[n])
+        for n, (source, target) in enumerate(
+            [(other_ref, other_out), (own_ref, own_out), (down_ref, down_out)]
+        )
+    ]
+    local[0].start()
+    greet([ts.core_peer, ts.y_peer, x_peer])
+    to_x = remote(activ_hbm.at[:, theirs], activ_x, x_send, x_recv, x_peer)
     to_x.start()
+    for copy in local[1:5]:
+        copy.start()
+    local[0].wait()
 
     @pl.loop(0, chunks)
     def _(k):
         at = ts.span(k)
-        part[at, :] = contract(dpre_ref[at, :], wu_ref[...], 1, 1).astype(BF16)
+        part[at, :] = contract(dpre_ref[at, :], weight_ref[...], 1, 1).astype(BF16)
         ts.first(k)
 
         @pl.when(k >= 1)
@@ -152,13 +238,15 @@
             ts.second(k - 1)
 
     ts.second(chunks - 1)
+    local[5].start()
+    local[1].wait()
     grad_rows(n2_ref, dpre_ref, other_ref, 1 - side)
-    rest = remote(
-        other_ref.at[pl.ds(0, got_ref.shape[0])], got_ref, x_send.at[1], x_recv.at[1], x_peer
-    )
-    rest.start()
+    results[0].start()
     grad_rows(n2_ref, dpre_ref, own_ref, side)
+    results[1].start()
     levels, rows = down_ref.shape[0], down_ref.shape[1]
+    local[2].wait()
+    local[3].wait()
 
     @pl.loop(0, levels)
     def _(lev):
@@ -171,6 +259,28 @@
     def _(k):
         ts.third(k)
 
+    local[5].wait()
+    tiles = 4
+    tile = mlp_ref.shape[2]
+
+    def mlp_copy(j):
+        cols = pl.ds(pl.multiple_of(j * tile, tile), tile)
+        slot = lax.rem(j, 2)
+        return pltpu.make_async_copy(mlp_ref.at[slot], mlp_out.at[:, cols], mlp_sem.at[slot])
+
+    @pl.loop(0, tiles)
+    def _(j):
+        @pl.when(j >= 2)
+        def _():
+            mlp_copy(j - 2).wait()
+
+        cols = pl.ds(pl.multiple_of(j * tile, tile), tile)
+        mlp_ref[lax.rem(j, 2)] = jnp.dot(
+            activ_ref[...], weight_ref[:, cols], preferred_element_type=F32
+        ).astype(BF16)
+        mlp_copy(j).start()
+
+    local[4].wait()
     to_x.wait_recv()
 
     @pl.loop(0, levels)
@@ -179,57 +289,86 @@
         far = contract(far_ref[:, cols], activ_x[...], 0, 0)
         down_ref[lev] = (down_ref[lev].astype(F32) + far).astype(BF16)
 
+    results[2].start()
+
     @pl.loop(ready, chunks)
     def _(k):
         ts.third(k)
 
     ts.finish(chunks)
     to_x.wait_send()
-    rest.wait()
-
-
-def hidden_back(d_pre, up_weight, normed2, activ, cotangent, far_cotangent, count, chunks=4):
+    for copy in results:
+        copy.wait()
+    for j in (tiles - 2, tiles - 1):
+        mlp_copy(j).wait()
+
+
+def hidden_back(
+    d_pre, up_weight, normed2, activ, cotangent, far_cotangent, down_weight, count, chunks=4
+):
     rows, width = d_pre.shape[0], up_weight.shape[0]
     hidden = up_weight.shape[1]
     levels = count // 2
-    half = jax.ShapeDtypeStruct((levels, width // count, hidden), BF16)
-    got = jax.ShapeDtypeStruct((levels // 4, width // count, hidden), BF16)
+    half = (levels, width // count, hidden)
+    down = (levels, width // levels, hidden // 2)
+    dma = pltpu.SemaphoreType.DMA
     hbm = pl.BlockSpec(memory_space=pl.ANY)
-    dma = pltpu.SemaphoreType.DMA
     return pl.pallas_call(
         functools.partial(hidden_back_kernel, chunks),
         out_shape=(
             jax.ShapeDtypeStruct((rows, width), BF16),
-            half,
-            half,
-            jax.ShapeDtypeStruct((levels, width // levels, hidden // 2), BF16),
-            got,
+            jax.ShapeDtypeStruct(half, BF16),
+            jax.ShapeDtypeStruct(half, BF16),
+            jax.ShapeDtypeStruct(down, BF16),
+            jax.ShapeDtypeStruct((rows, width), BF16),
         ),
-        in_specs=[VMEM] * 6,
-        out_specs=(VMEM,) * 4 + (hbm,),
-        scratch_shapes=[pltpu.VMEM((rows, hidden // 2), BF16), dma((2,)), dma((2,))]
+        in_specs=[VMEM] + [hbm] * 6,
+        out_specs=(VMEM,) + (hbm,) * 4,
+        scratch_shapes=[
+            pltpu.VMEM(up_weight.shape, BF16),
+            pltpu.VMEM((rows, width), BF16),
+            pltpu.VMEM((rows, hidden), BF16),
+            pltpu.VMEM((rows, width), BF16),
+            pltpu.VMEM((rows, width), BF16),
+            pltpu.VMEM(half, BF16),
+            pltpu.VMEM(half, BF16),
+            pltpu.VMEM(down, BF16),
+            pltpu.VMEM((2, rows, width // 4), BF16),
+            dma((6,)),
+            dma((3,)),
+            dma((2,)),
+            pltpu.VMEM((rows, hidden // 2), BF16),
+            dma,
+            dma,
+        ]
         + sum_scratch(chunks, rows, width),
         compiler_params=pltpu.CompilerParams(
             collective_id=4, has_side_effects=True, vmem_limit_bytes=62 << 20
         ),
         name="hidden_back",
-    )(d_pre, up_weight, normed2, activ, cotangent, far_cotangent)
+    )(d_pre, up_weight, normed2, activ, cotangent, far_cotangent, down_weight)
 
 
 class Chain:
-    def __init__(self, length, level, upper, lower, pair, bufs, sems):
+    def __init__(self, length, level, upper, lower, pair, bufs, sems, early=None):
         self.length, self.level = length, level
         self.peers = (upper, lower)
         self.pair = pair
         self.bufs = bufs
         self.sems = sems
+        self.early = early
+        self.skip = 0 if early is None else 1
 
     def copy(self, way, s):
+        at = s - 1 - self.skip
         inward, outward = self.bufs[2 * way], self.bufs[2 * way + 1]
         send, recv = self.sems[2 * way], self.sems[2 * way + 1]
-        return remote(
-            outward.at[s - 1], inward.at[s - 1], send.at[s - 1], recv.at[s - 1], self.peers[way]
-        )
+        return remote(outward.at[at], inward.at[at], send.at[at], recv.at[at], self.peers[way])
+
+    def arrived(self, way, s):
+        if s == 1 and self.early is not None:
+            return self.early[way][...]
+        return self.bufs[2 * way][s - 1 - self.skip]
 
     def rank(self, way):
         return self.level if way == 0 else self.length - 1 - self.level
@@ -239,16 +378,17 @@
             rank = self.rank(way)
             slot = rank + self.length - s
             slot = jnp.clip(slot if way == 0 else self.length - 1 - slot, 0, self.length - 1)
-            inward, outward = self.bufs[2 * way], self.bufs[2 * way + 1]
+            outward = self.bufs[2 * way + 1]
+            at = s - 1 - self.skip
 
             @pl.when(rank <= s - 1)
-            def _(way=way, rank=rank, slot=slot, inward=inward, outward=outward):
-                outward[s - 1] = self.pair[slot]
+            def _(way=way, rank=rank, slot=slot, outward=outward, at=at):
+                outward[at] = self.pair[slot]
                 if s > 1:
                     @pl.when(rank >= 1)
                     def _():
-                        outward[s - 1] = (
-                            self.pair[slot].astype(F32) + inward[s - 2].astype(F32)
+                        outward[at] = (
+                            self.pair[slot].astype(F32) + self.arrived(way, s - 1).astype(F32)
                         ).astype(BF16)
 
                 self.copy(way, s).start()
@@ -262,21 +402,44 @@
                 self.copy(way, s).wait_recv()
 
     def result(self, target):
-        last = self.length - 2
         target[...] = self.pair[self.level].astype(F32)
         for way in range(2):
             @pl.when(self.rank(way) >= 1)
             def _(way=way):
-                target[...] += self.bufs[2 * way][last].astype(F32)
+                target[...] += self.arrived(way, self.length - 1).astype(F32)
 
     def drain(self, last=None):
-        for s in range(1, (last or self.length - 1) + 1):
+        for s in range(1 + self.skip, (last or self.length - 1) + 1):
             for way in range(2):
                 rank = self.rank(way)
 
                 @pl.when(rank <= s - 1)
                 def _(way=way, s=s):
                     self.copy(way, s).wait_send()
+
+
+class FirstStep:
+    def __init__(self, length, level, upper, lower, sources, targets, send, recv):
+        self.length, self.level = length, level
+        self.copies = [
+            remote(sources[way], targets[way], send.at[way], recv.at[way], (upper, lower)[way])
+            for way in range(2)
+        ]
+
+    def each(self, rank, act):
+        for way in range(2):
+            mine = self.level if way == 0 else self.length - 1 - self.level
+
+            @pl.when(mine == rank)
+            def _(way=way):
+                act(self.copies[way])
+
+    def start(self):
+        self.each(0, lambda copy: copy.start())
+
+    def wait(self):
+        self.each(1, lambda copy: copy.wait_recv())
+        self.each(0, lambda copy: copy.wait_send())
 
 
 def chain_scratch(length, shape):
@@ -295,14 +458,144 @@
     return count // 2, level, upper, lower
 
 
+def middle_kernel(
+    chunk, dn_ref, x_ref, attn_ref, cot_ref, vec_ref, part_ref, wo_hbm, ctx_hbm, down_hbm, own_hbm, other_hbm,
+    dm_ref, dctx_ref, mlp_ref, out_own, out_other, sums_ref, edge_ref, far_up, far_down, wo_ref, ctx_ref,
+    edge_own, edge_got, local_sem, x_send, x_recv, z_send, z_recv, acc,
+):
+    dp = lax.axis_index("dp")
+    lane = lax.axis_index("tensor")
+    side = lax.rem(dp, 2)
+    x_peer = (dp + 1 - 2 * side, lane)
+    length, level, upper, lower = chain_peers()
+    edge = jnp.where(level < length // 2, length - 1, 0)
+    local = [
+        pltpu.make_async_copy(source, target, local_sem.at[n])
+        for n, (source, target) in enumerate(
+            [
+                (wo_hbm, wo_ref),
+                (ctx_hbm, ctx_ref),
+                (own_hbm.at[edge], edge_own),
+            ]
+        )
+    ]
+    for copy in local:
+        copy.start()
+    greet([x_peer, upper, lower])
+    to_x = remote(other_hbm.at[edge], edge_got, x_send, x_recv, x_peer)
+    to_x.start()
+    first_step = FirstStep(
+        length, level, upper, lower, (down_hbm.at[length - 1], down_hbm.at[0]), (far_up, far_down), z_send,
+        z_recv,
+    )
+    first_step.start()
+    rows, width = x_ref.shape
+    acc[...] = jnp.zeros_like(acc)
+    share = 1.0 / lax.axis_size("tensor")
+
+    def fold(values):
+        return jnp.sum(values.reshape(chunk // 8, 8, width), axis=0)
+
+    def norm_rows(k):
+        at = pl.ds(pl.multiple_of(k * chunk, chunk), chunk)
+        values = x_ref[at, :].astype(F32) + attn_ref[at, :].astype(F32) + vec_ref[0:1, :]
+        base = share * (values + vec_ref[2:3, :])
+        mlp_ref[at, :] = (part_ref[at, :].astype(F32) + base).astype(BF16)
+        centred = values - jnp.mean(values, axis=-1, keepdims=True)
+        scale = lax.rsqrt(jnp.mean(centred * centred, axis=-1, keepdims=True) + EPSILON)
+        hat = centred * scale
+        grad = dn_ref[at, :].astype(F32)
+        acc[0] += fold(grad * hat)
+        acc[1] += fold(grad)
+        scaled = grad * vec_ref[1:2, :]
+        first = jnp.mean(scaled, axis=-1, keepdims=True)
+        second = jnp.mean(scaled * hat, axis=-1, keepdims=True)
+        cot = cot_ref[at, :].astype(F32)
+        d_middle = cot + scale * (scaled - first - hat * second)
+        acc[2] += fold(d_middle)
+        acc[3] += fold(cot)
+        dm_ref[at, :] = d_middle.astype(BF16)
+
+    @pl.loop(0, rows // chunk)
+    def _(k):
+        norm_rows(k)
+
+    for n in range(4):
+        sums_ref[n : n + 1, :] = jnp.sum(acc[n], axis=0, keepdims=True)
+    sums_ref[4:8, :] = jnp.zeros((4, width), F32)
+    local[0].wait()
+
+    @pl.loop(0, 4)
+    def _(k):
+        at = pl.ds(pl.multiple_of(k * (rows // 4), rows // 4), rows // 4)
+        dctx_ref[at, :] = contract(dm_ref[at, :], wo_ref[...], 1, 1).astype(BF16)
+
+    local[1].wait()
+    grad_rows(dm_ref, ctx_ref, out_other, 1 - side)
+    grad_rows(dm_ref, ctx_ref, out_own, side)
+    local[2].wait()
+    to_x.wait()
+    edge_ref[...] = (edge_own[...].astype(F32) + edge_got[...].astype(F32)).astype(BF16)
+    first_step.wait()
+
+
+def middle_stage(
+    d_normed2, inputs, attn_sum, cotangent, output_bias, gain, down_bias, part, output_weight, context, down,
+    up_own, up_other, count, chunk=128,
+):
+    rows, width = inputs.shape
+    heads = context.shape[1]
+    vec = jnp.stack([output_bias, gain, down_bias])
+    vec = jnp.pad(vec, ((0, 5), (0, 0)))
+    half = jax.ShapeDtypeStruct((count // 2, width // count, heads), BF16)
+    hbm = pl.BlockSpec(memory_space=pl.ANY)
+    dma = pltpu.SemaphoreType.DMA
+    low = lambda shape: jax.ShapeDtypeStruct(shape, BF16)
+    edge = pltpu.VMEM(up_own.shape[1:], BF16)
+    return pl.pallas_call(
+        functools.partial(middle_kernel, chunk),
+        out_shape=(
+            low((rows, width)),
+            low((rows, heads)),
+            low((rows, width)),
+            half,
+            half,
+            jax.ShapeDtypeStruct((8, width), F32),
+            low(up_own.shape[1:]),
+            low(down.shape[1:]),
+            low(down.shape[1:]),
+        ),
+        in_specs=[VMEM] * 6 + [hbm] * 5,
+        out_specs=(VMEM,) * 7 + (hbm,) * 2,
+        scratch_shapes=[
+            pltpu.VMEM(output_weight.shape, BF16),
+            pltpu.VMEM(context.shape, BF16),
+            edge,
+            edge,
+            dma((3,)),
+            dma,
+            dma,
+            dma((2,)),
+            dma((2,)),
+            pltpu.VMEM((4, 8, width), F32),
+        ],
+        compiler_params=pltpu.CompilerParams(
+            collective_id=7, has_side_effects=True, vmem_limit_bytes=60 << 20
+        ),
+        name="middle",
+    )(
+        d_normed2, inputs, attn_sum, cotangent, vec, part, output_weight, context, down, up_own, up_other,
+    )
+
+
 def query_back_kernel(
-    chunks, steps, dq_ref, wq_ref, n1_ref, dkv_ref, wide_ref, down_ref, dn_ref, grad_ref, tot_ref,
-    far_up, far_down, down_out, d_send, d_recv, down_low, down_got,
-    part, from_core, summed, from_y, kv_core, kv_sum, kv_x, kv_pair, kv_z, kv_up, kv_y, kv_sems, own_ref,
-    other_ref, got_ref, q_send, q_recv, *rest,
+    chunks, steps, dq_ref, wq_ref, n1_ref, dkv_ref, wide_ref, wide_up, wide_down, proj_ref, proj_x, dn_ref,
+    grad_ref, proj_grad, tot_ref, far_up, far_down, kv_local, part, from_core, summed, from_y, kv_core, kv_sum, kv_x,
+    kv_pair, kv_z, kv_up, kv_y, kv_sems, own_ref, other_ref, got_ref, q_send, q_recv, proj_pair, *rest,
 ):
     chain_bufs, chain_sems, sems = rest[:4], rest[4:8], rest[8:14]
-    wide_bufs, wide_sems = rest[14:18], rest[18:]
+    wide_bufs, wide_sems = rest[14:18], rest[18:22]
+    proj_bufs, proj_sems = rest[22:26], rest[26:]
     ts = TensorSum(chunks, part, dn_ref, from_core, summed, from_y, sems)
     block = lax.axis_index("dp")
     lane = lax.axis_index("tensor")
@@ -319,7 +612,9 @@
     else:
         greet([ts.core_peer, ts.y_peer, x_peer, upper, lower, chain_upper, chain_lower])
     chain = Chain(length, chain_level, chain_upper, chain_lower, own_ref, chain_bufs, chain_sems)
-    wide = Chain(length, chain_level, chain_upper, chain_lower, wide_ref, wide_bufs, wide_sems)
+    early = (wide_up, wide_down)
+    wide = Chain(length, chain_level, chain_upper, chain_lower, wide_ref, wide_bufs, wide_sems, early)
+    proj = Chain(length, chain_level, chain_upper, chain_lower, proj_pair, proj_bufs, proj_sems)
     core = lax.rem(lane, 2)
     seq_rows = tot_ref.shape[0]
     half = seq_rows // 2
@@ -335,9 +630,23 @@
         )
         for lev in range(levels)
     ]
-    for copy in to_core:
+    keep = [
+        pltpu.make_async_copy(dkv_ref.at[pl.ds(2 * lev, 2), mine], kv_sum.at[lev], kv_local.at[lev])
+        for lev in range(levels)
+    ]
+    for copy in to_core + keep:
         copy.start()
+    proj_pair[...] = (proj_ref[...].astype(F32) + proj_x[...].astype(F32)).astype(BF16)
+    proj.start(1)
+    wide.start(2)
     grad_levels, rows = own_ref.shape[0], own_ref.shape[1]
+    for lev in range(levels):
+        to_core[lev].wait_recv()
+        keep[lev].wait()
+        kv_sum[lev] = (kv_sum[lev].astype(F32) + kv_core[lev].astype(F32)).astype(BF16)
+
+    to_x = kv_copy(kv_sum.at[:, 1 - side], kv_x, 1, x_peer)
+    to_x.start()
 
     @pl.loop(0, chunks)
     def _(k):
@@ -350,14 +659,6 @@
             ts.second(k - 1)
 
     ts.second(chunks - 1)
-    for lev in range(levels):
-        to_core[lev].wait_recv()
-        total = dkv_ref[pl.ds(2 * lev, 2), mine].astype(F32) + kv_core[lev].astype(F32)
-        kv_sum[lev] = total.astype(BF16)
-
-    to_x = kv_copy(kv_sum.at[:, 1 - side], kv_x, 1, x_peer)
-    to_x.start()
-    wide.start(1)
 
     def grad(target, which):
         grad_rows(n1_ref, dq_ref, target, which)
@@ -365,14 +666,11 @@
     grad(other_ref, 1 - side)
     q_to_x = remote(other_ref, got_ref, q_send, q_recv, x_peer)
     grad(own_ref, side)
-    half_rows, half_cols = down_low.shape
-    down_mine = pl.ds(pl.multiple_of(side * half_rows, half_rows), half_rows)
-    down_theirs = pl.ds(pl.multiple_of((1 - side) * half_rows, half_rows), half_rows)
-    down_low[...] = down_ref[down_theirs].astype(BF16)
+    for s in range(1, length - 1):
+        proj.arrive(s)
+        proj.start(s + 1)
     to_x.wait_recv()
     q_to_x.start()
-    d_to_x = remote(down_low, down_got, d_send, d_recv, x_peer)
-    d_to_x.start()
 
     @pl.loop(0, levels)
     def _(lev):
@@ -411,7 +709,7 @@
 
     to_y = kv_copy(kv_up.at[levels - 1], kv_y, 1 + levels, ts.y_peer)
     to_y.start()
-    for s in range(1, steps):
+    for s in range(2, steps):
         wide.arrive(s)
         wide.start(s + 1)
     q_to_x.wait_recv()
@@ -441,15 +739,13 @@
         ts.third(k)
 
     chain.result(grad_ref)
-    d_to_x.wait()
-    first = pl.ds(pl.multiple_of(side * half_cols, half_cols), half_cols)
-    second = pl.ds(pl.multiple_of((1 - side) * half_cols, half_cols), half_cols)
-    down_out[:, first] = down_ref[down_mine]
-    down_out[:, second] = down_got[...].astype(F32)
+    proj.arrive(length - 1)
+    proj.result(proj_grad)
     wide.arrive(steps)
-    far_up[...] = wide.bufs[0][steps - 1]
-    far_down[...] = wide.bufs[2][steps - 1]
+    far_up[...] = wide.arrived(0, steps)
+    far_down[...] = wide.arrived(1, steps)
     chain.drain()
+    proj.drain()
     wide.drain(steps)
     q_to_x.wait_send()
     back.wait()
@@ -467,7 +763,9 @@
     ts.finish(chunks)
 
 
-def query_back(d_queries, query_weight, normed1, parts, wide, down, count, chunks=4):
+def query_back(
+    d_queries, query_weight, normed1, parts, wide, wide_up, wide_down, proj, proj_x, count, chunks=4
+):
     rows, width = d_queries.shape[0], query_weight.shape[0]
     kv_width = parts.shape[2]
     steps = count // 2 - 2
@@ -480,18 +778,15 @@
         out_shape=(
             jax.ShapeDtypeStruct((rows, width), BF16),
             jax.ShapeDtypeStruct(shape, F32),
+            jax.ShapeDtypeStruct(proj.shape[1:], F32),
             jax.ShapeDtypeStruct((rows, kv_width), BF16),
             jax.ShapeDtypeStruct(wide.shape[1:], BF16),
             jax.ShapeDtypeStruct(wide.shape[1:], BF16),
-            jax.ShapeDtypeStruct((down.shape[0] // 2, 2 * down.shape[1]), F32),
         ),
-        in_specs=[VMEM] * 6,
+        in_specs=[VMEM] * 3 + [pl.BlockSpec(memory_space=pl.ANY)] + [VMEM] * 5,
         out_specs=(VMEM,) * 6,
         scratch_shapes=[
-            pltpu.SemaphoreType.DMA,
-            pltpu.SemaphoreType.DMA,
-            pltpu.VMEM((down.shape[0] // 2, down.shape[1]), BF16),
-            pltpu.VMEM((down.shape[0] // 2, down.shape[1]), BF16),
+            pltpu.SemaphoreType.DMA((levels,)),
         ]
         + sum_scratch(chunks, rows, width)[:4]
         + [
@@ -508,21 +803,83 @@
             half,
             pltpu.SemaphoreType.DMA,
             pltpu.SemaphoreType.DMA,
+            pltpu.VMEM(proj.shape, BF16),
         ]
         + chain_scratch(count // 2, shape)
         + [pltpu.SemaphoreType.DMA((chunks,))] * 6
-        + chain_scratch(steps + 1, wide.shape[1:]),
+        + chain_scratch(steps, wide.shape[1:])
+        + chain_scratch(count // 2, proj.shape[1:]),
         compiler_params=pltpu.CompilerParams(
             collective_id=5, has_side_effects=True, vmem_limit_bytes=63 << 20
         ),
         name="query_back",
-    )(d_queries, query_weight, normed1, parts, wide, down)
+    )(d_queries, query_weight, normed1, parts, wide, wide_up, wide_down, proj, proj_x)
+
+
+def norm_back_kernel(dkv_ref, wkv_ref, dn_ref, x_ref, dm_ref, gain_ref, grad_x, sums_ref, acc, acc_kv):
+    k = pl.program_id(0)
+
+    @pl.when(k == 0)
+    def _():
+        acc[...] = jnp.zeros_like(acc)
+        acc_kv[...] = jnp.zeros_like(acc_kv)
+
+    chunk, width = x_ref.shape
+
+    def fold(values):
+        return jnp.sum(values.reshape(chunk // 8, 8, values.shape[1]), axis=0)
+
+    values = x_ref[...].astype(F32)
+    centred = values - jnp.mean(values, axis=-1, keepdims=True)
+    scale = lax.rsqrt(jnp.mean(centred * centred, axis=-1, keepdims=True) + EPSILON)
+    hat = centred * scale
+    grad = dn_ref[...].astype(F32) + contract(dkv_ref[...], wkv_ref[...], 1, 1)
+    acc[0] += fold(grad * hat)
+    acc[1] += fold(grad)
+    acc_kv[...] += fold(dkv_ref[...].astype(F32))
+    scaled = grad * gain_ref[...]
+    first = jnp.mean(scaled, axis=-1, keepdims=True)
+    second = jnp.mean(scaled * hat, axis=-1, keepdims=True)
+    grad_x[...] = dm_ref[...].astype(F32) + scale * (scaled - first - hat * second)
+
+    @pl.when(k == pl.num_programs(0) - 1)
+    def _():
+        sums_ref[...] = jnp.zeros_like(sums_ref)
+        sums_ref[0:1, :] = jnp.sum(acc[0], axis=0, keepdims=True)
+        sums_ref[1:2, :] = jnp.sum(acc[1], axis=0, keepdims=True)
+        sums_ref[2:3, 0 : acc_kv.shape[1]] = jnp.sum(acc_kv[...], axis=0, keepdims=True)
+
+
+def norm_back(d_keyval, keyval_weight, d_normed1, inputs, d_middle, gain, chunk=128):
+    rows, width = inputs.shape
+    kv_width = d_keyval.shape[1]
+    row = lambda cols: pl.BlockSpec((chunk, cols), lambda k: (k, 0))
+    fixed = lambda shape: pl.BlockSpec(shape, lambda k: (0, 0))
+    return pl.pallas_call(
+        norm_back_kernel,
+        grid=(rows // chunk,),
+        out_shape=(
+            jax.ShapeDtypeStruct((rows, width), F32),
+            jax.ShapeDtypeStruct((8, width), F32),
+        ),
+        in_specs=[
+            row(kv_width),
+            fixed((width, kv_width)),
+            row(width),
+            row(width),
+            row(width),
+            fixed((1, width)),
+        ],
+        out_specs=(row(width), fixed((8, width))),
+        scratch_shapes=[pltpu.VMEM((2, 8, width), F32), pltpu.VMEM((8, kv_width), F32)],
+        compiler_params=pltpu.CompilerParams(vmem_limit_bytes=62 << 20),
+        name="norm_back",
+    )(d_keyval, keyval_weight, d_normed1, inputs, d_middle, gain.reshape(1, width))
 
 
 def finish_kernel(
-    chunk, n1_ref, dkv_ref, wkv_ref, dn_ref, x_ref, dm_ref, gain_ref, vec_in, ends_ref, far_up, far_down,
-    grad_x, grad_ref, vec_ref, up_ref, up_out, up_in, up_send, up_recv, own_ref, other_ref, got_ref,
-    x_send, x_recv, own_vec, low_vec, slots, send, recv, acc, *chain_refs,
+    n1_ref, dkv_ref, vec_in, wide_ref, far_up, far_down, down_ref, grad_ref, vec_ref, up_ref, down_out, ends_ref,
+    local_sem, d_send, d_recv, down_low, down_got, up_out, up_in, up_send, up_recv, own_ref, other_ref, got_ref, x_send, x_recv, own_vec, low_vec, slots, send, recv, *chain_refs,
 ):
     block = lax.axis_index("dp")
     lane = lax.axis_index("tensor")
@@ -531,8 +888,19 @@
     pairs = count // 2
     others = [(lax.rem(block + 2 * k, count), lane) for k in range(1, pairs)]
     x_peer = (block + 1 - 2 * side, lane)
+    length, level, upper, lower = chain_peers()
+    local = [
+        pltpu.make_async_copy(
+            wide_ref.at[jnp.clip(level + k, 0, length - 1)], ends_ref.at[n], local_sem.at[n]
+        )
+        for n, k in enumerate((0, 1, -1))
+    ]
+    for copy in local:
+        copy.start()
     greet([x_peer] + others)
-    length, level, upper, lower = chain_peers()
+    low_vec[0] = vec_in[...].astype(BF16)
+    to_pair = remote(low_vec.at[0], slots.at[0], send.at[0], recv.at[0], x_peer)
+    to_pair.start()
 
     def last(way):
         return remote(
@@ -540,9 +908,8 @@
         )
 
     ranks = (level, length - 1 - level)
-    grad_rows(n1_ref, dkv_ref, other_ref, 1 - side)
-    to_x = remote(other_ref, got_ref, x_send, x_recv, x_peer)
-    to_x.start()
+    for copy in local:
+        copy.wait()
     for way, far in enumerate((far_up, far_down)):
         @pl.when(ranks[way] < length - 1)
         def _(way=way, far=far):
@@ -554,64 +921,38 @@
 
             last(way).start()
 
-    grad_rows(n1_ref, dkv_ref, own_ref, side)
-    rows, width = x_ref.shape
-    acc[...] = jnp.zeros_like(acc)
-
-    def norm_back(k):
-        at = pl.ds(pl.multiple_of(k * chunk, chunk), chunk)
-        values = x_ref[at, :].astype(F32)
-        centred = values - jnp.mean(values, axis=-1, keepdims=True)
-        scale = lax.rsqrt(jnp.mean(centred * centred, axis=-1, keepdims=True) + EPSILON)
-        hat = centred * scale
-        grad = dn_ref[at, :].astype(F32) + contract(dkv_ref[at, :], wkv_ref[...], 1, 1)
-        acc[0] += jnp.sum((grad * hat).reshape(chunk // 8, 8, width), axis=0)
-        acc[1] += jnp.sum(grad.reshape(chunk // 8, 8, width), axis=0)
-        scaled = grad * gain_ref[...]
-        first = jnp.mean(scaled, axis=-1, keepdims=True)
-        second = jnp.mean(scaled * hat, axis=-1, keepdims=True)
-        grad_x[at, :] = dm_ref[at, :].astype(F32) + scale * (scaled - first - hat * second)
-
-    chain = Chain(length, level, upper, lower, own_ref, chain_refs[:4], chain_refs[4:8])
-    chunks = rows // chunk
-    half = chunks // 2
-
-    @pl.loop(0, half)
-    def _(k):
-        norm_back(k)
-
-    to_x.wait_recv()
-    own_ref[...] = (own_ref[...].astype(F32) + got_ref[...].astype(F32)).astype(BF16)
-    chain.start(1)
-
-    @pl.loop(half, chunks)
-    def _(k):
-        norm_back(k)
-
-    own_vec[...] = vec_in[...]
-    own_vec[0:1, :] = jnp.sum(acc[0], axis=0, keepdims=True)
-    own_vec[1:2, :] = jnp.sum(acc[1], axis=0, keepdims=True)
-    head = dkv_ref.shape[1] // 2
-    own_vec[2:3, 0:head] = jnp.sum(dkv_ref[:, head:].astype(F32), axis=0, keepdims=True)
-    low_vec[0] = own_vec[...].astype(BF16)
-    to_pair = remote(low_vec.at[0], slots.at[0], send.at[0], recv.at[0], x_peer)
-    to_pair.start()
-    chain.arrive(1)
-    if length > 2:
-        chain.start(2)
+    grad_rows(n1_ref, dkv_ref, other_ref, 1 - side)
+    to_x = remote(other_ref, got_ref, x_send, x_recv, x_peer)
+    to_x.start()
+    half_rows, half_cols = down_low.shape
+    down_mine = pl.ds(pl.multiple_of(side * half_rows, half_rows), half_rows)
+    down_theirs = pl.ds(pl.multiple_of((1 - side) * half_rows, half_rows), half_rows)
+    down_low[...] = down_ref[down_theirs].astype(BF16)
+    d_to_x = remote(down_low, down_got, d_send, d_recv, x_peer)
     to_pair.wait()
-    own_vec[...] += slots[0].astype(F32)
+    own_vec[...] = vec_in[...] + slots[0].astype(F32)
     low_vec[1] = own_vec[...].astype(BF16)
     copies = []
     for k in range(1, pairs):
         copy = remote(low_vec.at[1], slots.at[k], send.at[k], recv.at[k], others[k - 1])
         copy.start()
         copies.append(copy)
-    for s in range(2, length):
+    grad_rows(n1_ref, dkv_ref, own_ref, side)
+    chain = Chain(length, level, upper, lower, own_ref, chain_refs[:4], chain_refs[4:8])
+    to_x.wait_recv()
+    own_ref[...] = (own_ref[...].astype(F32) + got_ref[...].astype(F32)).astype(BF16)
+    chain.start(1)
+    d_to_x.start()
+    for s in range(1, length):
         chain.arrive(s)
         if s + 1 < length:
             chain.start(s + 1)
     chain.result(grad_ref)
+    d_to_x.wait()
+    first = pl.ds(pl.multiple_of(side * half_cols, half_cols), half_cols)
+    second = pl.ds(pl.multiple_of((1 - side) * half_cols, half_cols), half_cols)
+    down_out[:, first] = down_ref[down_mine]
+    down_out[:, second] = down_got[...].astype(F32)
     total = own_vec[...]
     for k in range(1, pairs):
         copies[k - 1].wait()
@@ -632,136 +973,50 @@
     to_x.wait_send()
 
 
-def finish(
-    normed1, d_keyval, keyval_weight, d_normed1, inputs, d_middle, gain, values, ends, far_up, far_down, count,
-    chunk=128,
-):
-    rows, width = inputs.shape
-    flat = jnp.concatenate(values)
+def finish(normed1, d_keyval, rows_of_vectors, vectors, wide, far_up, far_down, down, count):
+    width = normed1.shape[1]
+    flat = jnp.concatenate(vectors)
     lines = -(-flat.shape[0] // width)
-    height = -(-(3 + lines) // 8) * 8
-    packed = jnp.pad(flat, (3 * width, (height - 3) * width - flat.shape[0])).reshape(height, width)
+    flat = jnp.pad(flat, (0, lines * width - flat.shape[0])).reshape(lines, width)
+    packed = jnp.concatenate(rows_of_vectors + [flat], axis=0)
+    height = -(-packed.shape[0] // 8) * 8
+    packed = jnp.pad(packed, ((0, height - packed.shape[0]), (0, 0)))
     shape = (width // count, d_keyval.shape[1])
     half = pltpu.VMEM((count // 2,) + shape, BF16)
     dma = pltpu.SemaphoreType.DMA
     two = pltpu.VMEM((2,) + far_up.shape, BF16)
-    grad_x, grad, total, wide = pl.pallas_call(
-        functools.partial(finish_kernel, chunk),
+    return pl.pallas_call(
+        finish_kernel,
         out_shape=(
-            jax.ShapeDtypeStruct((rows, width), F32),
             jax.ShapeDtypeStruct(shape, F32),
             jax.ShapeDtypeStruct((height, width), F32),
             jax.ShapeDtypeStruct(far_up.shape, F32),
+            jax.ShapeDtypeStruct((down.shape[0] // 2, 2 * down.shape[1]), F32),
         ),
-        in_specs=[VMEM] * 11,
+        in_specs=[VMEM] * 3 + [pl.BlockSpec(memory_space=pl.ANY)] + [VMEM] * 3,
         out_specs=(VMEM,) * 4,
-        scratch_shapes=[two, two, dma((2,)), dma((2,)), half, half, half, dma, dma]
+        scratch_shapes=[
+            pltpu.VMEM((3,) + far_up.shape, BF16),
+            dma((3,)),
+            dma,
+            dma,
+            pltpu.VMEM((down.shape[0] // 2, down.shape[1]), BF16),
+            pltpu.VMEM((down.shape[0] // 2, down.shape[1]), BF16),
+        ]
+        + [two, two, dma((2,)), dma((2,)), half, half, half, dma, dma]
         + [
             pltpu.VMEM((height, width), F32),
             pltpu.VMEM((2, height, width), BF16),
             pltpu.VMEM((count // 2, height, width), BF16),
             dma((count // 2,)),
             dma((count // 2,)),
-            pltpu.VMEM((2, 8, width), F32),
         ]
         + chain_scratch(count // 2, shape),
         compiler_params=pltpu.CompilerParams(
-            collective_id=2, has_side_effects=True, vmem_limit_bytes=56 << 20
+            collective_id=2, has_side_effects=True, vmem_limit_bytes=62 << 20
         ),
         name="finish",
-    )(
-        normed1, d_keyval, keyval_weight, d_normed1, inputs, d_middle, gain.reshape(1, width), packed, ends,
-        far_up, far_down,
-    )
-    flat = total[3:].reshape(-1)
-    pieces = []
-    start = 0
-    for value in values:
-        pieces.append(flat[start : start + value.shape[0]])
-        start += value.shape[0]
-    head = d_keyval.shape[1] // 2
-    return grad_x, grad, total[0], total[1], total[2, :head], pieces, wide
-
-
-def together(*values):
-    return lax.optimization_barrier(values)
-
-
-class ScatterSum:
-    def __init__(self, own, other, arrived=None):
-        self.count = lax.axis_size("dp")
-        self.length = self.count // 2
-        self.level = lax.axis_index("dp") // 2
-        self.own = own
-        if arrived is not None:
-            other = other[arrived.shape[0] :]
-        got = lax.ppermute(other, "dp", [(p, p ^ 1) for p in range(self.count)])
-        if arrived is not None:
-            got = jnp.concatenate([arrived, got], axis=0)
-        self.flying = (got,)
-        self.s = 0
-
-    def shifted(self, value, sources, step):
-        pairs = [
-            (2 * source + side, 2 * (source + step) + side)
-            for source in sources
-            for side in range(2)
-        ]
-        return lax.ppermute(value, "dp", pairs)
-
-    def slot(self, index):
-        index = jnp.clip(index, 0, self.length - 1)
-        return lax.dynamic_index_in_dim(self.total, index, 0, keepdims=False)
-
-    def step(self, *values):
-        length, level = self.length, self.level
-        self.s += 1
-        s = self.s
-        if s == 1:
-            self.total = (self.own.astype(F32) + self.flying[0].astype(F32)).astype(BF16)
-            up, down = self.slot(level + length - 1), self.slot(level - length + 1)
-        else:
-            up, down = self.flying
-            up = self.slot(level + length - s).astype(F32) + up.astype(F32)
-            if s == length:
-                self.result = up + down.astype(F32)
-                return values
-            down = self.slot(level - length + s).astype(F32) + down.astype(F32)
-            up, down = up.astype(BF16), down.astype(BF16)
-        up, down, *values = together(up, down, *values)
-        self.flying = (
-            self.shifted(up, range(0, s), 1),
-            self.shifted(down, range(length - s, length), -1),
-        )
-        return values
-
-    def finish(self):
-        while self.s < self.length:
-            self.step()
-        return self.result
-
-
-def weight_grad_kernel(left_ref, right_ref, own_ref, other_ref):
-    side = lax.rem(lax.axis_index("dp"), 2)
-    grad_rows(left_ref, right_ref, other_ref, 1 - side)
-    grad_rows(left_ref, right_ref, own_ref, side)
-
-
-def weight_grad(left, right, count):
-    half = jax.ShapeDtypeStruct((count // 2, left.shape[1] // count, right.shape[1]), BF16)
-    return pl.pallas_call(
-        weight_grad_kernel,
-        out_shape=(half, half),
-        in_specs=[VMEM] * 2,
-        out_specs=(VMEM,) * 2,
-        compiler_params=pltpu.CompilerParams(vmem_limit_bytes=40 << 20),
-        cost_estimate=pl.CostEstimate(
-            flops=2 * left.shape[0] * left.shape[1] * right.shape[1],
-            bytes_accessed=16 << 20,
-            transcendentals=0,
-        ),
-        name="weight_grad",
-    )(left, right)
+    )(normed1, d_keyval, packed, wide, far_up, far_down, down)
 
 
 def front_kernel(
@@ -1052,8 +1307,9 @@
 
 
 def attend_back_kernel(
-    block, chunks, q_ref, kv_ref, do_ref, ctx_ref, lse_ref, pair_ref, mlp_ref, sent_ref, dq_ref, dkv_ref,
-    grad_ref, out_ref, got_ref, dq_acc, dkv_acc, delta, x_send, x_recv, from_core, summed, from_y, *rest,
+    block, chunks, q_ref, kv_ref, do_ref, ctx_ref, lse_ref, pair_ref, far_up, far_down, mlp_ref, sent_ref,
+    edge_ref, proj_ref, dq_ref, dkv_ref, grad_ref, out_ref, got_ref, wide_up, wide_down, proj_got, dq_acc, dkv_acc,
+    delta, x_send, x_recv, z_send, z_recv, from_core, summed, from_y, *rest,
 ):
     sems, chain_refs = rest[:6], rest[6:]
     rows = q_ref.shape[0]
@@ -1064,23 +1320,28 @@
     x_peer = (lax.axis_index("dp") + 1 - 2 * side, lax.axis_index("tensor"))
     ts = TensorSum(chunks, mlp_ref, out_ref, from_core, summed, from_y, sems)
     length, level, upper, lower = chain_peers()
-    chain = Chain(length, level, upper, lower, pair_ref, chain_refs[:4], chain_refs[4:])
+    early = (far_up, far_down)
+    chain = Chain(length, level, upper, lower, pair_ref, chain_refs[:4], chain_refs[4:], early)
     greet([ts.core_peer, ts.y_peer, x_peer, upper, lower])
-    left = got_ref.shape[0]
-    to_x = remote(
-        sent_ref.at[pl.ds(sent_ref.shape[0] - left, left)], got_ref, x_send, x_recv, x_peer
-    )
+    left = pl.ds(jnp.where(level < length // 2, 0, 1), length - 1)
+    proj_to_x = remote(proj_ref, proj_got, x_send.at[1], x_recv.at[1], x_peer)
+    proj_to_x.start()
+    to_x = remote(sent_ref.at[left], got_ref.at[left], x_send.at[0], x_recv.at[0], x_peer)
     to_x.start()
 
     @pl.loop(0, chunks)
     def _(k):
         ts.first(k)
 
-    chain.start(1)
+    chain.start(2)
+    wide_step = FirstStep(
+        length, level, upper, lower, (edge_ref, edge_ref), (wide_up, wide_down), z_send, z_recv
+    )
+    wide_step.start()
     levels = SPAN // 2
     parts = 2 * rows // block
-    per_slot = -(-(length - 1) // (levels - 1))
-    done = 0
+    per_slot = -(-(length - 2) // (levels - 1))
+    done = 1
     for target in range(levels):
         dkv_acc[...] = jnp.zeros_like(dkv_acc)
         for i in range(rows // block):
@@ -1147,8 +1408,8 @@
                     chain.arrive(done)
                     if done < length - 1:
                         chain.start(done + 1)
-            if done == length - 1:
-                chain.result(grad_ref)
+                    else:
+                        chain.result(grad_ref)
         if target == levels - 2:
             @pl.loop(0, chunks)
             def _(k):
@@ -1161,41 +1422,53 @@
                 (dq_acc[i, h] * head**-0.5).T.astype(BF16)
             )
     chain.drain()
+    wide_step.wait()
     ts.finish(chunks)
     to_x.wait()
-
-
-def attend_back(queries, keyval, d_context, context, lse, pair, mlp_part, sent, block=512, chunks=4):
+    proj_to_x.wait()
+
+
+def attend_back(
+    queries, keyval, d_context, context, lse, pair, far_up, far_down, mlp_part, sent, edge, proj, block=512, chunks=4
+):
     rows, width = queries.shape
     head = keyval.shape[1] // 2
     heads = width // head
     hbm = pl.BlockSpec(memory_space=pl.ANY)
     dma = pltpu.SemaphoreType.DMA
+    low = lambda shape: jax.ShapeDtypeStruct(shape, BF16)
     return pl.pallas_call(
         functools.partial(attend_back_kernel, block, chunks),
         out_shape=(
-            jax.ShapeDtypeStruct((rows, width), BF16),
-            jax.ShapeDtypeStruct((SPAN, rows, 2 * head), BF16),
+            low((rows, width)),
+            low((SPAN, rows, 2 * head)),
             jax.ShapeDtypeStruct(pair.shape[1:], F32),
-            jax.ShapeDtypeStruct(mlp_part.shape, BF16),
-            jax.ShapeDtypeStruct((sent.shape[0] * 3 // 4,) + sent.shape[1:], BF16),
+            low(mlp_part.shape),
+            low(sent.shape),
+            low(edge.shape),
+            low(edge.shape),
+            low(proj.shape),
         ),
-        in_specs=[VMEM] * 7 + [hbm],
-        out_specs=(VMEM,) * 4 + (hbm,),
+        in_specs=[VMEM] * 9 + [hbm] * 3,
+        out_specs=(VMEM,) * 4 + (hbm,) * 4,
         scratch_shapes=[
             pltpu.VMEM((rows // block, heads, head, block), F32),
             pltpu.VMEM((2 * rows, 2 * head), F32),
             pltpu.VMEM((heads, rows), F32),
-            dma,
-            dma,
+            dma((2,)),
+            dma((2,)),
+            dma((2,)),
+            dma((2,)),
         ]
         + sum_scratch(chunks, *mlp_part.shape)[1:]
-        + chain_scratch(*pair.shape[:1], pair.shape[1:]),
+        + chain_scratch(pair.shape[0] - 1, pair.shape[1:]),
         compiler_params=pltpu.CompilerParams(
             collective_id=6, has_side_effects=True, vmem_limit_bytes=63 << 20
         ),
         name="attend_back",
-    )(queries, keyval, d_context, context, lse, pair, mlp_part, sent)
+    )(
+        queries, keyval, d_context, context, lse, pair, far_up, far_down, mlp_part, sent, edge, proj
+    )
 
 
 def layer_norm(values, norm_gain, norm_bias):
@@ -1203,10 +1476,6 @@
     centred = values - average
     variance = jnp.mean(centred * centred, axis=-1, keepdims=True)
     return centred * lax.rsqrt(variance + EPSILON) * norm_gain + norm_bias
-
-
-def gelu_tanh(values):
-    return jax.nn.gelu(values, approximate=True)
 
 
 def per_device(
@@ -1240,76 +1509,94 @@
         queries, keyval, cotangent, output_weight, down_weight
     )
     keyval_all = keyval_all.reshape(-1, keyval.shape[1])
-    middle = x_full + attn_sum.astype(F32) + output_bias
-    normed2_full, second_pull = jax.vjp(layer_norm, middle, second_gain, second_bias)
-    normed2 = normed2_full.astype(BF16)
-    pre_act = jnp.dot(normed2, up_weight, preferred_element_type=F32) + up_bias
-    act_full, gelu_pull = jax.vjp(gelu_tanh, pre_act)
-    activ = act_full.astype(BF16)
-    grad_full = cotangent.astype(F32)
-    d_pre = gelu_pull(d_activ.astype(F32))[0].astype(BF16)
-    d_normed2, up_own, up_other, pair_down, arrived = hidden_back(
-        d_pre, up_weight, normed2, activ, cotangent, far_cotangent, count
-    )
-    d_up_bias = jnp.sum(d_pre.astype(F32), axis=0)
-    d_down_bias = jnp.sum(grad_full, axis=0)
-    d_middle_norm, d_second_gain, d_second_bias = second_pull(d_normed2.astype(F32))
-    d_middle = grad_full + d_middle_norm
-    d_output_bias = jnp.sum(d_middle, axis=0)
-    d_middle_low = d_middle.astype(BF16)
-    d_context = contract(d_middle_low, output_weight, 1, 1).astype(BF16)
-    mlp_part = jnp.dot(activ, down_weight, preferred_element_type=F32).astype(BF16)
-    grad_out_own, grad_out_other = weight_grad(d_middle_low, context_low, count)
-    scatter_out = ScatterSum(grad_out_own, grad_out_other)
-    d_queries, d_kv_parts, half_down, mlp_sum, rest = attend_back(
-        queries, keyval_all, d_context, context_low, lse, pair_down, mlp_part, up_other
-    )
-    arrived = jnp.concatenate([arrived, rest], axis=0)
-    pair_up = (up_own.astype(F32) + arrived.astype(F32)).astype(BF16)
-    scatter_out.finish()
+    normed2, activ, d_pre, d_up_bias = hidden_stage(
+        inputs, attn_sum, d_activ, up_weight, up_bias, output_bias, second_gain, second_bias
+    )
+    d_up_bias = d_up_bias[0]
+    d_normed2, up_own, up_other, pair_down, out_part = hidden_back(
+        d_pre, up_weight, normed2, activ, cotangent, far_cotangent, down_weight, count
+    )
+    d_middle, d_context, out_part, proj_own, proj_other, row_sums, edge, far_up, far_down = middle_stage(
+        d_normed2,
+        inputs,
+        attn_sum,
+        cotangent,
+        output_bias,
+        second_gain,
+        down_bias,
+        out_part,
+        output_weight,
+        context_low,
+        pair_down,
+        up_own,
+        up_other,
+        count,
+    )
+    d_queries, d_kv_parts, half_down, layer_out, rest, wide_up, wide_down, proj_got = attend_back(
+        queries,
+        keyval_all,
+        d_context,
+        context_low,
+        lse,
+        pair_down,
+        far_up,
+        far_down,
+        out_part,
+        up_other,
+        edge,
+        proj_other,
+    )
+    length = count // 2
+    at_edge = jnp.where(lax.axis_index("dp") // 2 < length // 2, length - 1, 0)
+    pair_up = (up_own.astype(F32) + rest.astype(F32)).astype(BF16)
+    pair_up = lax.dynamic_update_index_in_dim(pair_up, edge, at_edge, 0)
     d_query_bias = jnp.sum(d_queries.astype(F32), axis=0)
-    d_normed1_sum, sent_query, d_keyval, far_up, far_down, sent_down = query_back(
-        d_queries, query_weight, normed1, d_kv_parts, pair_up, half_down, count
-    )
-    layer_out = (middle + mlp_sum.astype(F32) + down_bias).astype(BF16)
-    level = lax.axis_index("dp") // 2
-    ends = jnp.stack(
-        [
-            lax.dynamic_index_in_dim(pair_up, jnp.clip(level + k, 0, count // 2 - 1), 0, False)
-            for k in (0, 1, -1)
-        ]
-    )
-    grad_inputs, sent_kv, sum_gain, sum_bias, sum_value, sums, sent_up = finish(
+    d_normed1, sent_query, sent_proj, d_keyval, far_up, far_down = query_back(
+        d_queries,
+        query_weight,
+        normed1,
+        d_kv_parts,
+        pair_up,
+        wide_up,
+        wide_down,
+        proj_own,
+        proj_got,
+        count,
+    )
+    grad_inputs, first_sums = norm_back(
+        d_keyval, keyval_weight, d_normed1, inputs, d_middle, first_gain
+    )
+    sent_kv, sums, sent_up, sent_down = finish(
         normed1,
         d_keyval,
-        keyval_weight,
-        d_normed1_sum,
-        inputs,
-        d_middle_low,
-        first_gain,
-        [d_up_bias, d_output_bias, d_second_gain, d_second_bias, d_down_bias, d_query_bias],
-        ends,
+        [first_sums[:3], row_sums[:4]],
+        [d_up_bias, d_query_bias],
+        pair_up,
         far_up,
         far_down,
+        half_down,
         count,
     )
+    local = query_weight.shape[1]
+    hidden = d_up_bias.shape[0]
+    flat = sums[7:].reshape(-1)
     return (
         layer_out,
         grad_inputs,
-        sum_gain,
-        sum_bias,
+        sums[0],
+        sums[1],
         sent_query,
+        flat[hidden : hidden + local],
+        sent_kv,
+        sums[2, head_size : 2 * head_size],
+        sent_proj.T,
         sums[5],
-        sent_kv,
-        sum_value,
-        scatter_out.result.T,
-        sums[1],
-        sums[2],
         sums[3],
+        sums[4],
         sent_up,
-        sums[0],
+        flat[:hidden],
         sent_down.T,
-        sums[4],
+        sums[6],
     )
 
 

time: 612 us -> 538 us (0.88)
  other arithmetic: 55.1 us -> 16.1 us
  matrix products: 36.5 us -> 5.37 us
  Pallas kernels: 464 us -> 489 us
  starting transfers between devices: 16.3 us -> 0 us
    pallas_call x2 -> x4, Pallas kernels: 60.2 us -> 152 us  [the longest x1 65.6 us: middle_stage(): pl.pallas_call(functools.partial(middle_kernel, chunk), out_shape=(low((r...]
    pallas_call x1, Pallas kernels: 124 us -> 92.5 us  [query_back(): pl.pallas_call(functools.partial(query_back_kernel, chunks, steps), out_s...]
    dot_general x3 -> x0, matrix products: 31.1 us -> none  [the longest x1 17.2 us: per_device(): pre_act = jnp.dot(normed2, up_weight, preferred_element_type=F32) + up_bias]
    pallas_call x1, Pallas kernels: 91.1 us -> 65.6 us  [hidden_back(): pl.pallas_call(functools.partial(hidden_back_kernel, chunks), out_shape=(...]
    ppermute x7 -> x0, starting transfers between devices: 16.3 us -> none  [the longest x6 15 us: shifted(): return lax.ppermute(value, 'dp', pairs)]
    reduce_sum x3 -> x0, other arithmetic: 16 us -> none  [the longest x1 8.87 us: layer_norm(): return centred * lax.rsqrt(variance + EPSILON) * norm_gain + norm_bias]
    convert_element_type x6 -> x1, other arithmetic: 18.7 us -> 7.84 us  [per_device(): pair_up = (up_own.astype(F32) + rest.astype(F32)).astype(BF16)]
    pallas_call x1, Pallas kernels: 113 us -> 103 us  [attend_back(): pl.pallas_call(functools.partial(attend_back_kernel, block, chunks), out_...]
  transfers between devices with their start and end apart: 7 -> 0, of which waited for: 1 -> 0; matrix products, arithmetic and copies ran while one was open for 7% -> 0% of each run, Pallas kernels for 49% -> 0%
where the time goes in v4:
time: 538 us; the launch traced here: 529 us
  Pallas kernels  489 us (91%)
  local copies, waits for them, and re-layouts  17.2 us (3%)
  other arithmetic  16.1 us (3%)
    pallas_call x1, Pallas kernels, attend_back(): pl.pallas_call(functools.partial(attend_back_kernel, block, chunks), out_...  103 us
    pallas_call x1, Pallas kernels, query_back(): pl.pallas_call(functools.partial(query_back_kernel, chunks, steps), out_s...  92.5 us
    pallas_call x1, Pallas kernels, front(): pl.pallas_call(functools.partial(front_kernel, block, chunks), out_shape=...  75.6 us
    pallas_call x1, Pallas kernels, hidden_back(): pl.pallas_call(functools.partial(hidden_back_kernel, chunks), out_shape=(...  65.6 us
    pallas_call x1, Pallas kernels, middle_stage(): pl.pallas_call(functools.partial(middle_kernel, chunk), out_shape=(low((r...  65.6 us
    pallas_call x1, Pallas kernels, finish(): pl.pallas_call(finish_kernel, out_shape=(jax.ShapeDtypeStruct(shape, F32)...  49 us
    pallas_call x1, Pallas kernels, hidden_stage(): pl.pallas_call(functools.partial(hidden_kernel, tiles), grid=(rows // blo...  24.4 us
    pallas_call x1, Pallas kernels, norm_back(): pl.pallas_call(norm_back_kernel, grid=(rows // chunk,), out_shape=(jax.Sh...  13.5 us

profile of v4, /device:TPU:0, one launch (start us, length us, event | category | flops | bytes accessed | tf_op | source)
XLA Modules:
  0.0 529.2 jit_solution(5357058581005497530)
XLA Ops:
  0.6 0.0 copy-start
  0.7 0.0 copy-start.10
  0.7 0.0 copy-start.12
  0.7 3.0 convert_reduce_fusion
  3.6 0.5 copy-done
  4.1 1.2 fusion.2
  5.3 0.0 copy-done.10
  5.4 0.0 copy-start.3
  5.4 0.0 copy-start.19
  5.4 1.9 fusion.5.n1_ref
  7.3 0.0 copy-start.18
  7.3 0.0 copy-start.5
  7.3 3.3 multiply_convert_fusion.q_ref
  10.6 2.1 fusion.6.own_kv
  12.7 75.6 %front.1 = (bf16[8,1024,256]{2,1,0:T(8,128)(2,1)}, bf16[1024,512]{1,0:T(8,128)(2,1)}, f32[4,1024]{1,0:T(4,128)}, bf16[1024,2048]{1,0:T(8,128)(2,1)}, bf16[1024,2...) custom-call(bf16[1024,512]{1,0:T(8,128)(2,1)} %multiply_convert_fusion.q_ref, bf16[1024,256]{1,0:T(8,128)(2,1)} %fusion.6.own_kv, ...), custom_call_target="tpu_custom_call" | custom-call | tf_op jit(solution)/shard_map/front/pallas_call | solution.py:1273
  88.3 0.0 copy-done.13
  88.3 0.0 copy-done.14
  88.3 0.0 copy-done.15
  88.3 0.0 copy-done.16
  88.4 0.6 pad.16.vec_ref
  89.0 24.4 %hidden.1 = (bf16[1024,2048]{1,0:T(8,128)(2,1)}, bf16[1024,2048]{1,0:T(8,128)(2,1)}, bf16[1024,2048]{1,0:T(8,128)(2,1)}, f32[1,2048]{1,0:T(1,128)}) custom-call(bf16[1024,2048]{1,0:T(8,128)(2,1)} %x_ref.5, bf16[1024,2048]{1,0:T(8,128)(2,1)} %get-tuple-element.61.attn_ref, bf16[1024,2048]{1,0:T(8,128)(2,1)} %get-tuple-element.62.g_ref, ...), custom_call_target="tpu_custom_call" | custom-call | tf_op jit(solution)/shard_map/hidden/pallas_call | solution.py:167
  113.4 65.6 %hidden_back.1 = (bf16[1024,2048]{1,0:T(8,128)(2,1)}, bf16[4,256,2048]{2,1,0:T(8,128)(2,1)}, bf16[4,256,2048]{2,1,0:T(8,128)(2,1)}, bf16[4,512,1024]{2,1,0:T(8,128)(2,1)}, bf16[1024,2048]{1,0:T(8,128)(2,1)}) custom-call(bf16[1024,2048]{1,0:T(8,128)(2,1)} %get-tuple-element.63.dpre_ref, bf16[2048,2048]{1,0:T(8,128)(2,1)} %wu_hbm.1, ...), custom_call_target="tpu_custom_call" | custom-call | tf_op jit(solution)/shard_map/hidden_back/pallas_call | solution.py:316
  179.1 0.6 pad.17.vec_ref
  179.7 65.6 %middle.1 = (bf16[1024,2048]{1,0:T(8,128)(2,1)}, bf16[1024,512]{1,0:T(8,128)(2,1)}, bf16[1024,2048]{1,0:T(8,128)(2,1)}, bf16[4,256,512]{2,1,0:T(8,128)(2,1)}, bf...) custom-call(bf16[1024,2048]{1,0:T(8,128)(2,1)} %get-tuple-element.67, ...), custom_call_target="tpu_custom_call" | custom-call | tf_op jit(solution)/shard_map/middle/pallas_call | solution.py:555
  245.3 0.0 copy-start.17
  245.3 103.3 %attend_back.1 = (bf16[1024,512]{1,0:T(8,128)(2,1)}, bf16[8,1024,256]{2,1,0:T(8,128)(2,1)}, f32[512,1024]{1,0:T(8,128)}, bf16[1024,2048]{1,0:T(8,128)(2,1)}, bf1...) custom-call(bf16[1024,512]{1,0:T(8,128)(2,1)} %multiply_convert_fusi, ...), custom_call_target="tpu_custom_call" | custom-call | tf_op jit(solution)/shard_map/attend_back/pallas_call | solution.py:1440
  348.6 1.4 convert_reduce_fusion.1
  350.0 0.0 copy-done.17
  350.1 7.8 %add_convert_fusion = bf16[4,256,2048]{2,1,0:T(8,128)(2,1)} fusion(bf16[4,256,2048]{2,1,0:T(8,128)(2,1)} %get-tuple-element.83, bf16[4,256,2048]{2,1,0:T(8,128)(2,1)} %get-tuple-element.71.own_hbm), kind=kLoop, calls=%fused_computation.8 | loop fusion | flops 8388608 | bytes 12582912 | tf_op jit(solution)/shard_map/convert_element_type | solution.py:1551
  357.9 1.0 bitcast_dynamic-update-slice_fusion.wide_ref
  358.9 92.5 %query_back.1 = (bf16[1024,2048]{1,0:T(8,128)(2,1)}, f32[256,512]{1,0:T(8,128)}, f32[256,512]{1,0:T(8,128)}, bf16[1024,256]{1,0:T(8,128)(2,1)}, bf16[256,2048]{1,0:T(8,128)(2,1)}, /*index=5*/bf16[256,2048]{1,0:T(8,128)(2,1)}) custom-call(bf16[1024,512]{1,0:T(8,128)(2,1)} %get-tuple-element.81.dq_ref, bf16[2048,512]{1,0:T(8,128)(2,1)} %wq_ref.1, ...), custom_call_target="tpu_custom_call" | custom-call | tf_op jit(solution)/shard_map/query_back/pallas_call | solution.py:776
  451.5 13.5 %norm_back.1 = (f32[1024,2048]{1,0:T(8,128)}, f32[8,2048]{1,0:T(8,128)}) custom-call(bf16[1024,256]{1,0:T(8,128)(2,1)} %get-tuple-element.88.dkv_ref, bf16[2048,256]{1,0:T(8,128)(2,1)} %wkv_ref.1, bf16[1024,2048]{1,0:T(8,128)(2,1)} %get-tuple-element.89.dn_ref, bf16[1024,2048]{1,0:T(8,128)(2,1)} %x_ref.5, bf16[1024,2048]{1,0:T(8,128)(2,1)} %get-tuple-element.90.dm_ref, ...), custom_call_target="tpu_custom_call" | custom-call | tf_op jit(solution)/shard_map/norm_back/pallas_call | solution.py:858
  465.0 0.8 slice.40
  465.8 0.0 copy-done.11
  465.8 0.7 select_maximum_fusion.vec_in
  466.5 49.0 %finish.1 = (f32[256,256]{1,0:T(8,128)}, f32[16,2048]{1,0:T(8,128)}, f32[256,2048]{1,0:T(8,128)}, f32[256,2048]{1,0:T(8,128)}) custom-call(bf16[1024,2048]{1,0:T(8,128)(2,1)} %copy-done.1, bf16[1024,256]{1,0:T(8,128)(2,1)} %get-tuple-element.88.dkv_ref, f32[16,2048]{1,0:T(8,128)} %select_maximum_fusion.vec_in, ...), custom_call_target="tpu_custom_call" | custom-call | tf_op jit(solution)/shard_map/finish/pallas_call | solution.py:988
  515.5 0.0 copy-start.8
  515.5 0.0 copy-start.7
  515.5 2.9 copy.33
  518.5 0.6 slice.53
  519.1 0.6 fusion.7
  519.8 0.5 slice_bitcast_fusion
  520.3 1.0 copy.32
  521.3 4.9 copy.39
  526.2 0.8 copy.40
  527.0 0.7 copy.41
  527.7 0.0 copy-done.4
  527.7 1.3 copy.42
  (30 shorter events, 0.2 us)
Async XLA Ops:
  0.6 3.5 copy-start
  0.7 4.7 copy-start.10
  0.7 4.7 copy-start.12
  5.4 1.9 copy-start.3
  5.4 1.9 copy-start.19
  7.3 3.4 copy-start.1
  7.3 3.3 copy-start.18
  7.3 3.3 copy-start.5
  12.7 75.6 %copy-start.13 = (f32[2048]{0:T(1024)S(1)}, f32[2048]{0:T(1024)}, u32[]{:S(2)}) copy-start(f32[2048]{0:T(1024)} %param.30) | copy-start | bytes 24580
  12.7 75.6 %copy-start.14 = (f32[2048]{0:T(1024)S(1)}, f32[2048]{0:T(1024)}, u32[]{:S(2)}) copy-start(f32[2048]{0:T(1024)} %param.25) | copy-start | bytes 24580
  12.7 75.6 %copy-start.15 = (f32[2048]{0:T(1024)S(1)}, f32[2048]{0:T(1024)}, u32[]{:S(2)}) copy-start(f32[2048]{0:T(1024)} %param.24) | copy-start | bytes 24580
  12.7 75.6 %copy-start.16 = (f32[2048]{0:T(1024)S(1)}, f32[2048]{0:T(1024)}, u32[]{:S(2)}) copy-start(f32[2048]{0:T(1024)} %param.26) | copy-start | bytes 24580
  245.3 104.7 %copy-start.17 = (f32[1,2048]{1,0:T(1,128)S(1)}, f32[1,2048]{1,0:T(1,128)}, u32[]{:S(2)}) copy-start(f32[1,2048]{1,0:T(1,128)} %get-tuple-element.94) | copy-start | bytes 24580
  350.1 7.9 %copy-start.2 = (bf16[256,2048]{1,0:T(8,128)(2,1)S(1)}, bf16[256,2048]{1,0:T(8,128)(2,1)}, u32[]{:S(2)}) copy-start(bf16[256,2048]{1,0:T(8,128)(2,1)} %get-tuple-element.78.edge_ref) | copy-start | bytes 3145732
  451.5 14.3 %copy-start.11 = (f32[8,2048]{1,0:T(8,128)S(1)}, f32[8,2048]{1,0:T(8,128)}, u32[]{:S(2)}) copy-start(f32[8,2048]{1,0:T(8,128)} %get-tuple-element.93) | copy-start | bytes 196612
  515.5 3.0 copy-start.8
  515.5 4.8 copy-start.7
  521.3 4.9 copy-start.6
  521.3 5.7 %copy-start.9 = (f32[256,256]{1,0:T(8,128)S(1)}, f32[256,256]{1,0:T(8,128)}, u32[]{:S(2)}) copy-start(f32[256,256]{1,0:T(8,128)} %get-tuple-element.151) | copy-start | bytes 786436
  521.3 6.4 %copy-start.4 = (f32[256,2048]{1,0:T(8,128)S(1)}, f32[256,2048]{1,0:T(8,128)}, u32[]{:S(2)}) copy-start(f32[256,2048]{1,0:T(8,128)} %get-tuple-element.157) | copy-start | bytes 6291460

commit v5 on v4

--- a/solution.py
+++ b/solution.py
@@ -459,9 +459,9 @@
 
 
 def middle_kernel(
-    chunk, dn_ref, x_ref, attn_ref, cot_ref, vec_ref, part_ref, wo_hbm, ctx_hbm, down_hbm, own_hbm, other_hbm,
-    dm_ref, dctx_ref, mlp_ref, out_own, out_other, sums_ref, edge_ref, far_up, far_down, wo_ref, ctx_ref,
-    edge_own, edge_got, local_sem, x_send, x_recv, z_send, z_recv, acc,
+    chunk, vec_ref, dn_hbm, x_hbm, attn_hbm, cot_hbm, part_hbm, wo_hbm, ctx_hbm, down_hbm, own_hbm, other_hbm,
+    dm_out, dctx_ref, mlp_out, out_own, out_other, sums_ref, edge_ref, far_up, far_down, dm_ref, x_ref, attn_ref,
+    cot_ref, mlp_ref, row_sem, out_sem, wo_ref, ctx_ref, edge_own, edge_got, local_sem, x_send, x_recv, z_send, z_recv, acc,
 ):
     dp = lax.axis_index("dp")
     lane = lax.axis_index("tensor")
@@ -479,6 +479,35 @@
             ]
         )
     ]
+    half = x_ref.shape[0] // 2
+    rows_in = [
+        [
+            pltpu.make_async_copy(
+                source.at[pl.ds(n * half, half)], target.at[pl.ds(n * half, half)], row_sem.at[n, k]
+            )
+            for k, (source, target) in enumerate(
+                [
+                    (x_hbm, x_ref),
+                    (attn_hbm, attn_ref),
+                    (dn_hbm, dm_ref),
+                    (cot_hbm, cot_ref),
+                    (part_hbm, mlp_ref),
+                ]
+            )
+        ]
+        for n in range(2)
+    ]
+    rows_out = [
+        [
+            pltpu.make_async_copy(
+                source.at[pl.ds(n * half, half)], target.at[pl.ds(n * half, half)], out_sem.at[n, k]
+            )
+            for k, (source, target) in enumerate([(dm_ref, dm_out), (mlp_ref, mlp_out)])
+        ]
+        for n in range(2)
+    ]
+    for copy in rows_in[0] + rows_in[1]:
+        copy.start()
     for copy in local:
         copy.start()
     greet([x_peer, upper, lower])
@@ -500,11 +529,11 @@
         at = pl.ds(pl.multiple_of(k * chunk, chunk), chunk)
         values = x_ref[at, :].astype(F32) + attn_ref[at, :].astype(F32) + vec_ref[0:1, :]
         base = share * (values + vec_ref[2:3, :])
-        mlp_ref[at, :] = (part_ref[at, :].astype(F32) + base).astype(BF16)
+        mlp_ref[at, :] = (mlp_ref[at, :].astype(F32) + base).astype(BF16)
         centred = values - jnp.mean(values, axis=-1, keepdims=True)
         scale = lax.rsqrt(jnp.mean(centred * centred, axis=-1, keepdims=True) + EPSILON)
         hat = centred * scale
-        grad = dn_ref[at, :].astype(F32)
+        grad = dm_ref[at, :].astype(F32)
         acc[0] += fold(grad * hat)
         acc[1] += fold(grad)
         scaled = grad * vec_ref[1:2, :]
@@ -516,10 +545,17 @@
         acc[3] += fold(cot)
         dm_ref[at, :] = d_middle.astype(BF16)
 
-    @pl.loop(0, rows // chunk)
-    def _(k):
-        norm_rows(k)
-
+    each = rows // chunk // 2
+    for n in range(2):
+        for copy in rows_in[n]:
+            copy.wait()
+
+        @pl.loop(n * each, (n + 1) * each)
+        def _(k):
+            norm_rows(k)
+
+        for copy in rows_out[n]:
+            copy.start()
     for n in range(4):
         sums_ref[n : n + 1, :] = jnp.sum(acc[n], axis=0, keepdims=True)
     sums_ref[4:8, :] = jnp.zeros((4, width), F32)
@@ -534,6 +570,8 @@
     grad_rows(dm_ref, ctx_ref, out_other, 1 - side)
     grad_rows(dm_ref, ctx_ref, out_own, side)
     local[2].wait()
+    for copy in rows_out[0] + rows_out[1]:
+        copy.wait()
     to_x.wait()
     edge_ref[...] = (edge_own[...].astype(F32) + edge_got[...].astype(F32)).astype(BF16)
     first_step.wait()
@@ -565,9 +603,12 @@
             low(down.shape[1:]),
             low(down.shape[1:]),
         ),
-        in_specs=[VMEM] * 6 + [hbm] * 5,
-        out_specs=(VMEM,) * 7 + (hbm,) * 2,
-        scratch_shapes=[
+        in_specs=[VMEM] + [hbm] * 10,
+        out_specs=(hbm, VMEM, hbm) + (VMEM,) * 4 + (hbm,) * 2,
+        scratch_shapes=[pltpu.VMEM((rows, width), BF16)] * 5
+        + [
+            dma((2, 5)),
+            dma((2, 2)),
             pltpu.VMEM(output_weight.shape, BF16),
             pltpu.VMEM(context.shape, BF16),
             edge,
@@ -584,7 +625,7 @@
         ),
         name="middle",
     )(
-        d_normed2, inputs, attn_sum, cotangent, vec, part, output_weight, context, down, up_own, up_other,
+        vec, d_normed2, inputs, attn_sum, cotangent, part, output_weight, context, down, up_own, up_other,
     )
 
 
@@ -816,8 +857,11 @@
     )(d_queries, query_weight, normed1, parts, wide, wide_up, wide_down, proj, proj_x)
 
 
-def norm_back_kernel(dkv_ref, wkv_ref, dn_ref, x_ref, dm_ref, gain_ref, grad_x, sums_ref, acc, acc_kv):
+def norm_back_kernel(
+    dkv_ref, wkv_ref, dn_ref, x_ref, dm_ref, gain_ref, pass_in, grad_x, sums_ref, pass_out, acc, acc_kv
+):
     k = pl.program_id(0)
+    pass_out[...] = pass_in[...]
 
     @pl.when(k == 0)
     def _():
@@ -850,7 +894,7 @@
         sums_ref[2:3, 0 : acc_kv.shape[1]] = jnp.sum(acc_kv[...], axis=0, keepdims=True)
 
 
-def norm_back(d_keyval, keyval_weight, d_normed1, inputs, d_middle, gain, chunk=128):
+def norm_back(d_keyval, keyval_weight, d_normed1, inputs, d_middle, gain, passed, chunk=128):
     rows, width = inputs.shape
     kv_width = d_keyval.shape[1]
     row = lambda cols: pl.BlockSpec((chunk, cols), lambda k: (k, 0))
@@ -861,6 +905,7 @@
         out_shape=(
             jax.ShapeDtypeStruct((rows, width), F32),
             jax.ShapeDtypeStruct((8, width), F32),
+            jax.ShapeDtypeStruct(passed.shape, BF16),
         ),
         in_specs=[
             row(kv_width),
@@ -869,17 +914,18 @@
             row(width),
             row(width),
             fixed((1, width)),
+            row(width),
         ],
-        out_specs=(row(width), fixed((8, width))),
+        out_specs=(row(width), fixed((8, width)), row(width)),
         scratch_shapes=[pltpu.VMEM((2, 8, width), F32), pltpu.VMEM((8, kv_width), F32)],
         compiler_params=pltpu.CompilerParams(vmem_limit_bytes=62 << 20),
         name="norm_back",
-    )(d_keyval, keyval_weight, d_normed1, inputs, d_middle, gain.reshape(1, width))
+    )(d_keyval, keyval_weight, d_normed1, inputs, d_middle, gain.reshape(1, width), passed)
 
 
 def finish_kernel(
-    n1_ref, dkv_ref, vec_in, wide_ref, far_up, far_down, down_ref, grad_ref, vec_ref, up_ref, down_out, ends_ref,
-    local_sem, d_send, d_recv, down_low, down_got, up_out, up_in, up_send, up_recv, own_ref, other_ref, got_ref, x_send, x_recv, own_vec, low_vec, slots, send, recv, *chain_refs,
+    dkv_ref, vec_in, far_up, far_down, down_ref, n1_hbm, wide_ref, grad_ref, vec_ref, up_ref, down_out, n1_ref,
+    n1_sem, g_send, g_recv, ends_ref, local_sem, d_send, d_recv, down_low, down_got, up_out, up_in, up_send, up_recv, own_ref, other_ref, got_ref, x_send, x_recv, own_vec, low_vec, slots, send, recv, *chain_refs,
 ):
     block = lax.axis_index("dp")
     lane = lax.axis_index("tensor")
@@ -895,9 +941,15 @@
         )
         for n, k in enumerate((0, 1, -1))
     ]
+    take = pltpu.make_async_copy(n1_hbm, n1_ref, n1_sem)
+    take.start()
     for copy in local:
         copy.start()
-    greet([x_peer] + others)
+    core = lax.rem(lane, 2)
+    core_peer = (block, lane + 1 - 2 * core)
+    half_kv = dkv_ref.shape[1] // 2
+    mine = pl.ds(pl.multiple_of(core * half_kv, half_kv), half_kv)
+    greet([core_peer, x_peer] + others)
     low_vec[0] = vec_in[...].astype(BF16)
     to_pair = remote(low_vec.at[0], slots.at[0], send.at[0], recv.at[0], x_peer)
     to_pair.start()
@@ -921,7 +973,9 @@
 
             last(way).start()
 
-    grad_rows(n1_ref, dkv_ref, other_ref, 1 - side)
+    take.wait()
+    kv_half = dkv_ref.at[:, mine]
+    grad_rows(n1_ref, kv_half, other_ref, 1 - side)
     to_x = remote(other_ref, got_ref, x_send, x_recv, x_peer)
     to_x.start()
     half_rows, half_cols = down_low.shape
@@ -937,7 +991,7 @@
         copy = remote(low_vec.at[1], slots.at[k], send.at[k], recv.at[k], others[k - 1])
         copy.start()
         copies.append(copy)
-    grad_rows(n1_ref, dkv_ref, own_ref, side)
+    grad_rows(n1_ref, kv_half, own_ref, side)
     chain = Chain(length, level, upper, lower, own_ref, chain_refs[:4], chain_refs[4:8])
     to_x.wait_recv()
     own_ref[...] = (own_ref[...].astype(F32) + got_ref[...].astype(F32)).astype(BF16)
@@ -947,7 +1001,9 @@
         chain.arrive(s)
         if s + 1 < length:
             chain.start(s + 1)
-    chain.result(grad_ref)
+    chain.result(grad_ref.at[:, mine])
+    to_core = remote(grad_ref.at[:, mine], grad_ref.at[:, mine], g_send, g_recv, core_peer)
+    to_core.start()
     d_to_x.wait()
     first = pl.ds(pl.multiple_of(side * half_cols, half_cols), half_cols)
     second = pl.ds(pl.multiple_of((1 - side) * half_cols, half_cols), half_cols)
@@ -971,6 +1027,7 @@
 
     chain.drain()
     to_x.wait_send()
+    to_core.wait()
 
 
 def finish(normed1, d_keyval, rows_of_vectors, vectors, wide, far_up, far_down, down, count):
@@ -982,7 +1039,8 @@
     height = -(-packed.shape[0] // 8) * 8
     packed = jnp.pad(packed, ((0, height - packed.shape[0]), (0, 0)))
     shape = (width // count, d_keyval.shape[1])
-    half = pltpu.VMEM((count // 2,) + shape, BF16)
+    part = (shape[0], shape[1] // 2)
+    half = pltpu.VMEM((count // 2,) + part, BF16)
     dma = pltpu.SemaphoreType.DMA
     two = pltpu.VMEM((2,) + far_up.shape, BF16)
     return pl.pallas_call(
@@ -993,9 +1051,13 @@
             jax.ShapeDtypeStruct(far_up.shape, F32),
             jax.ShapeDtypeStruct((down.shape[0] // 2, 2 * down.shape[1]), F32),
         ),
-        in_specs=[VMEM] * 3 + [pl.BlockSpec(memory_space=pl.ANY)] + [VMEM] * 3,
+        in_specs=[VMEM] * 5 + [pl.BlockSpec(memory_space=pl.ANY)] * 2,
         out_specs=(VMEM,) * 4,
         scratch_shapes=[
+            pltpu.VMEM(normed1.shape, BF16),
+            dma,
+            dma,
+            dma,
             pltpu.VMEM((3,) + far_up.shape, BF16),
             dma((3,)),
             dma,
@@ -1011,12 +1073,12 @@
             dma((count // 2,)),
             dma((count // 2,)),
         ]
-        + chain_scratch(count // 2, shape),
+        + chain_scratch(count // 2, part),
         compiler_params=pltpu.CompilerParams(
             collective_id=2, has_side_effects=True, vmem_limit_bytes=62 << 20
         ),
         name="finish",
-    )(normed1, d_keyval, packed, wide, far_up, far_down, down)
+    )(d_keyval, packed, far_up, far_down, down, normed1, wide)
 
 
 def front_kernel(
@@ -1307,9 +1369,10 @@
 
 
 def attend_back_kernel(
-    block, chunks, q_ref, kv_ref, do_ref, ctx_ref, lse_ref, pair_ref, far_up, far_down, mlp_ref, sent_ref,
-    edge_ref, proj_ref, dq_ref, dkv_ref, grad_ref, out_ref, got_ref, wide_up, wide_down, proj_got, dq_acc, dkv_acc,
-    delta, x_send, x_recv, z_send, z_recv, from_core, summed, from_y, *rest,
+    block, chunks, q_ref, do_ref, ctx_ref, lse_ref, far_up, far_down, kv_hbm, pair_hbm, mlp_hbm, sent_ref,
+    edge_ref, proj_ref, dq_ref, grad_ref, dkv_out, sum_out, got_ref, wide_up, wide_down, proj_got, kv_ref, pair_ref,
+    mlp_ref, dkv_ref, out_ref, in_sem, dkv_sem, sum_sem, dq_acc, dkv_acc, delta, x_send, x_recv, z_send, z_recv,
+    from_core, summed, from_y, *rest,
 ):
     sems, chain_refs = rest[:6], rest[6:]
     rows = q_ref.shape[0]
@@ -1322,6 +1385,25 @@
     length, level, upper, lower = chain_peers()
     early = (far_up, far_down)
     chain = Chain(length, level, upper, lower, pair_ref, chain_refs[:4], chain_refs[4:], early)
+    depth = 2 * rows
+    local = [
+        pltpu.make_async_copy(mlp_hbm, mlp_ref, in_sem.at[0]),
+        pltpu.make_async_copy(pair_hbm, pair_ref, in_sem.at[1]),
+    ] + [
+        pltpu.make_async_copy(
+            kv_hbm.at[pl.ds(n * depth, depth)], kv_ref.at[pl.ds(n * depth, depth)], in_sem.at[2 + n]
+        )
+        for n in range(SPAN // 2)
+    ]
+    dkv_copies = [
+        pltpu.make_async_copy(
+            dkv_ref.at[pl.ds(2 * n, 2)], dkv_out.at[pl.ds(2 * n, 2)], dkv_sem.at[n]
+        )
+        for n in range(SPAN // 2)
+    ]
+    sum_copy = pltpu.make_async_copy(out_ref, sum_out, sum_sem)
+    for copy in local:
+        copy.start()
     greet([ts.core_peer, ts.y_peer, x_peer, upper, lower])
     left = pl.ds(jnp.where(level < length // 2, 0, 1), length - 1)
     proj_to_x = remote(proj_ref, proj_got, x_send.at[1], x_recv.at[1], x_peer)
@@ -1329,10 +1411,13 @@
     to_x = remote(sent_ref.at[left], got_ref.at[left], x_send.at[0], x_recv.at[0], x_peer)
     to_x.start()
 
+    local[0].wait()
+
     @pl.loop(0, chunks)
     def _(k):
         ts.first(k)
 
+    local[1].wait()
     chain.start(2)
     wide_step = FirstStep(
         length, level, upper, lower, (edge_ref, edge_ref), (wide_up, wide_down), z_send, z_recv
@@ -1343,6 +1428,7 @@
     per_slot = -(-(length - 2) // (levels - 1))
     done = 1
     for target in range(levels):
+        local[2 + target].wait()
         dkv_acc[...] = jnp.zeros_like(dkv_acc)
         for i in range(rows // block):
             span = slice(i * block, (i + 1) * block)
@@ -1401,6 +1487,7 @@
 
         for b in range(2):
             dkv_ref[2 * target + b] = dkv_acc[b * rows : (b + 1) * rows].astype(BF16)
+        dkv_copies[target].start()
         if target < levels - 1:
             for _ in range(per_slot):
                 if done < length - 1:
@@ -1415,6 +1502,9 @@
             def _(k):
                 ts.third(k)
 
+            ts.finish(chunks)
+            sum_copy.start()
+
     for i in range(rows // block):
         span = slice(i * block, (i + 1) * block)
         for h in range(heads):
@@ -1423,7 +1513,8 @@
             )
     chain.drain()
     wide_step.wait()
-    ts.finish(chunks)
+    for copy in dkv_copies + [sum_copy]:
+        copy.wait()
     to_x.wait()
     proj_to_x.wait()
 
@@ -1441,17 +1532,25 @@
         functools.partial(attend_back_kernel, block, chunks),
         out_shape=(
             low((rows, width)),
+            jax.ShapeDtypeStruct(pair.shape[1:], F32),
             low((SPAN, rows, 2 * head)),
-            jax.ShapeDtypeStruct(pair.shape[1:], F32),
             low(mlp_part.shape),
             low(sent.shape),
             low(edge.shape),
             low(edge.shape),
             low(proj.shape),
         ),
-        in_specs=[VMEM] * 9 + [hbm] * 3,
-        out_specs=(VMEM,) * 4 + (hbm,) * 4,
+        in_specs=[VMEM] * 6 + [hbm] * 6,
+        out_specs=(VMEM,) * 2 + (hbm,) * 6,
         scratch_shapes=[
+            pltpu.VMEM(keyval.shape, BF16),
+            pltpu.VMEM(pair.shape, BF16),
+            pltpu.VMEM(mlp_part.shape, BF16),
+            pltpu.VMEM((SPAN, rows, 2 * head), BF16),
+            pltpu.VMEM(mlp_part.shape, BF16),
+            dma((2 + SPAN // 2,)),
+            dma((SPAN // 2,)),
+            dma,
             pltpu.VMEM((rows // block, heads, head, block), F32),
             pltpu.VMEM((2 * rows, 2 * head), F32),
             pltpu.VMEM((heads, rows), F32),
@@ -1467,7 +1566,7 @@
         ),
         name="attend_back",
     )(
-        queries, keyval, d_context, context, lse, pair, far_up, far_down, mlp_part, sent, edge, proj
+        queries, d_context, context, lse, far_up, far_down, keyval, pair, mlp_part, sent, edge, proj
     )
 
 
@@ -1532,7 +1631,7 @@
         up_other,
         count,
     )
-    d_queries, d_kv_parts, half_down, layer_out, rest, wide_up, wide_down, proj_got = attend_back(
+    d_queries, half_down, d_kv_parts, layer_out, rest, wide_up, wide_down, proj_got = attend_back(
         queries,
         keyval_all,
         d_context,
@@ -1563,8 +1662,8 @@
         proj_got,
         count,
     )
-    grad_inputs, first_sums = norm_back(
-        d_keyval, keyval_weight, d_normed1, inputs, d_middle, first_gain
+    grad_inputs, first_sums, layer_out = norm_back(
+        d_keyval, keyval_weight, d_normed1, inputs, d_middle, first_gain, layer_out
     )
     sent_kv, sums, sent_up, sent_down = finish(
         normed1,

time: 538 us -> 526 us (0.978)
  Pallas kernels: 489 us -> 481 us
    pallas_call x1, Pallas kernels: 65.6 us -> 56.9 us  [middle_stage(): pl.pallas_call(functools.partial(middle_kernel, chunk), out_shape=(low((r...]
    pallas_call x1, Pallas kernels: 92.5 us -> 99.7 us  [query_back(): pl.pallas_call(functools.partial(query_back_kernel, chunks, steps), out_s...]
    pallas_call x1, Pallas kernels: 103 us -> 97 us  [attend_back(): pl.pallas_call(functools.partial(attend_back_kernel, block, chunks), out_...]
    unnamed x46 -> x43, local copies, waits for them, and re-layouts: 12.2 us -> 8.35 us
where the time goes in v5:
time: 526 us; the launch traced here: 517 us
  Pallas kernels  481 us (91%)
  other arithmetic  16 us (3%)
  local copies, waits for them, and re-layouts  13.3 us (3%)
  matrix products  5.37 us (1%)
    pallas_call x1, Pallas kernels, query_back(): pl.pallas_call(functools.partial(query_back_kernel, chunks, steps), out_s...  99.7 us
    pallas_call x1, Pallas kernels, attend_back(): pl.pallas_call(functools.partial(attend_back_kernel, block, chunks), out_...  97 us
    pallas_call x1, Pallas kernels, front(): pl.pallas_call(functools.partial(front_kernel, block, chunks), out_shape=...  75.6 us
    pallas_call x1, Pallas kernels, hidden_back(): pl.pallas_call(functools.partial(hidden_back_kernel, chunks), out_shape=(...  65.7 us
    pallas_call x1, Pallas kernels, middle_stage(): pl.pallas_call(functools.partial(middle_kernel, chunk), out_shape=(low((r...  56.9 us
    pallas_call x1, Pallas kernels, finish(): pl.pallas_call(finish_kernel, out_shape=(jax.ShapeDtypeStruct(shape, F32)...  45.7 us
    pallas_call x1, Pallas kernels, hidden_stage(): pl.pallas_call(functools.partial(hidden_kernel, tiles), grid=(rows // blo...  24.4 us
    pallas_call x1, Pallas kernels, norm_back(): pl.pallas_call(norm_back_kernel, grid=(rows // chunk,), out_shape=(jax.Sh...  16.2 us

profile of v5, /device:TPU:0, one launch (start us, length us, event | category | flops | bytes accessed | tf_op | source)
XLA Modules:
  0.0 517.0 jit_solution(3936360274573160008)
XLA Ops:
  0.6 0.0 copy-start
  0.7 0.0 copy-start.9
  0.7 0.0 copy-start.11
  0.7 3.0 convert_reduce_fusion
  3.6 0.5 copy-done
  4.1 1.2 fusion.2
  5.4 0.0 copy-start.3
  5.4 0.0 copy-start.18
  5.4 1.9 fusion.5.n1_ref.n1_hbm
  7.3 0.0 copy-done.3
  7.3 0.0 copy-done.18
  7.3 0.0 copy-start.1
  7.3 0.0 copy-start.17
  7.3 0.0 copy-start.5
  7.3 3.3 multiply_convert_fusion.q_ref
  10.6 0.0 copy-done.17
  10.6 2.1 fusion.6.own_kv
  12.7 75.6 %front.1 = (bf16[8,1024,256]{2,1,0:T(8,128)(2,1)}, bf16[1024,512]{1,0:T(8,128)(2,1)}, f32[4,1024]{1,0:T(4,128)}, bf16[1024,2048]{1,0:T(8,128)(2,1)}, bf16[1024,2...) custom-call(bf16[1024,512]{1,0:T(8,128)(2,1)} %multiply_convert_fusion.q_ref, bf16[1024,256]{1,0:T(8,128)(2,1)} %fusion.6.own_kv, ...), custom_call_target="tpu_custom_call" | custom-call | tf_op jit(solution)/shard_map/front/pallas_call | solution.py:1335
  88.3 0.0 copy-done.12
  88.3 0.0 copy-done.13
  88.3 0.0 copy-done.14
  88.3 0.0 copy-done.15
  88.4 0.6 pad.17.vec_ref
  89.0 24.4 %hidden.1 = (bf16[1024,2048]{1,0:T(8,128)(2,1)}, bf16[1024,2048]{1,0:T(8,128)(2,1)}, bf16[1024,2048]{1,0:T(8,128)(2,1)}, f32[1,2048]{1,0:T(1,128)}) custom-call(bf16[1024,2048]{1,0:T(8,128)(2,1)} %x_ref.3, bf16[1024,2048]{1,0:T(8,128)(2,1)} %get-tuple-element.61.attn_ref.attn_hbm, bf16[1024,2048]{1,0:T(8,128)(2,1)} %get-tuple-element.62.g_ref, ...), custom_call_target="tpu_custom_call" | custom-call | tf_op jit(solution)/shard_map/hidden/pallas_call | solution.py:167
  113.5 65.7 %hidden_back.1 = (bf16[1024,2048]{1,0:T(8,128)(2,1)}, bf16[4,256,2048]{2,1,0:T(8,128)(2,1)}, bf16[4,256,2048]{2,1,0:T(8,128)(2,1)}, bf16[4,512,1024]{2,1,0:T(8,128)(2,1)}, bf16[1024,2048]{1,0:T(8,128)(2,1)}) custom-call(bf16[1024,2048]{1,0:T(8,128)(2,1)} %get-tuple-element.63.dpre_ref, bf16[2048,2048]{1,0:T(8,128)(2,1)} %wu_hbm.1, ...), custom_call_target="tpu_custom_call" | custom-call | tf_op jit(solution)/shard_map/hidden_back/pallas_call | solution.py:316
  179.1 0.6 pad.16.vec_ref
  179.8 56.9 %middle.1 = (bf16[1024,2048]{1,0:T(8,128)(2,1)}, bf16[1024,512]{1,0:T(8,128)(2,1)}, bf16[1024,2048]{1,0:T(8,128)(2,1)}, bf16[4,256,512]{2,1,0:T(8,128)(2,1)}, bf...) custom-call(f32[8,2048]{1,0:T(8,128)} %pad.16.vec_ref, ...), custom_call_target="tpu_custom_call" | custom-call | tf_op jit(solution)/shard_map/middle/pallas_call | solution.py:593
  236.7 0.0 copy-start.16
  236.7 97.0 %attend_back.1 = (bf16[1024,512]{1,0:T(8,128)(2,1)}, f32[512,1024]{1,0:T(8,128)}, bf16[8,1024,256]{2,1,0:T(8,128)(2,1)}, bf16[1024,2048]{1,0:T(8,128)(2,1)}, bf1...) custom-call(bf16[1024,512]{1,0:T(8,128)(2,1)} %multiply_convert_fusi, ...), custom_call_target="tpu_custom_call" | custom-call | tf_op jit(solution)/shard_map/attend_back/pallas_call | solution.py:1531
  333.7 1.4 convert_reduce_fusion.1
  335.2 0.0 copy-start.2
  335.2 7.8 %add_convert_fusion = bf16[4,256,2048]{2,1,0:T(8,128)(2,1)} fusion(bf16[4,256,2048]{2,1,0:T(8,128)(2,1)} %get-tuple-element.83, bf16[4,256,2048]{2,1,0:T(8,128)(2,1)} %get-tuple-element.71.own_hbm), kind=kLoop, calls=%fused_computation.8 | loop fusion | flops 8388608 | bytes 12582912 | tf_op jit(solution)/shard_map/convert_element_type | solution.py:1650
  343.0 1.0 bitcast_dynamic-update-slice_fusion.wide_ref
  344.0 99.7 %query_back.1 = (bf16[1024,2048]{1,0:T(8,128)(2,1)}, f32[256,512]{1,0:T(8,128)}, f32[256,512]{1,0:T(8,128)}, bf16[1024,256]{1,0:T(8,128)(2,1)}, bf16[256,2048]{1,0:T(8,128)(2,1)}, /*index=5*/bf16[256,2048]{1,0:T(8,128)(2,1)}) custom-call(bf16[1024,512]{1,0:T(8,128)(2,1)} %get-tuple-element.81.dq_ref, bf16[2048,512]{1,0:T(8,128)(2,1)} %wq_ref.1, ...), custom_call_target="tpu_custom_call" | custom-call | tf_op jit(solution)/shard_map/query_back/pallas_call | solution.py:817
  443.7 16.2 %norm_back.1 = (f32[1024,2048]{1,0:T(8,128)}, f32[8,2048]{1,0:T(8,128)}, bf16[1024,2048]{1,0:T(8,128)(2,1)}) custom-call(bf16[1024,256]{1,0:T(8,128)(2,1)} %get-tuple-element.88.dkv_ref, bf16[2048,256]{1,0:T(8,128)(2,1)} %wkv_ref.1, bf16[1024,2048]{1,0:T(8,128)(2,1)} %get-tuple-element.89.dn_ref, bf16[1024,2048]{1,0:T(8,128)(2,1)} %x_ref.3, ...), custom_call_target="tpu_custom_call" | custom-call | tf_op jit(solution)/shard_map/norm_back/pallas_call | solution.py:902
  459.9 0.8 slice.40
  460.8 0.7 select_maximum_fusion.vec_in
  461.5 45.7 %finish.1 = (f32[256,256]{1,0:T(8,128)}, f32[16,2048]{1,0:T(8,128)}, f32[256,2048]{1,0:T(8,128)}, f32[256,2048]{1,0:T(8,128)}) custom-call(bf16[1024,256]{1,0:T(8,128)(2,1)} %get-tuple-element.88.dkv_ref, f32[16,2048]{1,0:T(8,128)} %select_maximum_fusion.vec_in, bf16[256,2048]{1,0:T(8,128)(2,1)} %get-tuple-element.97.far_up, ...), custom_call_target="tpu_custom_call" | custom-call | tf_op jit(solution)/shard_map/finish/pallas_call | solution.py:1046
  507.2 3.0 copy.33
  510.2 0.6 slice.53
  510.8 0.6 fusion.7
  511.5 0.5 slice_bitcast_fusion
  512.0 1.0 copy.32
  513.0 0.0 copy-done.6
  513.0 0.8 copy.38
  513.8 1.7 copy.39
  515.4 0.0 copy-done.4
  515.4 1.3 copy.40
  (27 shorter events, 0.1 us)
Async XLA Ops:
  0.6 3.5 copy-start
  0.7 4.7 copy-start.9
  0.7 4.7 copy-start.11
  5.4 1.9 copy-start.3
  5.4 1.9 copy-start.18
  7.3 3.4 copy-start.1
  7.3 3.3 copy-start.17
  7.3 3.3 copy-start.5
  12.7 75.6 %copy-start.12 = (f32[2048]{0:T(1024)S(1)}, f32[2048]{0:T(1024)}, u32[]{:S(2)}) copy-start(f32[2048]{0:T(1024)} %param.26) | copy-start | bytes 24580
  12.7 75.6 %copy-start.13 = (f32[2048]{0:T(1024)S(1)}, f32[2048]{0:T(1024)}, u32[]{:S(2)}) copy-start(f32[2048]{0:T(1024)} %param.25) | copy-start | bytes 24580
  12.7 75.6 %copy-start.14 = (f32[2048]{0:T(1024)S(1)}, f32[2048]{0:T(1024)}, u32[]{:S(2)}) copy-start(f32[2048]{0:T(1024)} %param.24) | copy-start | bytes 24580
  12.7 75.6 %copy-start.15 = (f32[2048]{0:T(1024)S(1)}, f32[2048]{0:T(1024)}, u32[]{:S(2)}) copy-start(f32[2048]{0:T(1024)} %param.30) | copy-start | bytes 24580
  236.7 98.5 %copy-start.16 = (f32[1,2048]{1,0:T(1,128)S(1)}, f32[1,2048]{1,0:T(1,128)}, u32[]{:S(2)}) copy-start(f32[1,2048]{1,0:T(1,128)} %get-tuple-element.96) | copy-start | bytes 24580
  335.2 7.8 %copy-start.2 = (bf16[256,2048]{1,0:T(8,128)(2,1)S(1)}, bf16[256,2048]{1,0:T(8,128)(2,1)}, u32[]{:S(2)}) copy-start(bf16[256,2048]{1,0:T(8,128)(2,1)} %get-tuple-element.79.edge_ref) | copy-start | bytes 3145732
  443.7 17.0 %copy-start.10 = (f32[8,2048]{1,0:T(8,128)S(1)}, f32[8,2048]{1,0:T(8,128)}, u32[]{:S(2)}) copy-start(f32[8,2048]{1,0:T(8,128)} %get-tuple-element.95) | copy-start | bytes 196612
  507.1 3.1 copy-start.8
  507.1 4.9 copy-start.7
  507.1 5.8 %copy-start.6 = (f32[256,512]{1,0:T(8,128)S(1)}, f32[256,512]{1,0:T(8,128)}, u32[]{:S(2)}) copy-start(f32[256,512]{1,0:T(8,128)} %get-tuple-element.151) | copy-start | bytes 1572868
  507.1 8.3 %copy-start.4 = (f32[256,2048]{1,0:T(8,128)S(1)}, f32[256,2048]{1,0:T(8,128)}, u32[]{:S(2)}) copy-start(f32[256,2048]{1,0:T(8,128)} %get-tuple-element.159) | copy-start | bytes 6291460

commit v6 on v5

--- a/solution.py
+++ b/solution.py
@@ -857,6 +857,33 @@
     )(d_queries, query_weight, normed1, parts, wide, wide_up, wide_down, proj, proj_x)
 
 
+def pair_kernel(own_ref, rest_ref, edge_ref, out_ref):
+    length = pl.num_programs(0)
+    lev = pl.program_id(0)
+    at_edge = jnp.where(lax.axis_index("dp") // 2 < length // 2, length - 1, 0)
+
+    @pl.when(lev == at_edge)
+    def _():
+        out_ref[0] = edge_ref[...]
+
+    @pl.when(lev != at_edge)
+    def _():
+        out_ref[0] = (own_ref[0].astype(F32) + rest_ref[0].astype(F32)).astype(BF16)
+
+
+def pair_sum(own, rest, edge):
+    level = pl.BlockSpec((1,) + own.shape[1:], lambda k: (k, 0, 0))
+    return pl.pallas_call(
+        pair_kernel,
+        grid=(own.shape[0],),
+        out_shape=jax.ShapeDtypeStruct(own.shape, BF16),
+        in_specs=[level, level, pl.BlockSpec(edge.shape, lambda k: (0, 0))],
+        out_specs=level,
+        compiler_params=pltpu.CompilerParams(vmem_limit_bytes=62 << 20),
+        name="pair_sum",
+    )(own, rest, edge)
+
+
 def norm_back_kernel(
     dkv_ref, wkv_ref, dn_ref, x_ref, dm_ref, gain_ref, pass_in, grad_x, sums_ref, pass_out, acc, acc_kv
 ):
@@ -894,7 +921,7 @@
         sums_ref[2:3, 0 : acc_kv.shape[1]] = jnp.sum(acc_kv[...], axis=0, keepdims=True)
 
 
-def norm_back(d_keyval, keyval_weight, d_normed1, inputs, d_middle, gain, passed, chunk=128):
+def norm_back(d_keyval, keyval_weight, d_normed1, inputs, d_middle, gain, passed, chunk=256):
     rows, width = inputs.shape
     kv_width = d_keyval.shape[1]
     row = lambda cols: pl.BlockSpec((chunk, cols), lambda k: (k, 0))
@@ -1645,10 +1672,7 @@
         edge,
         proj_other,
     )
-    length = count // 2
-    at_edge = jnp.where(lax.axis_index("dp") // 2 < length // 2, length - 1, 0)
-    pair_up = (up_own.astype(F32) + rest.astype(F32)).astype(BF16)
-    pair_up = lax.dynamic_update_index_in_dim(pair_up, edge, at_edge, 0)
+    pair_up = pair_sum(up_own, rest, edge)
     d_query_bias = jnp.sum(d_queries.astype(F32), axis=0)
     d_normed1, sent_query, sent_proj, d_keyval, far_up, far_down = query_back(
         d_queries,

time: 526 us -> 527 us (level)
  other arithmetic: 16 us -> 8.55 us
    convert_element_type x1 -> x0, other arithmetic: 7.75 us -> none  [per_device(): pair_up = (up_own.astype(F32) + rest.astype(F32)).astype(BF16)]
    pallas_call x0 -> x1, Pallas kernels: none -> 6.19 us  [pair_sum(): pl.pallas_call(pair_kernel, grid=(own.shape[0],), out_shape=jax.ShapeDtyp...]
where the time goes in v6:
time: 527 us; the launch traced here: 518 us
  Pallas kernels  486 us (92%)
  local copies, waits for them, and re-layouts  16.8 us (3%)
  other arithmetic  8.55 us (2%)
  matrix products  5.36 us (1%)
    pallas_call x1, Pallas kernels, query_back(): pl.pallas_call(functools.partial(query_back_kernel, chunks, steps), out_s...  99.5 us
    pallas_call x1, Pallas kernels, attend_back(): pl.pallas_call(functools.partial(attend_back_kernel, block, chunks), out_...  97 us
    pallas_call x1, Pallas kernels, front(): pl.pallas_call(functools.partial(front_kernel, block, chunks), out_shape=...  75.5 us
    pallas_call x1, Pallas kernels, hidden_back(): pl.pallas_call(functools.partial(hidden_back_kernel, chunks), out_shape=(...  65.6 us
    pallas_call x1, Pallas kernels, middle_stage(): pl.pallas_call(functools.partial(middle_kernel, chunk), out_shape=(low((r...  56.9 us
    pallas_call x1, Pallas kernels, finish(): pl.pallas_call(finish_kernel, out_shape=(jax.ShapeDtypeStruct(shape, F32)...  45.7 us
    pallas_call x1, Pallas kernels, hidden_stage(): pl.pallas_call(functools.partial(hidden_kernel, tiles), grid=(rows // blo...  24.5 us
    pallas_call x1, Pallas kernels, norm_back(): pl.pallas_call(norm_back_kernel, grid=(rows // chunk,), out_shape=(jax.Sh...  15 us

profile of v6, /device:TPU:0, one launch (start us, length us, event | category | flops | bytes accessed | tf_op | source)
XLA Modules:
  0.0 517.7 jit_solution(4883507445782135593)
XLA Ops:
  0.6 0.0 copy-start
  0.7 0.8 concatenate.9
  1.5 0.0 copy-start.14
  1.5 0.0 copy-start.8
  1.5 0.0 copy-start.10
  1.5 3.3 convert_reduce_fusion
  4.8 0.0 copy-done
  4.8 1.2 fusion.2
  6.1 0.0 copy-done.11
  6.1 0.0 copy-done.12
  6.1 0.0 copy-done.13
  6.1 0.0 copy-done.14
  6.2 0.6 pad.17.vec_ref
  6.8 0.6 pad.16.vec_ref
  7.4 0.0 copy-done.8
  7.4 0.0 copy-done.10
  7.5 1.8 fusion.5.n1_ref.n1_hbm
  9.3 0.0 copy-start.2
  9.3 0.0 copy-start.16
  9.3 2.0 fusion.6.own_kv
  11.4 0.3 copy-done.1
  11.7 0.8 copy-done.2
  12.5 0.0 copy-done.16
  12.5 3.3 multiply_convert_fusion.q_ref
  15.8 75.5 %front.1 = (bf16[8,1024,256]{2,1,0:T(8,128)(2,1)}, bf16[1024,512]{1,0:T(8,128)(2,1)}, f32[4,1024]{1,0:T(4,128)}, bf16[1024,2048]{1,0:T(8,128)(2,1)}, bf16[1024,2...) custom-call(bf16[1024,512]{1,0:T(8,128)(2,1)} %multiply_convert_fusion.q_ref, bf16[1024,256]{1,0:T(8,128)(2,1)} %fusion.6.own_kv, ...), custom_call_target="tpu_custom_call" | custom-call | tf_op jit(solution)/shard_map/front/pallas_call | solution.py:1362
  91.3 24.5 %hidden.1 = (bf16[1024,2048]{1,0:T(8,128)(2,1)}, bf16[1024,2048]{1,0:T(8,128)(2,1)}, bf16[1024,2048]{1,0:T(8,128)(2,1)}, f32[1,2048]{1,0:T(1,128)}) custom-call(bf16[1024,2048]{1,0:T(8,128)(2,1)} %x_ref.3, bf16[1024,2048]{1,0:T(8,128)(2,1)} %get-tuple-element.61.attn_ref.attn_hbm, bf16[1024,2048]{1,0:T(8,128)(2,1)} %get-tuple-element.62.g_ref, ...), custom_call_target="tpu_custom_call" | custom-call | tf_op jit(solution)/shard_map/hidden/pallas_call | solution.py:167
  115.8 65.6 %hidden_back.1 = (bf16[1024,2048]{1,0:T(8,128)(2,1)}, bf16[4,256,2048]{2,1,0:T(8,128)(2,1)}, bf16[4,256,2048]{2,1,0:T(8,128)(2,1)}, bf16[4,512,1024]{2,1,0:T(8,128)(2,1)}, bf16[1024,2048]{1,0:T(8,128)(2,1)}) custom-call(bf16[1024,2048]{1,0:T(8,128)(2,1)} %get-tuple-element.63.dpre_ref, bf16[2048,2048]{1,0:T(8,128)(2,1)} %wu_hbm.1, ...), custom_call_target="tpu_custom_call" | custom-call | tf_op jit(solution)/shard_map/hidden_back/pallas_call | solution.py:316
  181.4 56.9 %middle.1 = (bf16[1024,2048]{1,0:T(8,128)(2,1)}, bf16[1024,512]{1,0:T(8,128)(2,1)}, bf16[1024,2048]{1,0:T(8,128)(2,1)}, bf16[4,256,512]{2,1,0:T(8,128)(2,1)}, bf...) custom-call(f32[8,2048]{1,0:T(8,128)} %pad.16.vec_ref, ...), custom_call_target="tpu_custom_call" | custom-call | tf_op jit(solution)/shard_map/middle/pallas_call | solution.py:593
  238.4 97.0 %attend_back.1 = (bf16[1024,512]{1,0:T(8,128)(2,1)}, f32[512,1024]{1,0:T(8,128)}, bf16[8,1024,256]{2,1,0:T(8,128)(2,1)}, bf16[1024,2048]{1,0:T(8,128)(2,1)}, bf1...) custom-call(bf16[1024,512]{1,0:T(8,128)(2,1)} %multiply_convert_fusi, ...), custom_call_target="tpu_custom_call" | custom-call | tf_op jit(solution)/shard_map/attend_back/pallas_call | solution.py:1558
  335.4 6.2 %pair_sum.1.wide_ref = bf16[4,256,2048]{2,1,0:T(8,128)(2,1)} custom-call(bf16[4,256,2048]{2,1,0:T(8,128)(2,1)} %get-tuple-element.71.own_hbm.own_ref, bf16[4,256,2048]{2,1,0:T(8,128)(2,1)} %get-tuple-element.83.rest_ref, bf16[256,2048]{1,0:T(8,128)(2,1)} %get-tuple-element.79.edge_ref), custom_call_target="tpu_custom_call" | custom-call | tf_op jit(solution)/shard_map/pair_sum/pallas_call | solution.py:876
  341.6 99.5 %query_back.1 = (bf16[1024,2048]{1,0:T(8,128)(2,1)}, f32[256,512]{1,0:T(8,128)}, f32[256,512]{1,0:T(8,128)}, bf16[1024,256]{1,0:T(8,128)(2,1)}, bf16[256,2048]{1,0:T(8,128)(2,1)}, /*index=5*/bf16[256,2048]{1,0:T(8,128)(2,1)}) custom-call(bf16[1024,512]{1,0:T(8,128)(2,1)} %get-tuple-element.81.dq_ref, bf16[2048,512]{1,0:T(8,128)(2,1)} %wq_ref.1, ...), custom_call_target="tpu_custom_call" | custom-call | tf_op jit(solution)/shard_map/query_back/pallas_call | solution.py:817
  441.1 1.4 convert_reduce_fusion.1
  442.6 0.0 copy-done.9
  442.6 15.0 %norm_back.1 = (f32[1024,2048]{1,0:T(8,128)}, f32[8,2048]{1,0:T(8,128)}, bf16[1024,2048]{1,0:T(8,128)(2,1)}) custom-call(bf16[1024,256]{1,0:T(8,128)(2,1)} %get-tuple-element.88.dkv_ref, bf16[2048,256]{1,0:T(8,128)(2,1)} %wkv_ref.1, bf16[1024,2048]{1,0:T(8,128)(2,1)} %get-tuple-element.89.dn_ref, bf16[1024,2048]{1,0:T(8,128)(2,1)} %x_ref.3, ...), custom_call_target="tpu_custom_call" | custom-call | tf_op jit(solution)/shard_map/norm_back/pallas_call | solution.py:929
  457.6 0.8 slice.40
  458.4 0.7 select_maximum_fusion.vec_in
  459.1 45.7 %finish.1 = (f32[256,256]{1,0:T(8,128)}, f32[16,2048]{1,0:T(8,128)}, f32[256,2048]{1,0:T(8,128)}, f32[256,2048]{1,0:T(8,128)}) custom-call(bf16[1024,256]{1,0:T(8,128)(2,1)} %get-tuple-element.88.dkv_ref, f32[16,2048]{1,0:T(8,128)} %select_maximum_fusion.vec_in, bf16[256,2048]{1,0:T(8,128)(2,1)} %get-tuple-element.97.far_up, ...), custom_call_target="tpu_custom_call" | custom-call | tf_op jit(solution)/shard_map/finish/pallas_call | solution.py:1073
  504.8 1.3 slice_bitcast_fusion
  506.2 1.8 fusion.7
  508.0 0.9 slice.44
  508.9 0.7 reshape.65
  509.6 1.3 slice.53
  510.8 1.0 copy.32
  511.8 2.9 copy.33
  514.7 0.8 copy.37
  515.5 0.0 copy-done.7
  515.5 0.7 copy.38
  516.2 1.3 copy.39
  (22 shorter events, 0.1 us)
Async XLA Ops:
  0.6 4.2 copy-start
  1.5 4.6 copy-start.11
  1.5 4.6 copy-start.12
  1.5 4.6 copy-start.13
  1.5 4.6 copy-start.14
  1.5 6.0 %copy-start.8 = (f32[2048]{0:T(1024)S(1)}, f32[2048]{0:T(1024)}, u32[]{:S(2)}) copy-start(f32[2048]{0:T(1024)} %param.17) | copy-start | bytes 24580
  1.5 5.9 %copy-start.10 = (f32[2048]{0:T(1024)S(1)}, f32[2048]{0:T(1024)}, u32[]{:S(2)}) copy-start(f32[2048]{0:T(1024)} %param.18) | copy-start | bytes 24580
  7.4 1.9 copy-start.4
  9.3 2.3 copy-start.1
  9.3 3.1 copy-start.2
  9.3 3.1 copy-start.16
  341.6 100.9 %copy-start.15 = (f32[1,2048]{1,0:T(1,128)S(1)}, f32[1,2048]{1,0:T(1,128)}, u32[]{:S(2)}) copy-start(f32[1,2048]{1,0:T(1,128)} %get-tuple-element.96) | copy-start | bytes 24580
  341.6 100.9 %copy-start.9 = (f32[8,2048]{1,0:T(8,128)S(1)}, f32[8,2048]{1,0:T(8,128)}, u32[]{:S(2)}) copy-start(f32[8,2048]{1,0:T(8,128)} %get-tuple-element.95) | copy-start | bytes 196612
  459.1 51.7 %copy-start.6 = (f32[256,512]{1,0:T(8,128)S(1)}, f32[256,512]{1,0:T(8,128)}, u32[]{:S(2)}) copy-start(f32[256,512]{1,0:T(8,128)} %get-tuple-element.103) | copy-start | bytes 1572868
  504.8 9.9 %copy-start.5 = (f32[256,512]{1,0:T(8,128)S(1)}, f32[256,512]{1,0:T(8,128)}, u32[]{:S(2)}) copy-start(f32[256,512]{1,0:T(8,128)} %get-tuple-element.151) | copy-start | bytes 1572868
  504.8 10.7 %copy-start.7 = (f32[256,256]{1,0:T(8,128)S(1)}, f32[256,256]{1,0:T(8,128)}, u32[]{:S(2)}) copy-start(f32[256,256]{1,0:T(8,128)} %get-tuple-element.153) | copy-start | bytes 786436
  504.8 11.4 %copy-start.3 = (f32[256,2048]{1,0:T(8,128)S(1)}, f32[256,2048]{1,0:T(8,128)}, u32[]{:S(2)}) copy-start(f32[256,2048]{1,0:T(8,128)} %get-tuple-element.159) | copy-start | bytes 6291460
